TPU v7x, 128 devices: a whole 4x4x4 slice. The times are simulated.
128 devices in a mesh: occ: 4 (over y_lo, core), vir: 32 (over z, x, y_hi).
Axes of the slice: x: 4, y: 4 (y_hi: 2, y_lo: 2; y = y_hi * 2 + y_lo), z: 4, core: 2. Of those that a mesh axis runs over, the one named last changes fastest.
Arguments:
- amplitudes: bfloat16 [8, 1024, 1024], P('occ', 'vir'), may hold values from -6 to 6
- factors: bfloat16 [96, 1024, 1024], P('vir'), may hold values from -0.0625 to 0.0625
- occ_energy: float32 [100], replicated, may hold values from -2 to -0.3
- vir_energy: float32 [1024], replicated, may hold values from 0.3 to 4
- occ_irrep: int32 [100], replicated, may hold values from 0 to 7
- vir_irrep: int32 [1024], replicated, may hold values from 0 to 7
- pair_orbitals: int32 [8, 2], replicated, may hold values from 0 to 99, as said below
Outputs:
- update: float32 [8, 1024, 1024], P('occ', 'vir')
Inputs may be any that keep to these rules, and one draw needn't show every extreme that they name: `pair_orbitals`: pair p + 4 is pair p with i and j swapped; the orbitals named by the first 4 pairs are all distinct.
All inputs are finite; a program needn't handle non-finite values.
Results may differ from a plain program's by a relative error of at most 0.0029.
Values may be sent and summed in bfloat16 or wider, within the bound.
A program may use at most 128 MiB of HBM per device.

v0:
```python
import jax
import jax.numpy as jnp
from jax import lax
from jax.sharding import PartitionSpec as P


def passed_along(block, axis, distance):
    devices = range(lax.axis_size(axis))
    route = [((i - distance) % len(devices), i) for i in devices]
    return lax.ppermute(block, axis, route)


def per_device(amplitudes, factors, occ_energy, vir_energy, occ_irrep, vir_irrep, pair_orbitals):
    local_pairs = amplitudes.shape[0]
    row_count = amplitudes.shape[1]
    occ_total = occ_energy.shape[0]
    occ_devices = lax.axis_size("occ")
    gathered = lax.all_gather(amplitudes, "vir", axis=1, tiled=True)

    def half_product(factor):
        product = jnp.einsum("pcd,bd->pbc", gathered, factor, preferred_element_type=jnp.float32)
        return product.astype(jnp.bfloat16)

    halves = lax.map(half_product, factors)
    scattered = lax.psum_scatter(
        jnp.einsum("qac,qpbc->apb", factors, halves, preferred_element_type=jnp.float32),
        "vir",
        scatter_dimension=0,
        tiled=True,
    )
    own_part = jnp.transpose(scattered, (1, 0, 2))
    shifted = passed_along(own_part, "occ", occ_devices // 2)
    turned = lax.all_to_all(shifted, "vir", split_axis=2, concat_axis=1, tiled=True)
    partner = jnp.transpose(turned, (0, 2, 1))
    occ_index = lax.axis_index("occ")
    vir_index = lax.axis_index("vir")
    pair_ids = lax.dynamic_slice_in_dim(pair_orbitals, occ_index * local_pairs, local_pairs, 0)
    row_start = vir_index * row_count
    energy_rows = lax.dynamic_slice_in_dim(vir_energy, row_start, row_count, 0)
    irrep_rows = lax.dynamic_slice_in_dim(vir_irrep, row_start, row_count, 0)
    positions = jnp.arange(occ_total, dtype=jnp.int32)
    first_hot = positions[None, :] == pair_ids[:, 0:1]
    second_hot = positions[None, :] == pair_ids[:, 1:2]
    pair_energy = jnp.sum(jnp.where(first_hot, occ_energy[None, :], 0.0), axis=1) + jnp.sum(
        jnp.where(second_hot, occ_energy[None, :], 0.0), axis=1
    )
    first_irrep = jnp.sum(jnp.where(first_hot, occ_irrep[None, :], 0), axis=1)
    second_irrep = jnp.sum(jnp.where(second_hot, occ_irrep[None, :], 0), axis=1)
    pair_sym = jnp.bitwise_xor(first_irrep, second_irrep)
    combined = jnp.bitwise_xor(
        jnp.bitwise_xor(pair_sym[:, None, None], irrep_rows[None, :, None]),
        vir_irrep[None, None, :],
    )
    allowed = combined == 0
    denominator = (
        energy_rows[None, :, None] + vir_energy[None, None, :] - pair_energy[:, None, None]
    )
    return jnp.where(allowed, (own_part + partner) / denominator, jnp.float32(0.0))


def solution(mesh):
    return jax.shard_map(
        per_device,
        mesh=mesh,
        in_specs=(P("occ", "vir", None), P("vir", None, None), P(), P(), P(), P(), P()),
        out_specs=P("occ", "vir", None),
        check_vma=False,
    )
```

profile of v0, /device:TPU:0, one launch (start us, length us, event | category | flops | bytes accessed | tf_op | source)
XLA Modules:
  0.0 593.3 jit_solution(9868051408352421275)
XLA Ops:
  6.5 0.7 all-gather.2.cloned.1.call-update
  7.3 86.0 %all-gather.2.cloned.1.call-done = bf16[2,1024,1024]{2,1,0:T(8,128)(2,1)} async-done(((bf16[2,32,1024]{2,1,0:T(8,128)(2,1)}), bf16[2,1024,1024]{2,1,0:T(8,128)(2,1)}) %all-gather.2.cloned.1.call-update) | async-done | bytes 4194320 | tf_op jit(solution)/shard_map/all_gather | solution.py:18
  93.3 27.9 %while.10 = (s32[]{:T(128)}, bf16[3,2,1024,1024]{3,2,1,0:T(8,128)(2,1)}, bf16[3,1024,1024]{2,1,0:T(8,128)(2,1)}, bf16[2,1024,1024]{2,1,0:T(8,128)(2,1)}, s32[]{:T(128)}) while((s32[]{:T(128)}, bf16[3,2,1024,1024]{3,2,1,0:T(8,128)(2,1)}, bf16[3,1024,1024]{2,1,0:T(8,128)(2,1)}, bf16[2,1024,1024]{2,1,0:T(8,128)(2,1)}, s32[]{:T(128)}) %tuple.21), condition=%wide.region_3.4_spmd, body=%wide.region_2.3_spmd.sunk | while | flops 4297064448 | bytes 10486853 | solution.py:24
  93.3 9.3 %bitcast_dynamic-update-slice_fusion.2 = bf16[3,2,1024,1024]{3,2,1,0:T(8,128)(2,1)} fusion(bf16[3,2,1024,1024]{3,2,1,0:T(8,128)(2,1)} %get-tuple-element.73, s32[]{:T(128)S(6)} %copy.28, bf16[2,1024,1024]{2,1,0:T(8,128)(2,1)} %get-tuple-element.80, bf16[3,1024,1024]{2,1,0:T(8,128)(2,1)} %get-tuple-element.79), kind=kOutput, calls=%fused_computation.clone.1 | convolution fusion | flops 4297064448 | bytes 10486784 | tf_op jit(solution)/shard_map/while/body/eval_jaxpr/pcd,bd->pbc/dot_general | solution.py:21
  102.6 9.3 %bitcast_dynamic-update-slice_fusion.2 = bf16[3,2,1024,1024]{3,2,1,0:T(8,128)(2,1)} fusion(bf16[3,2,1024,1024]{3,2,1,0:T(8,128)(2,1)} %get-tuple-element.73, s32[]{:T(128)S(6)} %copy.28, bf16[2,1024,1024]{2,1,0:T(8,128)(2,1)} %get-tuple-element.80, bf16[3,1024,1024]{2,1,0:T(8,128)(2,1)} %get-tuple-element.79), kind=kOutput, calls=%fused_computation.clone.1 | convolution fusion | flops 4297064448 | bytes 10486784 | tf_op jit(solution)/shard_map/while/body/eval_jaxpr/pcd,bd->pbc/dot_general | solution.py:21
  112.0 9.3 %bitcast_dynamic-update-slice_fusion.2 = bf16[3,2,1024,1024]{3,2,1,0:T(8,128)(2,1)} fusion(bf16[3,2,1024,1024]{3,2,1,0:T(8,128)(2,1)} %get-tuple-element.73, s32[]{:T(128)S(6)} %copy.28, bf16[2,1024,1024]{2,1,0:T(8,128)(2,1)} %get-tuple-element.80, bf16[3,1024,1024]{2,1,0:T(8,128)(2,1)} %get-tuple-element.79), kind=kOutput, calls=%fused_computation.clone.1 | convolution fusion | flops 4297064448 | bytes 10486784 | tf_op jit(solution)/shard_map/while/body/eval_jaxpr/pcd,bd->pbc/dot_general | solution.py:21
  121.3 19.4 %fusion.5 = f32[1024,2,1024]{0,2,1:T(8,128)} fusion(bf16[3,2,1024,1024]{3,2,1,0:T(8,128)(2,1)} %get-tuple-element.27, bf16[3,1024,1024]{2,1,0:T(8,128)(2,1)} %get-tuple-element.92), kind=kOutput, calls=%fused_computation.6 | convolution fusion | flops 12884901888 | bytes 27262976 | tf_op jit(solution)/shard_map/qac,qpbc->apb/dot_general | solution.py:26
  140.7 13.4 %copy.17 = f32[1024,2,1024]{2,1,0:T(2,128)} copy(f32[1024,2,1024]{0,2,1:T(8,128)} %fusion.5) | data formatting | bytes 16777216 | tf_op jit(solution)/shard_map/qac,qpbc->apb/dot_general | solution.py:26
  154.1 0.6 copy-done.5
  154.7 0.6 dynamic-slice
  156.0 397.3 %all-reduce.3.cloned.1.call-done = f32[1024,2,1024]{2,1,0:T(2,128)} async-done(((f32[1024,2,1024]{2,1,0:T(2,128)}), f32[1024,2,1024]{2,1,0:T(2,128)}) %all-reduce.3.cloned.1.call-update) | async-done | bytes 8388624
  553.3 1.0 dynamic-slice_bitcast_fusion
  554.8 6.0 %collective-permute-done = f32[2,32,1024]{2,1,0:T(8,128)S(1)} collective-permute-done((f32[2,32,1024]{2,1,0:T(8,128)S(1)}, f32[2,32,1024]{2,1,0:T(8,128)S(1)}, u32[]{:S(2)}, u32[]{:S(2)}) %collective-permute-start) | collective-permute-done | bytes 262176 | tf_op jit(solution)/shard_map/ppermute | solution.py:10
  560.8 0.5 copy.19
  561.3 1.8 reshape.80
  563.1 6.6 %all-to-all-start = ((f32[32,1,2048]{2,1,0:T(1,128)}), f32[32,1,2048]{2,1,0:T(1,128)S(1)}, u32[]{:S(2)}, u32[]{:S(2)}) async-start(f32[32,1,2048]{2,1,0:T(1,128)} %reshape.80), calls=%async_computation | async-start | bytes 524288 | tf_op jit(solution)/shard_map/all_to_all | solution.py:33
  570.1 10.3 %all-to-all-done = f32[32,1,2048]{2,1,0:T(1,128)S(1)} async-done(((f32[32,1,2048]{2,1,0:T(1,128)}), f32[32,1,2048]{2,1,0:T(1,128)S(1)}, u32[]{:S(2)}, u32[]{:S(2)}) %all-to-all-start) | async-done | bytes 262176 | tf_op jit(solution)/shard_map/all_to_all | solution.py:33
  580.5 0.5 broadcast.48
  581.0 1.3 reduce
  582.3 0.9 reshape.81
  583.2 0.6 copy.24
  583.8 0.6 all_to_all.16
  584.4 1.3 compare_select_fusion
  585.7 0.8 copy.21
  (27 shorter events, 1.1 us)
Async XLA Ops:
  6.5 149.4 %copy-start = (s32[8,2]{0,1:T(2,128)S(1)}, s32[8,2]{0,1:T(2,128)}, u32[]{:S(2)}) copy-start(s32[8,2]{0,1:T(2,128)} %param.15) | copy-start | bytes 196
  6.5 86.8 %all-gather.2.cloned.1.call-start = ((), (), s32[]{:S(2)}) async-start(), calls=%async_computation.1 | async-start | bytes 4325376 | tf_op jit(solution)/shard_map/all_gather | solution.py:18
  7.3 546.0 %all-reduce.3.cloned.1.call-start = ((), (), s32[]{:S(2)}) async-start(), calls=%async_computation.2 | async-start | bytes 16777216
  154.0 0.7 copy-start.5
  154.0 400.4 %copy-start.3 = (s32[100]{0:T(128)S(1)}, s32[100]{0:T(128)}, u32[]{:S(2)}) copy-start(s32[100]{0:T(128)} %param.13) | copy-start | bytes 1204
  154.0 400.6 %copy-start.1 = (s32[1024]{0:T(1024)S(1)}, s32[1024]{0:T(1024)}, u32[]{:S(2)}) copy-start(s32[1024]{0:T(1024)} %param.14) | copy-start | bytes 12292
  154.0 415.7 %copy-start.4 = (f32[100]{0:T(128)S(1)}, f32[100]{0:T(128)}, u32[]{:S(2)}) copy-start(f32[100]{0:T(128)} %param.11) | copy-start | bytes 1204
  154.0 415.9 %copy-start.2 = (f32[1024]{0:T(1024)S(1)}, f32[1024]{0:T(1024)}, u32[]{:S(2)}) copy-start(f32[1024]{0:T(1024)} %param.12) | copy-start | bytes 12292
  554.3 6.5 %collective-permute-start = (f32[2,32,1024]{2,1,0:T(8,128)S(1)}, f32[2,32,1024]{2,1,0:T(8,128)S(1)}, u32[]{:S(2)}, u32[]{:S(2)}) collective-permute-start(f32[2,32,1024]{2,1,0:T(8,128)S(1)} %copy.18), channel_id=1, source_target_pairs={{64,0},{96,32},{0,64},{32,96},{65,1},{97,33},{1,65},{33,97},{66,2}... | collective-permute-start | bytes 786440 | tf_op jit(solution)/shard_map/ppermute | solution.py:10
  563.1 17.4 %all-to-all-start = ((f32[32,1,2048]{2,1,0:T(1,128)}), f32[32,1,2048]{2,1,0:T(1,128)S(1)}, u32[]{:S(2)}, u32[]{:S(2)}) async-start(f32[32,1,2048]{2,1,0:T(1,128)} %reshape.80), calls=%async_computation | async-start | bytes 524288 | tf_op jit(solution)/shard_map/all_to_all | solution.py:33
Sparse Core Ops, SparseCore 0:
  10.4 82.9 all-gather.1
  154.2 399.0 all-reduce.2
where the time goes:
time: 594 us; the launch traced here: 593 us
  waiting for transfers between devices  500 us (84%)
  matrix products  47.3 us (8%)
  local copies, waits for them, and re-layouts  21.5 us (4%)
  between operations  14.2 us (2%)
  starting transfers between devices  6.75 us (1%)
    unnamed x3, waiting for transfers between devices  398 us
    all_gather x1, waiting for transfers between devices, per_device(): gathered = lax.all_gather(amplitudes, 'vir', axis=1, tiled=True)  86 us
    dot_general x3, matrix products, half_product(): jnp.einsum('pcd,bd->pbc', gathered, factor, preferred_element_type=jnp.fl...  27.9 us
    dot_general x1, matrix products, per_device(): jnp.einsum('qac,qpbc->apb', factors, halves, preferred_element_type=jnp.f...  19.4 us
    dot_general x1, local copies, waits for them, and re-layouts, per_device(): jnp.einsum('qac,qpbc->apb', factors, halves, preferred_element_type=jnp.f...  13.4 us
  transfers between devices with their start and end apart: 4, of which 4 were waited for; matrix products, arithmetic and copies ran while one was open for 0% of the time, Pallas kernels for 0%

commit v1 on v0

--- a/solution.py
+++ b/solution.py
@@ -15,25 +15,35 @@
     row_count = amplitudes.shape[1]
     occ_total = occ_energy.shape[0]
     occ_devices = lax.axis_size("occ")
-    gathered = lax.all_gather(amplitudes, "vir", axis=1, tiled=True)
+    vir_devices = lax.axis_size("vir")
+    occ_index = lax.axis_index("occ")
+    vir_index = lax.axis_index("vir")
+    lower_half = occ_index < occ_devices // 2
+
+    outgoing = jnp.where(lower_half, amplitudes[1], amplitudes[0])
+    incoming = passed_along(outgoing, "occ", occ_devices // 2)
+    first = jnp.where(lower_half, amplitudes[0], incoming)
+    second = jnp.where(lower_half, incoming, amplitudes[1])
+    couple = jnp.stack([first, second], axis=0)
+    gathered = lax.all_gather(couple, "vir", axis=1, tiled=True)
 
     def half_product(factor):
         product = jnp.einsum("pcd,bd->pbc", gathered, factor, preferred_element_type=jnp.float32)
         return product.astype(jnp.bfloat16)
 
     halves = lax.map(half_product, factors)
-    scattered = lax.psum_scatter(
-        jnp.einsum("qac,qpbc->apb", factors, halves, preferred_element_type=jnp.float32),
-        "vir",
-        scatter_dimension=0,
-        tiled=True,
-    )
-    own_part = jnp.transpose(scattered, (1, 0, 2))
-    shifted = passed_along(own_part, "occ", occ_devices // 2)
-    turned = lax.all_to_all(shifted, "vir", split_axis=2, concat_axis=1, tiled=True)
-    partner = jnp.transpose(turned, (0, 2, 1))
-    occ_index = lax.axis_index("occ")
-    vir_index = lax.axis_index("vir")
+    direct = jnp.einsum("qac,qbc->ab", factors, halves[:, 0], preferred_element_type=jnp.float32)
+    turned_term = jnp.einsum("qac,qbc->ab", halves[:, 1], factors, preferred_element_type=jnp.float32)
+    combined = direct + turned_term
+    own_rows = lax.psum_scatter(combined, "vir", scatter_dimension=0, tiled=True)
+    cols = lax.all_to_all(own_rows, "vir", split_axis=1, concat_axis=0, tiled=True)
+    own_cols = jnp.transpose(cols, (1, 0))
+    outgoing_block = jnp.where(lower_half, own_cols, own_rows)
+    incoming_block = passed_along(outgoing_block, "occ", occ_devices // 2)
+    first_out = jnp.where(lower_half, own_rows, incoming_block)
+    second_out = jnp.where(lower_half, incoming_block, own_cols)
+    summed_pair = jnp.stack([first_out, second_out], axis=0)
+
     pair_ids = lax.dynamic_slice_in_dim(pair_orbitals, occ_index * local_pairs, local_pairs, 0)
     row_start = vir_index * row_count
     energy_rows = lax.dynamic_slice_in_dim(vir_energy, row_start, row_count, 0)
@@ -47,15 +57,15 @@
     first_irrep = jnp.sum(jnp.where(first_hot, occ_irrep[None, :], 0), axis=1)
     second_irrep = jnp.sum(jnp.where(second_hot, occ_irrep[None, :], 0), axis=1)
     pair_sym = jnp.bitwise_xor(first_irrep, second_irrep)
-    combined = jnp.bitwise_xor(
+    combined_sym = jnp.bitwise_xor(
         jnp.bitwise_xor(pair_sym[:, None, None], irrep_rows[None, :, None]),
         vir_irrep[None, None, :],
     )
-    allowed = combined == 0
+    allowed = combined_sym == 0
     denominator = (
         energy_rows[None, :, None] + vir_energy[None, None, :] - pair_energy[:, None, None]
     )
-    return jnp.where(allowed, (own_part + partner) / denominator, jnp.float32(0.0))
+    return jnp.where(allowed, summed_pair / denominator, jnp.float32(0.0))
 
 
 def solution(mesh):

time: 594 us -> 381 us (0.64)
  waiting for transfers between devices: 500 us -> 289 us
  local copies, waits for them, and re-layouts: 21.5 us -> 15.1 us
    unnamed x3 -> x2, waiting for transfers between devices: 398 us -> 0.03 us
    reduce_scatter x0 -> x1, waiting for transfers between devices: none -> 190 us  [per_device(): lax.psum_scatter(combined, 'vir', scatter_dimension=0, tiled=True)]
    dot_general x1 -> x0, local copies, waits for them, and re-layouts: 13.4 us -> none  [per_device(): jnp.einsum('qac,qpbc->apb', factors, halves, preferred_element_type=jnp.f...]
    dot_general x1 -> x2, matrix products: 19.4 us -> 22 us  [the longest x1 12.1 us: per_device(): jnp.einsum('qac,qbc->ab', halves[:, 1], factors, preferred_element_type=j...]
  transfers between devices with their start and end apart: 4 -> 5, of which waited for: 4 -> 5; matrix products, arithmetic and copies ran while one was open for 0% -> 0% of each run, Pallas kernels for 0% -> 0%
where the time goes in v1:
time: 381 us; the launch traced here: 380 us
  waiting for transfers between devices  289 us (76%)
  matrix products  50.1 us (13%)
  local copies, waits for them, and re-layouts  15.1 us (4%)
  between operations  13.5 us (4%)
  starting transfers between devices  7.5 us (2%)
  other arithmetic  5.14 us (1%)
    reduce_scatter x1, waiting for transfers between devices, per_device(): lax.psum_scatter(combined, 'vir', scatter_dimension=0, tiled=True)  190 us
    all_gather x1, waiting for transfers between devices, per_device(): gathered = lax.all_gather(couple, 'vir', axis=1, tiled=True)  82.9 us
    dot_general x3, matrix products, half_product(): jnp.einsum('pcd,bd->pbc', gathered, factor, preferred_element_type=jnp.fl...  28.1 us
    dot_general x1, matrix products, per_device(): jnp.einsum('qac,qbc->ab', halves[:, 1], factors, preferred_element_type=j...  12.1 us
    all_to_all x1, waiting for transfers between devices, per_device(): lax.all_to_all(own_rows, 'vir', split_axis=1, concat_axis=0, tiled=True)  10.1 us
    dot_general x1, matrix products, per_device(): jnp.einsum('qac,qbc->ab', factors, halves[:, 0], preferred_element_type=j...  9.83 us
  transfers between devices with their start and end apart: 5, of which 5 were waited for; matrix products, arithmetic and copies ran while one was open for 0% of the time, Pallas kernels for 0%

profile of v1, /device:TPU:0, one launch (start us, length us, event | category | flops | bytes accessed | tf_op | source)
XLA Modules:
  0.0 380.3 jit_solution(12277028687982104228)
XLA Ops:
  6.5 0.9 bitcast_select_fusion.3
  7.4 1.7 collective-permute-start
  9.2 2.6 collective-permute-done
  11.8 0.9 fusion.14
  12.7 0.8 copy.44
  13.6 82.9 %all-gather.2.cloned.1.call-done = bf16[2,1024,1024]{2,0,1:T(2,128)(2,1)} async-done(((bf16[2,32,1024]{2,0,1:T(2,128)(2,1)}), bf16[2,1024,1024]{2,0,1:T(2,128)(2,1)}) %all-gather.2.cloned.1.call-update) | async-done | bytes 4194320 | tf_op jit(solution)/shard_map/all_gather | solution.py:28
  96.4 5.4 %copy.45 = bf16[2,1024,1024]{2,1,0:T(8,128)(2,1)} copy(bf16[2,1024,1024]{2,0,1:T(2,128)(2,1)} %all-gather.2.cloned.1.call-done) | data formatting | bytes 8388608 | tf_op jit(solution)/shard_map/while | solution.py:34
  101.9 28.1 %while.10 = (s32[]{:T(128)}, bf16[3,2,1024,1024]{3,2,0,1:T(8,128)(2,1)}, bf16[3,1024,1024]{2,1,0:T(8,128)(2,1)}, bf16[2,1024,1024]{2,1,0:T(8,128)(2,1)}, s32[]{:T(128)}) while((s32[]{:T(128)}, bf16[3,2,1024,1024]{3,2,0,1:T(8,128)(2,1)}, bf16[3,1024,1024]{2,1,0:T(8,128)(2,1)}, bf16[2,1024,1024]{2,1,0:T(8,128)(2,1)}, s32[]{:T(128)}) %tuple.28), condition=%wide.region_3.4_spmd, body=%wide.region_2.3_spmd.sunk | while | flops 4297064448 | bytes 10486845 | solution.py:34
  101.9 9.4 %bitcast_dynamic-update-slice_fusion.2 = bf16[3,2,1024,1024]{3,2,0,1:T(8,128)(2,1)} fusion(bf16[3,2,1024,1024]{3,2,0,1:T(8,128)(2,1)} %get-tuple-element.97, s32[]{:T(128)} %get-tuple-element.96, bf16[2,1024,1024]{2,1,0:T(8,128)(2,1)} %get-tuple-element.104, bf16[3,1024,1024]{2,1,0:T(8,128)(2,1)} %get-tuple-element.103), kind=kOutput, calls=%fused_computation.clone.1 | convolution fusion | flops 4297064448 | bytes 10486784 | tf_op jit(solution)/shard_map/while/body/eval_jaxpr/pcd,bd->pbc/dot_general | solution.py:31
  111.2 9.4 %bitcast_dynamic-update-slice_fusion.2 = bf16[3,2,1024,1024]{3,2,0,1:T(8,128)(2,1)} fusion(bf16[3,2,1024,1024]{3,2,0,1:T(8,128)(2,1)} %get-tuple-element.97, s32[]{:T(128)} %get-tuple-element.96, bf16[2,1024,1024]{2,1,0:T(8,128)(2,1)} %get-tuple-element.104, bf16[3,1024,1024]{2,1,0:T(8,128)(2,1)} %get-tuple-element.103), kind=kOutput, calls=%fused_computation.clone.1 | convolution fusion | flops 4297064448 | bytes 10486784 | tf_op jit(solution)/shard_map/while/body/eval_jaxpr/pcd,bd->pbc/dot_general | solution.py:31
  120.7 9.3 %bitcast_dynamic-update-slice_fusion.2 = bf16[3,2,1024,1024]{3,2,0,1:T(8,128)(2,1)} fusion(bf16[3,2,1024,1024]{3,2,0,1:T(8,128)(2,1)} %get-tuple-element.97, s32[]{:T(128)} %get-tuple-element.96, bf16[2,1024,1024]{2,1,0:T(8,128)(2,1)} %get-tuple-element.104, bf16[3,1024,1024]{2,1,0:T(8,128)(2,1)} %get-tuple-element.103), kind=kOutput, calls=%fused_computation.clone.1 | convolution fusion | flops 4297064448 | bytes 10486784 | tf_op jit(solution)/shard_map/while/body/eval_jaxpr/pcd,bd->pbc/dot_general | solution.py:31
  130.0 12.1 %fusion.3 = f32[1024,1024,1]{0,1,2:T(8,128)} fusion(bf16[3,1024,1024]{2,1,0:T(8,128)(2,1)} %get-tuple-element.119, bf16[3,2,1024,1024]{3,2,0,1:T(8,128)(2,1)} %get-tuple-element.27), kind=kOutput, calls=%fused_computation.4 | convolution fusion | flops 6442450944 | bytes 16777216 | tf_op jit(solution)/shard_map/qac,qbc->ab/dot_general | solution.py:36
  142.1 9.8 %bitcast_add_fusion = f32[1024,1024]{0,1:T(8,128)} fusion(f32[1024,1024,1]{0,1,2:T(8,128)} %fusion.3, bf16[3,1024,1024]{2,1,0:T(8,128)(2,1)S(1)} %copy-done.5, bf16[3,2,1024,1024]{3,2,0,1:T(8,128)(2,1)S(1)} %copy-done.6), kind=kOutput, calls=%fused_computation.10 | convolution fusion | flops 6443499520 | bytes 20971520 | tf_op jit(solution)/shard_map/qac,qbc->ab/dot_general | solution.py:35
  152.0 5.4 %copy.54 = f32[1024,1024]{1,0:T(8,128)} copy(f32[1024,1024]{0,1:T(8,128)} %bitcast_add_fusion) | data formatting | bytes 8388608
  158.1 189.9 %reduce-scatter.4.cloned.1.call-done = f32[32,1024]{1,0:T(8,128)} async-done(((f32[1024,1024]{1,0:T(8,128)}), f32[32,1024]{1,0:T(8,128)}) %reduce-scatter.4.cloned.1.call-update) | async-done | bytes 131088 | tf_op jit(solution)/shard_map/reduce_scatter | solution.py:38
  348.0 1.1 copy.55
  349.1 0.9 reshape.84
  350.0 4.1 %all-to-all-start = ((f32[32,1,1024]{2,1,0:T(1,128)}), f32[32,1,1024]{2,1,0:T(1,128)S(1)}, u32[]{:S(2)}, u32[]{:S(2)}) async-start(f32[32,1,1024]{2,1,0:T(1,128)} %reshape.84), calls=%async_computation | async-start | bytes 262144 | tf_op jit(solution)/shard_map/all_to_all | solution.py:39
  354.2 10.1 %all-to-all-done = f32[32,1,1024]{2,1,0:T(1,128)S(1)} async-done(((f32[32,1,1024]{2,1,0:T(1,128)}), f32[32,1,1024]{2,1,0:T(1,128)S(1)}, u32[]{:S(2)}, u32[]{:S(2)}) %all-to-all-start) | async-done | bytes 131104 | tf_op jit(solution)/shard_map/all_to_all | solution.py:39
  364.8 1.0 reduce
  366.6 1.7 collective-permute-start.1
  368.3 3.3 collective-permute-done.1
  371.7 0.9 select_bitcast_fusion
  372.6 0.8 fusion.11
  (36 shorter events, 2.2 us)
Async XLA Ops:
  6.5 151.0 %copy-start = (s32[8,2]{0,1:T(2,128)S(1)}, s32[8,2]{0,1:T(2,128)}, u32[]{:S(2)}) copy-start(s32[8,2]{0,1:T(2,128)} %param.15) | copy-start | bytes 196
  6.5 89.9 %all-gather.2.cloned.1.call-start = ((), (), s32[]{:S(2)}) async-start(), calls=%async_computation.2 | async-start | bytes 4325376 | tf_op jit(solution)/shard_map/all_gather | solution.py:28
  7.4 4.3 %collective-permute-start = (bf16[32,1024]{1,0:T(8,128)(2,1)S(1)}, bf16[32,1024]{1,0:T(8,128)(2,1)S(1)}, u32[]{:S(2)}, u32[]{:S(2)}) collective-permute-start(bf16[32,1024]{1,0:T(8,128)(2,1)S(1)} %bitcast_select_fusion.3), channel_id=1, source_target_pairs={{64,0},{96,32},{0,64},{32,96},{65,1},{97,33},{1,65},{33,97},{66,2}... | collective-permute-start | bytes 196616 | tf_op jit(solution)/shard_map/ppermute | solution.py:10
  13.5 334.5 %reduce-scatter.4.cloned.1.call-start = ((), (), s32[]{:S(2)}) async-start(), calls=%async_computation.3 | async-start | bytes 4325376 | tf_op jit(solution)/shard_map/reduce_scatter | solution.py:38
  130.0 12.1 %copy-start.5 = (bf16[3,1024,1024]{2,1,0:T(8,128)(2,1)S(1)}, bf16[3,1024,1024]{2,1,0:T(8,128)(2,1)}, u32[]{:S(2)}) copy-start(bf16[3,1024,1024]{2,1,0:T(8,128)(2,1)} %get-tuple-element.119) | copy-start | bytes 18874372
  130.0 12.1 %copy-start.6 = (bf16[3,2,1024,1024]{3,2,0,1:T(8,128)(2,1)S(1)}, bf16[3,2,1024,1024]{3,2,0,1:T(8,128)(2,1)}, u32[]{:S(2)}) copy-start(bf16[3,2,1024,1024]{3,2,0,1:T(8,128)(2,1)} %get-tuple-element.27) | copy-start | bytes 37748740
  152.0 5.4 %copy-start.1 = (s32[1024]{0:T(1024)S(1)}, s32[1024]{0:T(1024)}, u32[]{:S(2)}) copy-start(s32[1024]{0:T(1024)} %param.14) | copy-start | bytes 12292
  152.0 5.5 %copy-start.2 = (f32[1024]{0:T(1024)S(1)}, f32[1024]{0:T(1024)}, u32[]{:S(2)}) copy-start(f32[1024]{0:T(1024)} %param.12) | copy-start | bytes 12292
  152.0 5.7 %copy-start.3 = (s32[100]{0:T(128)S(1)}, s32[100]{0:T(128)}, u32[]{:S(2)}) copy-start(s32[100]{0:T(128)} %param.13) | copy-start | bytes 1204
  152.0 5.9 %copy-start.4 = (f32[100]{0:T(128)S(1)}, f32[100]{0:T(128)}, u32[]{:S(2)}) copy-start(f32[100]{0:T(128)} %param.11) | copy-start | bytes 1204
  350.0 14.3 %all-to-all-start = ((f32[32,1,1024]{2,1,0:T(1,128)}), f32[32,1,1024]{2,1,0:T(1,128)S(1)}, u32[]{:S(2)}, u32[]{:S(2)}) async-start(f32[32,1,1024]{2,1,0:T(1,128)} %reshape.84), calls=%async_computation | async-start | bytes 262144 | tf_op jit(solution)/shard_map/all_to_all | solution.py:39
  366.6 5.0 %collective-permute-start.1 = (f32[32,1024]{1,0:T(8,128)S(1)}, f32[32,1024]{1,0:T(8,128)S(1)}, u32[]{:S(2)}, u32[]{:S(2)}) collective-permute-start(f32[32,1024]{1,0:T(8,128)S(1)} %bitcast_select_fusion.1), channel_id=1, source_target_pairs={{64,0},{96,32},{0,64},{32,96},{65,1},{97,33},{1,65},{33,97},{66,2}... | collective-permute-start | bytes 393224 | tf_op jit(solution)/shard_map/ppermute | solution.py:10
Sparse Core Ops, SparseCore 0:
  13.6 82.7 all-gather.1
  157.5 190.4 reduce-scatter.3

commit v2 on v1

--- a/solution.py
+++ b/solution.py
@@ -25,7 +25,9 @@
     first = jnp.where(lower_half, amplitudes[0], incoming)
     second = jnp.where(lower_half, incoming, amplitudes[1])
     couple = jnp.stack([first, second], axis=0)
-    gathered = lax.all_gather(couple, "vir", axis=1, tiled=True)
+    spread = jnp.broadcast_to(couple[None], (vir_devices,) + couple.shape)
+    pieces = lax.all_to_all(spread, "vir", split_axis=0, concat_axis=0, tiled=True)
+    gathered = jnp.transpose(pieces, (1, 0, 2, 3)).reshape(2, vir_devices * row_count, couple.shape[-1])
 
     def half_product(factor):
         product = jnp.einsum("pcd,bd->pbc", gathered, factor, preferred_element_type=jnp.float32)
@@ -35,7 +37,9 @@
     direct = jnp.einsum("qac,qbc->ab", factors, halves[:, 0], preferred_element_type=jnp.float32)
     turned_term = jnp.einsum("qac,qbc->ab", halves[:, 1], factors, preferred_element_type=jnp.float32)
     combined = direct + turned_term
-    own_rows = lax.psum_scatter(combined, "vir", scatter_dimension=0, tiled=True)
+    blocks = combined.reshape(vir_devices, row_count, combined.shape[-1])
+    arrived = lax.all_to_all(blocks, "vir", split_axis=0, concat_axis=0, tiled=True)
+    own_rows = jnp.sum(arrived, axis=0)
     cols = lax.all_to_all(own_rows, "vir", split_axis=1, concat_axis=0, tiled=True)
     own_cols = jnp.transpose(cols, (1, 0))
     outgoing_block = jnp.where(lower_half, own_cols, own_rows)

time: 381 us -> 219 us (0.57)
  waiting for transfers between devices: 289 us -> 128 us
  starting transfers between devices: 7.5 us -> 26.3 us
  between operations: 13.5 us -> 0.15 us
  local copies, waits for them, and re-layouts: 15.1 us -> 9.9 us
    reduce_scatter x1 -> x0, waiting for transfers between devices: 190 us -> none  [per_device(): lax.psum_scatter(combined, 'vir', scatter_dimension=0, tiled=True)]
    all_to_all x0 -> x2, waiting for transfers between devices: none -> 112 us  [the longest x1 57.8 us: per_device(): lax.all_to_all(spread, 'vir', split_axis=0, concat_axis=0, tiled=True)]
    all_gather x1 -> x0, waiting for transfers between devices: 82.9 us -> none  [per_device(): gathered = lax.all_gather(couple, 'vir', axis=1, tiled=True)]
    all_to_all x0 -> x2, starting transfers between devices: none -> 16.2 us  [the longest x1 11 us: per_device(): lax.all_to_all(spread, 'vir', split_axis=0, concat_axis=0, tiled=True)]
    unnamed x18 -> x16, local copies, waits for them, and re-layouts: 7.57 us -> 1.1 us
    while x1 -> x0, local copies, waits for them, and re-layouts: 5.44 us -> none  [per_device(): halves = lax.map(half_product, factors)]
    all_to_all x0 -> x1, local copies, waits for them, and re-layouts: none -> 4.93 us  [per_device(): lax.all_to_all(spread, 'vir', split_axis=0, concat_axis=0, tiled=True)]
where the time goes in v2:
time: 219 us; the launch traced here: 218 us
  waiting for transfers between devices  128 us (58%)
  matrix products  47.2 us (22%)
  starting transfers between devices  26.3 us (12%)
  local copies, waits for them, and re-layouts  9.9 us (5%)
  other arithmetic  6.64 us (3%)
    all_to_all x1, waiting for transfers between devices, per_device(): lax.all_to_all(spread, 'vir', split_axis=0, concat_axis=0, tiled=True)  57.8 us
    all_to_all x1, waiting for transfers between devices, per_device(): lax.all_to_all(blocks, 'vir', split_axis=0, concat_axis=0, tiled=True)  54.2 us
    dot_general x3, matrix products, half_product(): jnp.einsum('pcd,bd->pbc', gathered, factor, preferred_element_type=jnp.fl...  28.1 us
    all_to_all x1, starting transfers between devices, per_device(): lax.all_to_all(spread, 'vir', split_axis=0, concat_axis=0, tiled=True)  11 us
    dot_general x1, matrix products, per_device(): jnp.einsum('qac,qbc->ab', halves[:, 1], factors, preferred_element_type=j...  10.8 us
    all_to_all x1, waiting for transfers between devices, per_device(): lax.all_to_all(own_rows, 'vir', split_axis=1, concat_axis=0, tiled=True)  10.1 us
    dot_general x1, matrix products, per_device(): jnp.einsum('qac,qbc->ab', factors, halves[:, 0], preferred_element_type=j...  8.3 us
    ppermute x2, starting transfers between devices, passed_along(): return lax.ppermute(block, axis, route)  6.29 us
  transfers between devices with their start and end apart: 5, of which 5 were waited for; matrix products, arithmetic and copies ran while one was open for 0% of the time, Pallas kernels for 0%

profile of v2, /device:TPU:0, one launch (start us, length us, event | category | flops | bytes accessed | tf_op | source)
XLA Modules:
  0.0 217.9 jit_solution(9271944882889166725)
XLA Ops:
  0.0 0.9 bitcast_select_fusion.3
  0.9 1.7 collective-permute-start
  2.6 2.6 %collective-permute-done = bf16[32,1024]{1,0:T(8,128)(2,1)S(1)} collective-permute-done((bf16[32,1024]{1,0:T(8,128)(2,1)S(1)}, bf16[32,1024]{1,0:T(8,128)(2,1)S(1)}, u32[]{:S(2)}, u32[]{:S(2)}) %collective-permute-start) | collective-permute-done | bytes 65568 | tf_op jit(solution)/shard_map/ppermute | solution.py:10
  5.2 0.9 fusion.14
  6.2 2.5 %broadcast_in_dim.64 = bf16[32,2,32,1024]{3,2,1,0:T(8,128)(2,1)} broadcast(bf16[2,32,1024]{2,1,0:T(8,128)(2,1)S(1)} %pad_maximum_fusion), dimensions={1,2,3} | broadcast | bytes 4325376 | tf_op jit(solution)/shard_map/broadcast_in_dim | solution.py:28
  8.6 11.0 %all-to-all-start = ((bf16[32,2,32,1024]{3,2,1,0:T(8,128)(2,1)}), bf16[32,2,32,1024]{3,2,1,0:T(8,128)(2,1)}, u32[]{:S(2)}, u32[]{:S(2)}) async-start(bf16[32,2,32,1024]{3,2,1,0:T(8,128)(2,1)} %broadcast_in_dim.64), calls=%async_computation | async-start | bytes 8388608 | tf_op jit(solution)/shard_map/all_to_all | solution.py:29
  19.7 57.8 %all-to-all-done = bf16[32,2,32,1024]{3,2,1,0:T(8,128)(2,1)} async-done(((bf16[32,2,32,1024]{3,2,1,0:T(8,128)(2,1)}), bf16[32,2,32,1024]{3,2,1,0:T(8,128)(2,1)}, u32[]{:S(2)}, u32[]{:S(2)}) %all-to-all-start) | async-done | bytes 4194336 | tf_op jit(solution)/shard_map/all_to_all | solution.py:29
  77.5 4.9 %copy.19 = bf16[32,2,32,1024]{3,2,0,1:T(8,128)(2,1)} copy(bf16[32,2,32,1024]{3,2,1,0:T(8,128)(2,1)} %all-to-all-done) | data formatting | bytes 8388608 | tf_op jit(solution)/shard_map/all_to_all | solution.py:29
  82.4 28.1 %while.10 = (s32[]{:T(128)}, bf16[3,2,1024,1024]{3,2,0,1:T(8,128)(2,1)}, bf16[3,1024,1024]{2,1,0:T(8,128)(2,1)}, bf16[2,1024,1024]{2,1,0:T(8,128)(2,1)}, s32[]{:T(128)}) while((s32[]{:T(128)}, bf16[3,2,1024,1024]{3,2,0,1:T(8,128)(2,1)}, bf16[3,1024,1024]{2,1,0:T(8,128)(2,1)}, bf16[2,1024,1024]{2,1,0:T(8,128)(2,1)}, s32[]{:T(128)}) %tuple.26), condition=%wide.region_3.4_spmd, body=%wide.region_2.3_spmd.sunk | while | flops 4297064448 | bytes 10486845 | solution.py:36
  82.4 9.3 %bitcast_dynamic-update-slice_fusion.2 = bf16[3,2,1024,1024]{3,2,0,1:T(8,128)(2,1)} fusion(bf16[3,2,1024,1024]{3,2,0,1:T(8,128)(2,1)} %get-tuple-element.77, s32[]{:T(128)} %get-tuple-element.76, bf16[2,1024,1024]{2,1,0:T(8,128)(2,1)} %get-tuple-element.84, bf16[3,1024,1024]{2,1,0:T(8,128)(2,1)} %get-tuple-element.83), kind=kOutput, calls=%fused_computation.clone.1 | convolution fusion | flops 4297064448 | bytes 10486784 | tf_op jit(solution)/shard_map/while/body/eval_jaxpr/pcd,bd->pbc/dot_general | solution.py:33
  91.7 9.4 %bitcast_dynamic-update-slice_fusion.2 = bf16[3,2,1024,1024]{3,2,0,1:T(8,128)(2,1)} fusion(bf16[3,2,1024,1024]{3,2,0,1:T(8,128)(2,1)} %get-tuple-element.77, s32[]{:T(128)} %get-tuple-element.76, bf16[2,1024,1024]{2,1,0:T(8,128)(2,1)} %get-tuple-element.84, bf16[3,1024,1024]{2,1,0:T(8,128)(2,1)} %get-tuple-element.83), kind=kOutput, calls=%fused_computation.clone.1 | convolution fusion | flops 4297064448 | bytes 10486784 | tf_op jit(solution)/shard_map/while/body/eval_jaxpr/pcd,bd->pbc/dot_general | solution.py:33
  101.2 9.3 %bitcast_dynamic-update-slice_fusion.2 = bf16[3,2,1024,1024]{3,2,0,1:T(8,128)(2,1)} fusion(bf16[3,2,1024,1024]{3,2,0,1:T(8,128)(2,1)} %get-tuple-element.77, s32[]{:T(128)} %get-tuple-element.76, bf16[2,1024,1024]{2,1,0:T(8,128)(2,1)} %get-tuple-element.84, bf16[3,1024,1024]{2,1,0:T(8,128)(2,1)} %get-tuple-element.83), kind=kOutput, calls=%fused_computation.clone.1 | convolution fusion | flops 4297064448 | bytes 10486784 | tf_op jit(solution)/shard_map/while/body/eval_jaxpr/pcd,bd->pbc/dot_general | solution.py:33
  110.5 10.8 %fusion.3 = f32[1024,1024,1]{1,0,2:T(8,128)S(1)} fusion(bf16[3,1024,1024]{2,1,0:T(8,128)(2,1)} %get-tuple-element.95, bf16[3,2,1024,1024]{3,2,0,1:T(8,128)(2,1)} %get-tuple-element.27), kind=kOutput, calls=%fused_computation.4 | convolution fusion | flops 6442450944 | bytes 16777216 | tf_op jit(solution)/shard_map/qac,qbc->ab/dot_general | solution.py:38
  121.4 8.3 %bitcast_add_fusion = f32[1024,1024]{1,0:T(8,128)} fusion(f32[1024,1024,1]{1,0,2:T(8,128)S(1)} %fusion.3, bf16[3,1024,1024]{2,1,0:T(8,128)(2,1)S(1)} %copy-done.5, bf16[3,2,1024,1024]{3,2,0,1:T(8,128)(2,1)S(1)} %copy-done.6), kind=kOutput, calls=%fused_computation.10 | convolution fusion | flops 6443499520 | bytes 20971520 | tf_op jit(solution)/shard_map/qac,qbc->ab/dot_general | solution.py:37
  129.7 5.2 %all-to-all-start.1 = ((f32[32,32,1024]{2,1,0:T(8,128)}), f32[32,32,1024]{2,1,0:T(8,128)}, u32[]{:S(2)}, u32[]{:S(2)}) async-start(f32[32,32,1024]{2,1,0:T(8,128)} %bitcast.71), calls=%async_computation.1 | async-start | bytes 8388608 | tf_op jit(solution)/shard_map/all_to_all | solution.py:41
  135.6 54.2 %all-to-all-done.1 = f32[32,32,1024]{2,1,0:T(8,128)} async-done(((f32[32,32,1024]{2,1,0:T(8,128)}), f32[32,32,1024]{2,1,0:T(8,128)}, u32[]{:S(2)}, u32[]{:S(2)}) %all-to-all-start.1) | async-done | bytes 4194336 | tf_op jit(solution)/shard_map/all_to_all | solution.py:41
  189.8 2.4 %reduce_sum.47 = f32[32,1024]{1,0:T(8,128)S(1)} reduce(f32[32,32,1024]{2,1,0:T(8,128)} %all-to-all-done.1, f32[]{:T(128)} %constant.32.clone.1), dimensions={0}, to_apply=%region_4.5 | reduce | flops 1015808 | bytes 4325380 | tf_op jit(solution)/shard_map/reduce_sum | solution.py:42
  192.7 0.9 reshape.91
  193.6 3.9 %all-to-all-start.2 = ((f32[32,1,1024]{2,1,0:T(1,128)}), f32[32,1,1024]{2,1,0:T(1,128)S(1)}, u32[]{:S(2)}, u32[]{:S(2)}) async-start(f32[32,1,1024]{2,1,0:T(1,128)} %reshape.91), calls=%async_computation.2 | async-start | bytes 262144 | tf_op jit(solution)/shard_map/all_to_all | solution.py:43
  197.6 10.1 %all-to-all-done.2 = f32[32,1,1024]{2,1,0:T(1,128)S(1)} async-done(((f32[32,1,1024]{2,1,0:T(1,128)}), f32[32,1,1024]{2,1,0:T(1,128)S(1)}, u32[]{:S(2)}, u32[]{:S(2)}) %all-to-all-start.2) | async-done | bytes 131104 | tf_op jit(solution)/shard_map/all_to_all | solution.py:43
  208.2 1.0 reduce
  209.5 4.6 %collective-permute-start.1 = (f32[32,1024]{1,0:T(8,128)S(1)}, f32[32,1024]{1,0:T(8,128)S(1)}, u32[]{:S(2)}, u32[]{:S(2)}) collective-permute-start(f32[32,1024]{1,0:T(8,128)S(1)} %bitcast_select_fusion.1), channel_id=1, source_target_pairs={{64,0},{96,32},{0,64},{32,96},{65,1},{97,33},{1,65},{33,97},{66,2}... | collective-permute-start | bytes 393224 | tf_op jit(solution)/shard_map/ppermute | solution.py:10
  214.2 2.9 %collective-permute-done.1 = f32[32,1024]{1,0:T(8,128)S(1)} collective-permute-done((f32[32,1024]{1,0:T(8,128)S(1)}, f32[32,1024]{1,0:T(8,128)S(1)}, u32[]{:S(2)}, u32[]{:S(2)}) %collective-permute-start.1) | collective-permute-done | bytes 131104 | tf_op jit(solution)/shard_map/ppermute | solution.py:10
  217.1 0.8 fusion.11
  (33 shorter events, 2.2 us)
Async XLA Ops:
  0.0 135.0 %copy-start = (s32[8,2]{0,1:T(2,128)S(1)}, s32[8,2]{0,1:T(2,128)}, u32[]{:S(2)}) copy-start(s32[8,2]{0,1:T(2,128)} %param.15) | copy-start | bytes 196
  0.9 4.3 %collective-permute-start = (bf16[32,1024]{1,0:T(8,128)(2,1)S(1)}, bf16[32,1024]{1,0:T(8,128)(2,1)S(1)}, u32[]{:S(2)}, u32[]{:S(2)}) collective-permute-start(bf16[32,1024]{1,0:T(8,128)(2,1)S(1)} %bitcast_select_fusion.3), channel_id=1, source_target_pairs={{64,0},{96,32},{0,64},{32,96},{65,1},{97,33},{1,65},{33,97},{66,2}... | collective-permute-start | bytes 196616 | tf_op jit(solution)/shard_map/ppermute | solution.py:10
  8.6 68.8 %all-to-all-start = ((bf16[32,2,32,1024]{3,2,1,0:T(8,128)(2,1)}), bf16[32,2,32,1024]{3,2,1,0:T(8,128)(2,1)}, u32[]{:S(2)}, u32[]{:S(2)}) async-start(bf16[32,2,32,1024]{3,2,1,0:T(8,128)(2,1)} %broadcast_in_dim.64), calls=%async_computation | async-start | bytes 8388608 | tf_op jit(solution)/shard_map/all_to_all | solution.py:29
  110.5 10.8 %copy-start.5 = (bf16[3,1024,1024]{2,1,0:T(8,128)(2,1)S(1)}, bf16[3,1024,1024]{2,1,0:T(8,128)(2,1)}, u32[]{:S(2)}) copy-start(bf16[3,1024,1024]{2,1,0:T(8,128)(2,1)} %get-tuple-element.95) | copy-start | bytes 18874372
  110.5 10.8 %copy-start.6 = (bf16[3,2,1024,1024]{3,2,0,1:T(8,128)(2,1)S(1)}, bf16[3,2,1024,1024]{3,2,0,1:T(8,128)(2,1)}, u32[]{:S(2)}) copy-start(bf16[3,2,1024,1024]{3,2,0,1:T(8,128)(2,1)} %get-tuple-element.27) | copy-start | bytes 37748740
  129.6 5.2 %copy-start.1 = (s32[1024]{0:T(1024)S(1)}, s32[1024]{0:T(1024)}, u32[]{:S(2)}) copy-start(s32[1024]{0:T(1024)} %param.14) | copy-start | bytes 12292
  129.7 5.3 %copy-start.2 = (f32[1024]{0:T(1024)S(1)}, f32[1024]{0:T(1024)}, u32[]{:S(2)}) copy-start(f32[1024]{0:T(1024)} %param.12) | copy-start | bytes 12292
  129.7 5.5 %copy-start.3 = (s32[100]{0:T(128)S(1)}, s32[100]{0:T(128)}, u32[]{:S(2)}) copy-start(s32[100]{0:T(128)} %param.13) | copy-start | bytes 1204
  129.7 5.7 %copy-start.4 = (f32[100]{0:T(128)S(1)}, f32[100]{0:T(128)}, u32[]{:S(2)}) copy-start(f32[100]{0:T(128)} %param.11) | copy-start | bytes 1204
  129.7 60.1 %all-to-all-start.1 = ((f32[32,32,1024]{2,1,0:T(8,128)}), f32[32,32,1024]{2,1,0:T(8,128)}, u32[]{:S(2)}, u32[]{:S(2)}) async-start(f32[32,32,1024]{2,1,0:T(8,128)} %bitcast.71), calls=%async_computation.1 | async-start | bytes 8388608 | tf_op jit(solution)/shard_map/all_to_all | solution.py:41
  193.6 14.1 %all-to-all-start.2 = ((f32[32,1,1024]{2,1,0:T(1,128)}), f32[32,1,1024]{2,1,0:T(1,128)S(1)}, u32[]{:S(2)}, u32[]{:S(2)}) async-start(f32[32,1,1024]{2,1,0:T(1,128)} %reshape.91), calls=%async_computation.2 | async-start | bytes 262144 | tf_op jit(solution)/shard_map/all_to_all | solution.py:43
  209.5 7.5 %collective-permute-start.1 = (f32[32,1024]{1,0:T(8,128)S(1)}, f32[32,1024]{1,0:T(8,128)S(1)}, u32[]{:S(2)}, u32[]{:S(2)}) collective-permute-start(f32[32,1024]{1,0:T(8,128)S(1)} %bitcast_select_fusion.1), channel_id=1, source_target_pairs={{64,0},{96,32},{0,64},{32,96},{65,1},{97,33},{1,65},{33,97},{66,2}... | collective-permute-start | bytes 393224 | tf_op jit(solution)/shard_map/ppermute | solution.py:10

commit v3 on v1

--- a/solution.py
+++ b/solution.py
@@ -24,18 +24,35 @@
     incoming = passed_along(outgoing, "occ", occ_devices // 2)
     first = jnp.where(lower_half, amplitudes[0], incoming)
     second = jnp.where(lower_half, incoming, amplitudes[1])
-    couple = jnp.stack([first, second], axis=0)
-    gathered = lax.all_gather(couple, "vir", axis=1, tiled=True)
+    def gather_rows(block):
+        spread = jnp.broadcast_to(block[None], (vir_devices,) + block.shape)
+        pieces = lax.all_to_all(spread, "vir", split_axis=0, concat_axis=0, tiled=True)
+        return pieces.reshape(vir_devices * row_count, block.shape[-1])
 
-    def half_product(factor):
-        product = jnp.einsum("pcd,bd->pbc", gathered, factor, preferred_element_type=jnp.float32)
-        return product.astype(jnp.bfloat16)
+    def half_products(rows):
+        def half_product(factor):
+            product = jnp.einsum("cd,bd->bc", rows, factor, preferred_element_type=jnp.float32)
+            return product.astype(jnp.bfloat16)
 
-    halves = lax.map(half_product, factors)
-    direct = jnp.einsum("qac,qbc->ab", factors, halves[:, 0], preferred_element_type=jnp.float32)
-    turned_term = jnp.einsum("qac,qbc->ab", halves[:, 1], factors, preferred_element_type=jnp.float32)
-    combined = direct + turned_term
-    own_rows = lax.psum_scatter(combined, "vir", scatter_dimension=0, tiled=True)
+        return lax.map(half_product, factors)
+
+    halves_first = half_products(gather_rows(first))
+    halves_second = half_products(gather_rows(second))
+    width = factors.shape[1]
+    chunks = 4
+    chunk = width // chunks
+    own_parts = []
+    for part in range(chunks):
+        cut = slice(part * chunk, (part + 1) * chunk)
+        direct = jnp.einsum("qac,qbc->ab", factors, halves_first[:, cut], preferred_element_type=jnp.float32)
+        turned_term = jnp.einsum(
+            "qac,qbc->ab", halves_second, factors[:, cut], preferred_element_type=jnp.float32
+        )
+        combined = direct + turned_term
+        blocks = combined.reshape(vir_devices, row_count, chunk)
+        arrived = lax.all_to_all(blocks, "vir", split_axis=0, concat_axis=0, tiled=True)
+        own_parts.append(jnp.sum(arrived, axis=0))
+    own_rows = jnp.concatenate(own_parts, axis=1)
     cols = lax.all_to_all(own_rows, "vir", split_axis=1, concat_axis=0, tiled=True)
     own_cols = jnp.transpose(cols, (1, 0))
     outgoing_block = jnp.where(lower_half, own_cols, own_rows)

time: 381 us -> 224 us (0.59)
  waiting for transfers between devices: 289 us -> 77 us
  starting transfers between devices: 7.5 us -> 44.3 us
  matrix products: 50.1 us -> 72.4 us
  between operations: 13.5 us -> 0.32 us
  local copies, waits for them, and re-layouts: 15.1 us -> 22 us
    reduce_scatter x1 -> x0, waiting for transfers between devices: 190 us -> none  [per_device(): lax.psum_scatter(combined, 'vir', scatter_dimension=0, tiled=True)]
    all_gather x1 -> x0, waiting for transfers between devices: 82.9 us -> none  [per_device(): gathered = lax.all_gather(couple, 'vir', axis=1, tiled=True)]
    all_to_all x0 -> x6, waiting for transfers between devices: none -> 61.2 us  [the longest x2 34.7 us: gather_rows(): lax.all_to_all(spread, 'vir', split_axis=0, concat_axis=0, tiled=True)]
    all_to_all x0 -> x6, starting transfers between devices: none -> 36.7 us  [the longest x4 21.8 us: per_device(): lax.all_to_all(blocks, 'vir', split_axis=0, concat_axis=0, tiled=True)]
    dot_general x5 -> x14, matrix products: 50.1 us -> 72.4 us  [the longest x6 33.8 us: half_product(): jnp.einsum('cd,bd->bc', rows, factor, preferred_element_type=jnp.float32)]
    add x0 -> x4, local copies, waits for them, and re-layouts: none -> 9.01 us  [per_device(): combined = direct + turned_term]
    unnamed x18 -> x26, local copies, waits for them, and re-layouts: 7.57 us -> 1.33 us
    another operation x1 -> x2, local copies, waits for them, and re-layouts: 0.79 us -> 6.89 us  [per_device(): couple = jnp.stack([first, second], axis=0)]
  transfers between devices with their start and end apart: 5 -> 9, of which waited for: 5 -> 9; matrix products, arithmetic and copies ran while one was open for 0% -> 30% of each run, Pallas kernels for 0% -> 0%
where the time goes in v3:
time: 224 us; the launch traced here: 223 us
  waiting for transfers between devices  77 us (34%)
  matrix products  72.4 us (32%)
  starting transfers between devices  44.3 us (20%)
  local copies, waits for them, and re-layouts  22 us (10%)
  other arithmetic  6.94 us (3%)
    all_to_all x2, waiting for transfers between devices, gather_rows(): lax.all_to_all(spread, 'vir', split_axis=0, concat_axis=0, tiled=True)  34.7 us
    dot_general x6, matrix products, half_product(): jnp.einsum('cd,bd->bc', rows, factor, preferred_element_type=jnp.float32)  33.8 us
    all_to_all x4, waiting for transfers between devices, per_device(): lax.all_to_all(blocks, 'vir', split_axis=0, concat_axis=0, tiled=True)  26.4 us
    all_to_all x4, starting transfers between devices, per_device(): lax.all_to_all(blocks, 'vir', split_axis=0, concat_axis=0, tiled=True)  21.8 us
    dot_general x4, matrix products, per_device(): jnp.einsum('qac,qbc->ab', factors, halves_first[:, cut], preferred_elemen...  20.8 us
    dot_general x4, matrix products, per_device(): jnp.einsum('qac,qbc->ab', halves_second, factors[:, cut], preferred_eleme...  17.8 us
    all_to_all x2, starting transfers between devices, gather_rows(): lax.all_to_all(spread, 'vir', split_axis=0, concat_axis=0, tiled=True)  14.9 us
    all_to_all x1, waiting for transfers between devices, per_device(): lax.all_to_all(own_rows, 'vir', split_axis=1, concat_axis=0, tiled=True)  10.1 us
  transfers between devices with their start and end apart: 9, of which 9 were waited for; matrix products, arithmetic and copies ran while one was open for 30% of the time, Pallas kernels for 0%

profile of v3, /device:TPU:0, one launch (start us, length us, event | category | flops | bytes accessed | tf_op | source)
XLA Modules:
  0.0 223.0 jit_solution(12529992736071782220)
XLA Ops:
  7.7 10.9 %all-to-all-start = ((bf16[32,32,1024]{2,1,0:T(8,128)(2,1)}), bf16[32,32,1024]{2,1,0:T(8,128)(2,1)S(1)}, u32[]{:S(2)}, u32[]{:S(2)}) async-start(bf16[32,32,1024]{2,1,0:T(8,128)(2,1)} %broadcast_in_dim.69), calls=%async_computation | async-start | bytes 4194304 | tf_op jit(solution)/shard_map/all_to_all | solution.py:29
  18.6 30.4 %all-to-all-done = bf16[32,32,1024]{2,1,0:T(8,128)(2,1)S(1)} async-done(((bf16[32,32,1024]{2,1,0:T(8,128)(2,1)}), bf16[32,32,1024]{2,1,0:T(8,128)(2,1)S(1)}, u32[]{:S(2)}, u32[]{:S(2)}) %all-to-all-start) | async-done | bytes 2097184 | tf_op jit(solution)/shard_map/all_to_all | solution.py:29
  58.5 17.8 %while.20 = (s32[]{:T(128)}, bf16[3,1024,1024]{2,1,0:T(8,128)(2,1)}, bf16[3,1024,1024]{2,1,0:T(8,128)(2,1)}, bf16[1024,1024]{1,0:T(8,128)(2,1)}, s32[]{:T(128)}) while((s32[]{:T(128)}, bf16[3,1024,1024]{2,1,0:T(8,128)(2,1)}, bf16[3,1024,1024]{2,1,0:T(8,128)(2,1)}, bf16[1024,1024]{1,0:T(8,128)(2,1)}, s32[]{:T(128)}) %tuple.43), condition=%wide.region_3.4_spmd, body=%wide.region_2.3_spmd.sunk | while | flops 2148532224 | bytes 6292549 | solution.py:37
  58.5 5.9 %bitcast_dynamic-update-slice_fusion.4 = bf16[3,1024,1024]{2,1,0:T(8,128)(2,1)} fusion(bf16[3,1024,1024]{2,1,0:T(8,128)(2,1)} %get-tuple-element.133, s32[]{:T(128)S(6)} %copy.65, bf16[1024,1024]{1,0:T(8,128)(2,1)} %get-tuple-element.140, bf16[3,1024,1024]{2,1,0:T(8,128)(2,1)} %get-tuple-element.139), kind=kOutput, calls=%fused_computation.clone.1 | convolution fusion | flops 2148532224 | bytes 6292480 | tf_op jit(solution)/shard_map/while/body/eval_jaxpr/cd,bd->bc/dot_general | solution.py:34
  64.4 5.9 %bitcast_dynamic-update-slice_fusion.4 = bf16[3,1024,1024]{2,1,0:T(8,128)(2,1)} fusion(bf16[3,1024,1024]{2,1,0:T(8,128)(2,1)} %get-tuple-element.133, s32[]{:T(128)S(6)} %copy.65, bf16[1024,1024]{1,0:T(8,128)(2,1)} %get-tuple-element.140, bf16[3,1024,1024]{2,1,0:T(8,128)(2,1)} %get-tuple-element.139), kind=kOutput, calls=%fused_computation.clone.1 | convolution fusion | flops 2148532224 | bytes 6292480 | tf_op jit(solution)/shard_map/while/body/eval_jaxpr/cd,bd->bc/dot_general | solution.py:34
  70.3 5.9 %bitcast_dynamic-update-slice_fusion.4 = bf16[3,1024,1024]{2,1,0:T(8,128)(2,1)} fusion(bf16[3,1024,1024]{2,1,0:T(8,128)(2,1)} %get-tuple-element.133, s32[]{:T(128)S(6)} %copy.65, bf16[1024,1024]{1,0:T(8,128)(2,1)} %get-tuple-element.140, bf16[3,1024,1024]{2,1,0:T(8,128)(2,1)} %get-tuple-element.139), kind=kOutput, calls=%fused_computation.clone.1 | convolution fusion | flops 2148532224 | bytes 6292480 | tf_op jit(solution)/shard_map/while/body/eval_jaxpr/cd,bd->bc/dot_general | solution.py:34
  76.2 5.1 %fusion.28 = f32[1024,256]{0,1:T(8,128)S(1)} fusion(bf16[3,1024,1024]{2,1,0:T(8,128)(2,1)} %get-tuple-element.172, bf16[3,1024,1024]{2,1,0:T(8,128)(2,1)} %get-tuple-element.49), kind=kOutput, calls=%fused_computation.26 | convolution fusion | flops 1610612736 | bytes 8912896 | tf_op jit(solution)/shard_map/qac,qbc->ab/dot_general | solution.py:47
  81.3 4.4 %all-to-all-done.1 = bf16[32,32,1024]{2,1,0:T(8,128)(2,1)S(1)} async-done(((bf16[32,32,1024]{2,1,0:T(8,128)(2,1)}), bf16[32,32,1024]{2,1,0:T(8,128)(2,1)S(1)}, u32[]{:S(2)}, u32[]{:S(2)}) %all-to-all-start.1) | async-done | bytes 2097184 | tf_op jit(solution)/shard_map/all_to_all | solution.py:29
  89.1 16.0 %while.21 = (s32[]{:T(128)}, bf16[3,1024,1024]{2,1,0:T(8,128)(2,1)}, bf16[3,1024,1024]{2,1,0:T(8,128)(2,1)}, bf16[1024,1024]{1,0:T(8,128)(2,1)S(1)}, s32[]{:T(128)}) while((s32[]{:T(128)}, bf16[3,1024,1024]{2,1,0:T(8,128)(2,1)}, bf16[3,1024,1024]{2,1,0:T(8,128)(2,1)}, bf16[1024,1024]{1,0:T(8,128)(2,1)S(1)}, s32[]{:T(128)}) %tuple.44), condition=%wide.region_5.6_spmd, body=%wide.region_4.5_spmd.sunk | while | flops 2148532224 | bytes 6292549 | solution.py:37
  89.1 5.3 %bitcast_dynamic-update-slice_fusion.5 = bf16[3,1024,1024]{2,1,0:T(8,128)(2,1)} fusion(bf16[3,1024,1024]{2,1,0:T(8,128)(2,1)} %get-tuple-element.148, s32[]{:T(128)S(6)} %copy.71, bf16[1024,1024]{1,0:T(8,128)(2,1)S(1)} %get-tuple-element.155, bf16[3,1024,1024]{2,1,0:T(8,128)(2,1)} %get-tuple-element.154), kind=kOutput, calls=%fused_computation.5.clone.1 | convolution fusion | flops 2148532224 | bytes 6292480 | tf_op jit(solution)/shard_map/while/body/eval_jaxpr/cd,bd->bc/dot_general | solution.py:34
  94.4 5.4 %bitcast_dynamic-update-slice_fusion.5 = bf16[3,1024,1024]{2,1,0:T(8,128)(2,1)} fusion(bf16[3,1024,1024]{2,1,0:T(8,128)(2,1)} %get-tuple-element.148, s32[]{:T(128)S(6)} %copy.71, bf16[1024,1024]{1,0:T(8,128)(2,1)S(1)} %get-tuple-element.155, bf16[3,1024,1024]{2,1,0:T(8,128)(2,1)} %get-tuple-element.154), kind=kOutput, calls=%fused_computation.5.clone.1 | convolution fusion | flops 2148532224 | bytes 6292480 | tf_op jit(solution)/shard_map/while/body/eval_jaxpr/cd,bd->bc/dot_general | solution.py:34
  99.8 5.3 %bitcast_dynamic-update-slice_fusion.5 = bf16[3,1024,1024]{2,1,0:T(8,128)(2,1)} fusion(bf16[3,1024,1024]{2,1,0:T(8,128)(2,1)} %get-tuple-element.148, s32[]{:T(128)S(6)} %copy.71, bf16[1024,1024]{1,0:T(8,128)(2,1)S(1)} %get-tuple-element.155, bf16[3,1024,1024]{2,1,0:T(8,128)(2,1)} %get-tuple-element.154), kind=kOutput, calls=%fused_computation.5.clone.1 | convolution fusion | flops 2148532224 | bytes 6292480 | tf_op jit(solution)/shard_map/while/body/eval_jaxpr/cd,bd->bc/dot_general | solution.py:34
  105.1 5.1 %fusion.61 = f32[1024,256]{0,1:T(8,128)S(1)} fusion(f32[1024,256]{0,1:T(8,128)S(1)} %fusion.28, bf16[3,1024,1024]{2,1,0:T(8,128)(2,1)} %get-tuple-element.50, bf16[3,1024,1024]{2,1,0:T(8,128)(2,1)} %get-tuple-element.173), kind=kOutput, calls=%fused_computation.37 | convolution fusion | flops 1610874880 | bytes 9961472 | tf_op jit(solution)/shard_map/qac,qbc->ab/dot_general | solution.py:48
  111.6 5.8 %all-to-all-start.2 = ((f32[32,32,256]{2,1,0:T(8,128)}), f32[32,32,256]{2,1,0:T(8,128)S(1)}, u32[]{:S(2)}, u32[]{:S(2)}) async-start(f32[32,32,256]{2,1,0:T(8,128)} %bitcast.108), calls=%async_computation.2 | async-start | bytes 2097152 | tf_op jit(solution)/shard_map/all_to_all | solution.py:53
  117.3 5.2 %fusion.46 = f32[1024,256]{0,1:T(8,128)S(1)} fusion(bf16[3,1024,1024]{2,1,0:T(8,128)(2,1)} %get-tuple-element.173, bf16[3,1024,1024]{2,1,0:T(8,128)(2,1)} %get-tuple-element.49), kind=kOutput, calls=%fused_computation.32 | convolution fusion | flops 1610612736 | bytes 8912896 | tf_op jit(solution)/shard_map/qac,qbc->ab/dot_general | solution.py:47
  129.4 5.7 %all-to-all-done.2 = f32[32,32,256]{2,1,0:T(8,128)S(1)} async-done(((f32[32,32,256]{2,1,0:T(8,128)}), f32[32,32,256]{2,1,0:T(8,128)S(1)}, u32[]{:S(2)}, u32[]{:S(2)}) %all-to-all-start.2) | async-done | bytes 1048608 | tf_op jit(solution)/shard_map/all_to_all | solution.py:53
  135.1 4.8 %all-to-all-start.5 = ((f32[32,32,256]{2,1,0:T(8,128)}), f32[32,32,256]{2,1,0:T(8,128)}, u32[]{:S(2)}, u32[]{:S(2)}) async-start(f32[32,32,256]{2,1,0:T(8,128)} %bitcast.107), calls=%async_computation.5 | async-start | bytes 2097152 | tf_op jit(solution)/shard_map/all_to_all | solution.py:53
  139.9 5.2 %fusion.34 = f32[1024,256]{0,1:T(8,128)S(1)} fusion(bf16[3,1024,1024]{2,1,0:T(8,128)(2,1)} %get-tuple-element.173, bf16[3,1024,1024]{2,1,0:T(8,128)(2,1)} %get-tuple-element.49), kind=kOutput, calls=%fused_computation.28 | convolution fusion | flops 1610612736 | bytes 8912896 | tf_op jit(solution)/shard_map/qac,qbc->ab/dot_general | solution.py:47
  152.0 4.7 %all-to-all-done.5 = f32[32,32,256]{2,1,0:T(8,128)} async-done(((f32[32,32,256]{2,1,0:T(8,128)}), f32[32,32,256]{2,1,0:T(8,128)}, u32[]{:S(2)}, u32[]{:S(2)}) %all-to-all-start.5) | async-done | bytes 1048608 | tf_op jit(solution)/shard_map/all_to_all | solution.py:53
  156.6 5.5 %all-to-all-start.3 = ((f32[32,32,256]{2,1,0:T(8,128)}), f32[32,32,256]{2,1,0:T(8,128)}, u32[]{:S(2)}, u32[]{:S(2)}) async-start(f32[32,32,256]{2,1,0:T(8,128)} %bitcast.106), calls=%async_computation.3 | async-start | bytes 2097152 | tf_op jit(solution)/shard_map/all_to_all | solution.py:53
  162.2 5.2 %fusion.40 = f32[1024,256]{0,1:T(8,128)S(1)} fusion(bf16[3,1024,1024]{2,1,0:T(8,128)(2,1)} %get-tuple-element.173, bf16[3,1024,1024]{2,1,0:T(8,128)(2,1)} %get-tuple-element.49), kind=kOutput, calls=%fused_computation.30 | convolution fusion | flops 1610612736 | bytes 8912896 | tf_op jit(solution)/shard_map/qac,qbc->ab/dot_general | solution.py:47
  178.1 5.7 %all-to-all-start.4 = ((f32[32,32,256]{2,1,0:T(8,128)}), f32[32,32,256]{2,1,0:T(8,128)S(1)}, u32[]{:S(2)}, u32[]{:S(2)}) async-start(f32[32,32,256]{2,1,0:T(8,128)} %bitcast.21), calls=%async_computation.4 | async-start | bytes 2097152 | tf_op jit(solution)/shard_map/all_to_all | solution.py:53
  187.3 12.2 %all-to-all-done.4 = f32[32,32,256]{2,1,0:T(8,128)S(1)} async-done(((f32[32,32,256]{2,1,0:T(8,128)}), f32[32,32,256]{2,1,0:T(8,128)S(1)}, u32[]{:S(2)}, u32[]{:S(2)}) %all-to-all-start.4) | async-done | bytes 1048608 | tf_op jit(solution)/shard_map/all_to_all | solution.py:53
  205.1 10.1 %all-to-all-done.6 = f32[32,1,1024]{2,1,0:T(1,128)S(1)} async-done(((f32[32,1,1024]{2,1,0:T(1,128)}), f32[32,1,1024]{2,1,0:T(1,128)S(1)}, u32[]{:S(2)}, u32[]{:S(2)}) %all-to-all-start.6) | async-done | bytes 131104 | tf_op jit(solution)/shard_map/all_to_all | solution.py:56
  (72 shorter events, 62.8 us)
Async XLA Ops:
  0.0 184.0 %copy-start = (s32[8,2]{0,1:T(2,128)S(1)}, s32[8,2]{0,1:T(2,128)}, u32[]{:S(2)}) copy-start(s32[8,2]{0,1:T(2,128)} %param.17) | copy-start | bytes 196
  0.9 4.3 %collective-permute-start = (bf16[32,1024]{1,0:T(8,128)(2,1)S(1)}, bf16[32,1024]{1,0:T(8,128)(2,1)S(1)}, u32[]{:S(2)}, u32[]{:S(2)}) collective-permute-start(bf16[32,1024]{1,0:T(8,128)(2,1)S(1)} %bitcast_select_fusion.3), channel_id=1, source_target_pairs={{64,0},{96,32},{0,64},{32,96},{65,1},{97,33},{1,65},{33,97},{66,2}... | collective-permute-start | bytes 196616 | tf_op jit(solution)/shard_map/ppermute | solution.py:10
  7.7 41.3 %all-to-all-start = ((bf16[32,32,1024]{2,1,0:T(8,128)(2,1)}), bf16[32,32,1024]{2,1,0:T(8,128)(2,1)S(1)}, u32[]{:S(2)}, u32[]{:S(2)}) async-start(bf16[32,32,1024]{2,1,0:T(8,128)(2,1)} %broadcast_in_dim.69), calls=%async_computation | async-start | bytes 4194304 | tf_op jit(solution)/shard_map/all_to_all | solution.py:29
  49.0 2.0 copy-start.1
  51.0 34.7 %all-to-all-start.1 = ((bf16[32,32,1024]{2,1,0:T(8,128)(2,1)}), bf16[32,32,1024]{2,1,0:T(8,128)(2,1)S(1)}, u32[]{:S(2)}, u32[]{:S(2)}) async-start(bf16[32,32,1024]{2,1,0:T(8,128)(2,1)} %broadcast_in_dim.70), calls=%async_computation.1 | async-start | bytes 4194304 | tf_op jit(solution)/shard_map/all_to_all | solution.py:29
  111.6 11.0 %slice-start = ((s8[6291456]{0:T(1024)(128)(4,1)}), s8[2097152]{0:T(1024)(128)(4,1)S(1)}, s32[]{:S(2)}) async-start(s8[6291456]{0:T(1024)(128)(4,1)} %bitcast.100), calls=%async_computation.7 | async-start | bytes 4194304
  111.6 23.5 %all-to-all-start.2 = ((f32[32,32,256]{2,1,0:T(8,128)}), f32[32,32,256]{2,1,0:T(8,128)S(1)}, u32[]{:S(2)}, u32[]{:S(2)}) async-start(f32[32,32,256]{2,1,0:T(8,128)} %bitcast.108), calls=%async_computation.2 | async-start | bytes 2097152 | tf_op jit(solution)/shard_map/all_to_all | solution.py:53
  117.3 5.3 %slice-start.1 = ((s8[6291456]{0:T(1024)(128)(4,1)}), s8[4194304]{0:T(1024)(128)(4,1)S(1)}, s32[]{:S(2)}) async-start(s8[6291456]{0:T(1024)(128)(4,1)} %bitcast.100), calls=%async_computation.8 | async-start | bytes 8388608
  135.1 10.1 %slice-start.2 = ((s8[6291456]{0:T(1024)(128)(4,1)}), s8[2097152]{0:T(1024)(128)(4,1)S(1)}, s32[]{:S(2)}) async-start(s8[6291456]{0:T(1024)(128)(4,1)} %bitcast.102), calls=%async_computation.9 | async-start | bytes 4194304
  135.1 21.6 %all-to-all-start.5 = ((f32[32,32,256]{2,1,0:T(8,128)}), f32[32,32,256]{2,1,0:T(8,128)}, u32[]{:S(2)}, u32[]{:S(2)}) async-start(f32[32,32,256]{2,1,0:T(8,128)} %bitcast.107), calls=%async_computation.5 | async-start | bytes 2097152 | tf_op jit(solution)/shard_map/all_to_all | solution.py:53
  139.9 5.3 %slice-start.3 = ((s8[6291456]{0:T(1024)(128)(4,1)}), s8[4194304]{0:T(1024)(128)(4,1)S(1)}, s32[]{:S(2)}) async-start(s8[6291456]{0:T(1024)(128)(4,1)} %bitcast.102), calls=%async_computation.10 | async-start | bytes 8388608
  156.6 10.8 %slice-start.4 = ((s8[6291456]{0:T(1024)(128)(4,1)}), s8[2097152]{0:T(1024)(128)(4,1)S(1)}, s32[]{:S(2)}) async-start(s8[6291456]{0:T(1024)(128)(4,1)} %bitcast.104), calls=%async_computation.11 | async-start | bytes 4194304
  156.6 21.5 %all-to-all-start.3 = ((f32[32,32,256]{2,1,0:T(8,128)}), f32[32,32,256]{2,1,0:T(8,128)}, u32[]{:S(2)}, u32[]{:S(2)}) async-start(f32[32,32,256]{2,1,0:T(8,128)} %bitcast.106), calls=%async_computation.3 | async-start | bytes 2097152 | tf_op jit(solution)/shard_map/all_to_all | solution.py:53
  162.2 5.3 %slice-start.5 = ((s8[6291456]{0:T(1024)(128)(4,1)}), s8[4194304]{0:T(1024)(128)(4,1)S(1)}, s32[]{:S(2)}) async-start(s8[6291456]{0:T(1024)(128)(4,1)} %bitcast.104), calls=%async_computation.12 | async-start | bytes 8388608
  167.5 16.4 %copy-start.3 = (f32[1024]{0:T(1024)S(1)}, f32[1024]{0:T(1024)}, u32[]{:S(2)}) copy-start(f32[1024]{0:T(1024)} %param.14) | copy-start | bytes 12292
  167.5 16.5 %copy-start.2 = (s32[1024]{0:T(1024)S(1)}, s32[1024]{0:T(1024)}, u32[]{:S(2)}) copy-start(s32[1024]{0:T(1024)} %param.16) | copy-start | bytes 12292
  167.5 16.6 %copy-start.4 = (f32[100]{0:T(128)S(1)}, f32[100]{0:T(128)}, u32[]{:S(2)}) copy-start(f32[100]{0:T(128)} %param.13) | copy-start | bytes 1204
  167.5 16.9 %copy-start.5 = (s32[100]{0:T(128)S(1)}, s32[100]{0:T(128)}, u32[]{:S(2)}) copy-start(s32[100]{0:T(128)} %param.15) | copy-start | bytes 1204
  178.1 21.4 %all-to-all-start.4 = ((f32[32,32,256]{2,1,0:T(8,128)}), f32[32,32,256]{2,1,0:T(8,128)S(1)}, u32[]{:S(2)}, u32[]{:S(2)}) async-start(f32[32,32,256]{2,1,0:T(8,128)} %bitcast.21), calls=%async_computation.4 | async-start | bytes 2097152 | tf_op jit(solution)/shard_map/all_to_all | solution.py:53
  201.0 14.2 %all-to-all-start.6 = ((f32[32,1,1024]{2,1,0:T(1,128)}), f32[32,1,1024]{2,1,0:T(1,128)S(1)}, u32[]{:S(2)}, u32[]{:S(2)}) async-start(f32[32,1,1024]{2,1,0:T(1,128)} %reshape.113), calls=%async_computation.6 | async-start | bytes 262144 | tf_op jit(solution)/shard_map/all_to_all | solution.py:56
  217.1 5.0 %collective-permute-start.1 = (f32[32,1024]{1,0:T(8,128)S(1)}, f32[32,1024]{1,0:T(8,128)S(1)}, u32[]{:S(2)}, u32[]{:S(2)}) collective-permute-start(f32[32,1024]{1,0:T(8,128)S(1)} %bitcast_select_fusion.1), channel_id=1, source_target_pairs={{64,0},{96,32},{0,64},{32,96},{65,1},{97,33},{1,65},{33,97},{66,2}... | collective-permute-start | bytes 393224 | tf_op jit(solution)/shard_map/ppermute | solution.py:10

commit v4 on v2

--- a/solution.py
+++ b/solution.py
@@ -1,13 +1,92 @@
+import functools
+
 import jax
 import jax.numpy as jnp
 from jax import lax
 from jax.sharding import PartitionSpec as P
+from jax.experimental import pallas as pl
+from jax.experimental.pallas import tpu as pltpu
 
 
 def passed_along(block, axis, distance):
     devices = range(lax.axis_size(axis))
     route = [((i - distance) % len(devices), i) for i in devices]
     return lax.ppermute(block, axis, route)
+
+
+def _scatter_kernel(n, c_ref, out_ref, send_sems, recv_sems, local_sem):
+    me = lax.axis_index("vir")
+    group = lax.axis_index("occ")
+    rows = out_ref.shape[1]
+
+    barrier = pltpu.get_barrier_semaphore()
+
+    def greet(k, carry):
+        peer = lax.rem(me + k, n)
+        pl.semaphore_signal(barrier, inc=1, device_id=(group, peer), device_id_type=pl.DeviceIdType.MESH)
+        return carry
+
+    lax.fori_loop(1, n, greet, 0)
+    pl.semaphore_wait(barrier, n - 1)
+
+    own = pltpu.make_async_copy(c_ref.at[pl.ds(me * rows, rows)], out_ref.at[me], local_sem)
+    own.start()
+
+    def send(k, carry):
+        peer = lax.rem(me + k, n)
+        pltpu.make_async_remote_copy(
+            src_ref=c_ref.at[pl.ds(peer * rows, rows)],
+            dst_ref=out_ref.at[me],
+            send_sem=send_sems.at[peer],
+            recv_sem=recv_sems.at[me],
+            device_id=(group, peer),
+            device_id_type=pl.DeviceIdType.MESH,
+        ).start()
+        return carry
+
+    lax.fori_loop(1, n, send, 0)
+
+    def finish(k, carry):
+        peer = lax.rem(me + k, n)
+        source = lax.rem(me + n - k, n)
+        pltpu.make_async_remote_copy(
+            src_ref=c_ref.at[pl.ds(peer * rows, rows)],
+            dst_ref=out_ref.at[me],
+            send_sem=send_sems.at[peer],
+            recv_sem=recv_sems.at[me],
+            device_id=(group, peer),
+            device_id_type=pl.DeviceIdType.MESH,
+        ).wait_send()
+        pltpu.make_async_remote_copy(
+            src_ref=c_ref.at[pl.ds(me * rows, rows)],
+            dst_ref=out_ref.at[source],
+            send_sem=send_sems.at[source],
+            recv_sem=recv_sems.at[source],
+            device_id=(group, source),
+            device_id_type=pl.DeviceIdType.MESH,
+        ).wait_recv()
+        return carry
+
+    lax.fori_loop(1, n, finish, 0)
+    own.wait()
+
+
+def reduce_rows(c, occ_axis, vir_axis):
+    n = lax.axis_size(vir_axis)
+    rows = c.shape[0] // n
+    arrived = pl.pallas_call(
+        functools.partial(_scatter_kernel, n),
+        out_shape=jax.ShapeDtypeStruct((n, rows, c.shape[1]), c.dtype),
+        in_specs=[pl.BlockSpec(memory_space=pl.ANY)],
+        out_specs=pl.BlockSpec(memory_space=pl.ANY),
+        scratch_shapes=[
+            pltpu.SemaphoreType.DMA((n,)),
+            pltpu.SemaphoreType.DMA((n,)),
+            pltpu.SemaphoreType.DMA,
+        ],
+        compiler_params=pltpu.CompilerParams(collective_id=0, has_side_effects=True),
+    )(c)
+    return jnp.sum(arrived, axis=0)
 
 
 def per_device(amplitudes, factors, occ_energy, vir_energy, occ_irrep, vir_irrep, pair_orbitals):
@@ -37,9 +116,7 @@
     direct = jnp.einsum("qac,qbc->ab", factors, halves[:, 0], preferred_element_type=jnp.float32)
     turned_term = jnp.einsum("qac,qbc->ab", halves[:, 1], factors, preferred_element_type=jnp.float32)
     combined = direct + turned_term
-    blocks = combined.reshape(vir_devices, row_count, combined.shape[-1])
-    arrived = lax.all_to_all(blocks, "vir", split_axis=0, concat_axis=0, tiled=True)
-    own_rows = jnp.sum(arrived, axis=0)
+    own_rows = reduce_rows(combined, "occ", "vir")
     cols = lax.all_to_all(own_rows, "vir", split_axis=1, concat_axis=0, tiled=True)
     own_cols = jnp.transpose(cols, (1, 0))
     outgoing_block = jnp.where(lower_half, own_cols, own_rows)

time: 219 us -> 225 us (1.027)
  Pallas kernels: 0 us -> 66.4 us
  waiting for transfers between devices: 128 us -> 73.5 us
  starting transfers between devices: 26.3 us -> 20.8 us
    pallas_call x0 -> x1, Pallas kernels: none -> 66.4 us  [reduce_rows(): pl.pallas_call(functools.partial(_scatter_kernel, n), out_shape=jax.Shape...]
    all_to_all x1 -> x0, waiting for transfers between devices: 54.2 us -> none  [per_device(): lax.all_to_all(blocks, 'vir', split_axis=0, concat_axis=0, tiled=True)]
    all_to_all x1 -> x0, starting transfers between devices: 5.18 us -> none  [per_device(): lax.all_to_all(blocks, 'vir', split_axis=0, concat_axis=0, tiled=True)]
    ppermute x2, starting transfers between devices: 6.29 us -> 3.03 us  [passed_along(): return lax.ppermute(block, axis, route)]
    all_to_all x1, starting transfers between devices: 3.86 us -> 6.79 us  [per_device(): lax.all_to_all(own_rows, 'vir', split_axis=1, concat_axis=0, tiled=True)]
  transfers between devices with their start and end apart: 5 -> 4, of which waited for: 5 -> 4; matrix products, arithmetic and copies ran while one was open for 0% -> 0% of each run, Pallas kernels for 0% -> 0%
where the time goes in v4:
time: 225 us
  waiting for transfers between devices  73.5 us (33%)
  Pallas kernels  66.4 us (30%)
  matrix products  47.2 us (21%)
  starting transfers between devices  20.8 us (9%)
  local copies, waits for them, and re-layouts  9.93 us (4%)
  other arithmetic  6.65 us (3%)
    pallas_call x1, Pallas kernels, reduce_rows(): pl.pallas_call(functools.partial(_scatter_kernel, n), out_shape=jax.Shape...  66.4 us
    all_to_all x1, waiting for transfers between devices, per_device(): lax.all_to_all(spread, 'vir', split_axis=0, concat_axis=0, tiled=True)  57.1 us
    dot_general x3, matrix products, half_product(): jnp.einsum('pcd,bd->pbc', gathered, factor, preferred_element_type=jnp.fl...  28.2 us
    all_to_all x1, starting transfers between devices, per_device(): lax.all_to_all(spread, 'vir', split_axis=0, concat_axis=0, tiled=True)  11 us
    dot_general x1, matrix products, per_device(): jnp.einsum('qac,qbc->ab', halves[:, 1], factors, preferred_element_type=j...  10.8 us
    all_to_all x1, waiting for transfers between devices, per_device(): lax.all_to_all(own_rows, 'vir', split_axis=1, concat_axis=0, tiled=True)  10.1 us
    dot_general x1, matrix products, per_device(): jnp.einsum('qac,qbc->ab', factors, halves[:, 0], preferred_element_type=j...  8.27 us
    all_to_all x1, starting transfers between devices, per_device(): lax.all_to_all(own_rows, 'vir', split_axis=1, concat_axis=0, tiled=True)  6.79 us
  transfers between devices with their start and end apart: 4, of which 4 were waited for; matrix products, arithmetic and copies ran while one was open for 0% of the time, Pallas kernels for 0%

profile of v4, /device:TPU:0, one launch (start us, length us, event | category | flops | bytes accessed | tf_op | source)
XLA Modules:
  0.0 224.7 jit_solution(4683423399716895390)
XLA Ops:
  0.0 0.9 bitcast_select_fusion.3
  0.9 1.7 collective-permute-start
  2.6 2.6 %collective-permute-done = bf16[32,1024]{1,0:T(8,128)(2,1)S(1)} collective-permute-done((bf16[32,1024]{1,0:T(8,128)(2,1)S(1)}, bf16[32,1024]{1,0:T(8,128)(2,1)S(1)}, u32[]{:S(2)}, u32[]{:S(2)}) %collective-permute-start) | collective-permute-done | bytes 65568 | tf_op jit(solution)/shard_map/ppermute | solution.py:14
  5.2 0.9 fusion.14
  6.2 2.5 %broadcast_in_dim.64 = bf16[32,2,32,1024]{3,2,1,0:T(8,128)(2,1)} broadcast(bf16[2,32,1024]{2,1,0:T(8,128)(2,1)S(1)} %pad_maximum_fusion), dimensions={1,2,3} | broadcast | bytes 4325376 | tf_op jit(solution)/shard_map/broadcast_in_dim | solution.py:107
  8.7 11.0 %all-to-all-start = ((bf16[32,2,32,1024]{3,2,1,0:T(8,128)(2,1)}), bf16[32,2,32,1024]{3,2,1,0:T(8,128)(2,1)}, u32[]{:S(2)}, u32[]{:S(2)}) async-start(bf16[32,2,32,1024]{3,2,1,0:T(8,128)(2,1)} %broadcast_in_dim.64), calls=%async_computation | async-start | bytes 8388608 | tf_op jit(solution)/shard_map/all_to_all | solution.py:108
  20.4 57.1 %all-to-all-done = bf16[32,2,32,1024]{3,2,1,0:T(8,128)(2,1)} async-done(((bf16[32,2,32,1024]{3,2,1,0:T(8,128)(2,1)}), bf16[32,2,32,1024]{3,2,1,0:T(8,128)(2,1)}, u32[]{:S(2)}, u32[]{:S(2)}) %all-to-all-start) | async-done | bytes 4194336 | tf_op jit(solution)/shard_map/all_to_all | solution.py:108
  77.5 4.9 %copy.22 = bf16[32,2,32,1024]{3,2,0,1:T(8,128)(2,1)} copy(bf16[32,2,32,1024]{3,2,1,0:T(8,128)(2,1)} %all-to-all-done) | data formatting | bytes 8388608 | tf_op jit(solution)/shard_map/all_to_all | solution.py:108
  82.5 28.2 %while.10 = (s32[]{:T(128)}, bf16[3,2,1024,1024]{3,2,0,1:T(8,128)(2,1)}, bf16[3,1024,1024]{2,1,0:T(8,128)(2,1)}, bf16[2,1024,1024]{2,1,0:T(8,128)(2,1)}, s32[]{:T(128)}) while((s32[]{:T(128)}, bf16[3,2,1024,1024]{3,2,0,1:T(8,128)(2,1)}, bf16[3,1024,1024]{2,1,0:T(8,128)(2,1)}, bf16[2,1024,1024]{2,1,0:T(8,128)(2,1)}, s32[]{:T(128)}) %tuple.26), condition=%wide.region_3.4_spmd, body=%wide.region_2.3_spmd.sunk | while | flops 4297064448 | bytes 10486845 | solution.py:115
  82.5 9.4 %bitcast_dynamic-update-slice_fusion.2 = bf16[3,2,1024,1024]{3,2,0,1:T(8,128)(2,1)} fusion(bf16[3,2,1024,1024]{3,2,0,1:T(8,128)(2,1)} %get-tuple-element.77, s32[]{:T(128)} %get-tuple-element.76, bf16[2,1024,1024]{2,1,0:T(8,128)(2,1)} %get-tuple-element.84, bf16[3,1024,1024]{2,1,0:T(8,128)(2,1)} %get-tuple-element.83), kind=kOutput, calls=%fused_computation.clone.1 | convolution fusion | flops 4297064448 | bytes 10486784 | tf_op jit(solution)/shard_map/while/body/eval_jaxpr/pcd,bd->pbc/dot_general | solution.py:112
  91.8 9.5 %bitcast_dynamic-update-slice_fusion.2 = bf16[3,2,1024,1024]{3,2,0,1:T(8,128)(2,1)} fusion(bf16[3,2,1024,1024]{3,2,0,1:T(8,128)(2,1)} %get-tuple-element.77, s32[]{:T(128)} %get-tuple-element.76, bf16[2,1024,1024]{2,1,0:T(8,128)(2,1)} %get-tuple-element.84, bf16[3,1024,1024]{2,1,0:T(8,128)(2,1)} %get-tuple-element.83), kind=kOutput, calls=%fused_computation.clone.1 | convolution fusion | flops 4297064448 | bytes 10486784 | tf_op jit(solution)/shard_map/while/body/eval_jaxpr/pcd,bd->pbc/dot_general | solution.py:112
  101.3 9.4 %bitcast_dynamic-update-slice_fusion.2 = bf16[3,2,1024,1024]{3,2,0,1:T(8,128)(2,1)} fusion(bf16[3,2,1024,1024]{3,2,0,1:T(8,128)(2,1)} %get-tuple-element.77, s32[]{:T(128)} %get-tuple-element.76, bf16[2,1024,1024]{2,1,0:T(8,128)(2,1)} %get-tuple-element.84, bf16[3,1024,1024]{2,1,0:T(8,128)(2,1)} %get-tuple-element.83), kind=kOutput, calls=%fused_computation.clone.1 | convolution fusion | flops 4297064448 | bytes 10486784 | tf_op jit(solution)/shard_map/while/body/eval_jaxpr/pcd,bd->pbc/dot_general | solution.py:112
  110.6 10.8 %fusion.3 = f32[1024,1024,1]{1,0,2:T(8,128)S(1)} fusion(bf16[3,1024,1024]{2,1,0:T(8,128)(2,1)} %get-tuple-element.93, bf16[3,2,1024,1024]{3,2,0,1:T(8,128)(2,1)} %get-tuple-element.27), kind=kOutput, calls=%fused_computation.4 | convolution fusion | flops 6442450944 | bytes 16777216 | tf_op jit(solution)/shard_map/qac,qbc->ab/dot_general | solution.py:117
  121.5 8.3 %bitcast_add_fusion.c_ref = f32[1024,1024]{1,0:T(8,128)} fusion(f32[1024,1024,1]{1,0,2:T(8,128)S(1)} %fusion.3, bf16[3,1024,1024]{2,1,0:T(8,128)(2,1)S(1)} %copy-done.5, bf16[3,2,1024,1024]{3,2,0,1:T(8,128)(2,1)S(1)} %copy-done.6), kind=kOutput, calls=%fused_computation.10 | convolution fusion | flops 6443499520 | bytes 20971520 | tf_op jit(solution)/shard_map/qac,qbc->ab/dot_general | solution.py:116
  129.7 66.4 %shard_map.73 = f32[32,32,1024]{2,1,0:T(8,128)} custom-call(f32[1024,1024]{1,0:T(8,128)} %bitcast_add_fusion.c_ref), custom_call_target="tpu_custom_call" | custom-call | tf_op jit(solution)/shard_map/pallas_call | solution.py:77
  196.1 2.4 %reduce_sum.47 = f32[32,1024]{1,0:T(8,128)S(1)} reduce(f32[32,32,1024]{2,1,0:T(8,128)} %shard_map.73, f32[]{:T(128)} %constant.32.clone.1), dimensions={0}, to_apply=%region_4.5 | reduce | flops 1015808 | bytes 4325380 | tf_op jit(solution)/shard_map/reduce_sum | solution.py:89
  199.1 0.9 reshape.87
  200.0 6.8 %all-to-all-start.1 = ((f32[32,1,1024]{2,1,0:T(1,128)}), f32[32,1,1024]{2,1,0:T(1,128)S(1)}, u32[]{:S(2)}, u32[]{:S(2)}) async-start(f32[32,1,1024]{2,1,0:T(1,128)} %reshape.87), calls=%async_computation.1 | async-start | bytes 262144 | tf_op jit(solution)/shard_map/all_to_all | solution.py:120
  206.9 10.1 %all-to-all-done.1 = f32[32,1,1024]{2,1,0:T(1,128)S(1)} async-done(((f32[32,1,1024]{2,1,0:T(1,128)}), f32[32,1,1024]{2,1,0:T(1,128)S(1)}, u32[]{:S(2)}, u32[]{:S(2)}) %all-to-all-start.1) | async-done | bytes 131104 | tf_op jit(solution)/shard_map/all_to_all | solution.py:120
  217.0 0.5 broadcast.49
  217.5 1.0 reduce
  218.8 1.3 collective-permute-start.1
  220.2 3.7 %collective-permute-done.1 = f32[32,1024]{1,0:T(8,128)S(1)} collective-permute-done((f32[32,1024]{1,0:T(8,128)S(1)}, f32[32,1024]{1,0:T(8,128)S(1)}, u32[]{:S(2)}, u32[]{:S(2)}) %collective-permute-start.1) | collective-permute-done | bytes 131104 | tf_op jit(solution)/shard_map/ppermute | solution.py:14
  223.9 0.8 fusion.11
  (32 shorter events, 1.7 us)
Async XLA Ops:
  0.0 19.9 %copy-start = (s32[8,2]{0,1:T(2,128)S(1)}, s32[8,2]{0,1:T(2,128)}, u32[]{:S(2)}) copy-start(s32[8,2]{0,1:T(2,128)} %param.15) | copy-start | bytes 196
  0.9 4.3 %collective-permute-start = (bf16[32,1024]{1,0:T(8,128)(2,1)S(1)}, bf16[32,1024]{1,0:T(8,128)(2,1)S(1)}, u32[]{:S(2)}, u32[]{:S(2)}) collective-permute-start(bf16[32,1024]{1,0:T(8,128)(2,1)S(1)} %bitcast_select_fusion.3), channel_id=1, source_target_pairs={{64,0},{96,32},{0,64},{32,96},{65,1},{97,33},{1,65},{33,97},{66,2}... | collective-permute-start | bytes 196616 | tf_op jit(solution)/shard_map/ppermute | solution.py:14
  6.2 13.6 %copy-start.1 = (s32[1024]{0:T(1024)S(1)}, s32[1024]{0:T(1024)}, u32[]{:S(2)}) copy-start(s32[1024]{0:T(1024)} %param.14) | copy-start | bytes 12292
  6.2 13.6 %copy-start.2 = (f32[1024]{0:T(1024)S(1)}, f32[1024]{0:T(1024)}, u32[]{:S(2)}) copy-start(f32[1024]{0:T(1024)} %param.12) | copy-start | bytes 12292
  6.2 13.8 %copy-start.3 = (s32[100]{0:T(128)S(1)}, s32[100]{0:T(128)}, u32[]{:S(2)}) copy-start(s32[100]{0:T(128)} %param.13) | copy-start | bytes 1204
  6.2 14.0 %copy-start.4 = (f32[100]{0:T(128)S(1)}, f32[100]{0:T(128)}, u32[]{:S(2)}) copy-start(f32[100]{0:T(128)} %param.11) | copy-start | bytes 1204
  8.7 68.8 %all-to-all-start = ((bf16[32,2,32,1024]{3,2,1,0:T(8,128)(2,1)}), bf16[32,2,32,1024]{3,2,1,0:T(8,128)(2,1)}, u32[]{:S(2)}, u32[]{:S(2)}) async-start(bf16[32,2,32,1024]{3,2,1,0:T(8,128)(2,1)} %broadcast_in_dim.64), calls=%async_computation | async-start | bytes 8388608 | tf_op jit(solution)/shard_map/all_to_all | solution.py:108
  110.6 10.8 %copy-start.5 = (bf16[3,1024,1024]{2,1,0:T(8,128)(2,1)S(1)}, bf16[3,1024,1024]{2,1,0:T(8,128)(2,1)}, u32[]{:S(2)}) copy-start(bf16[3,1024,1024]{2,1,0:T(8,128)(2,1)} %get-tuple-element.93) | copy-start | bytes 18874372
  110.6 10.8 %copy-start.6 = (bf16[3,2,1024,1024]{3,2,0,1:T(8,128)(2,1)S(1)}, bf16[3,2,1024,1024]{3,2,0,1:T(8,128)(2,1)}, u32[]{:S(2)}) copy-start(bf16[3,2,1024,1024]{3,2,0,1:T(8,128)(2,1)} %get-tuple-element.27) | copy-start | bytes 37748740
  200.0 17.0 %all-to-all-start.1 = ((f32[32,1,1024]{2,1,0:T(1,128)}), f32[32,1,1024]{2,1,0:T(1,128)S(1)}, u32[]{:S(2)}, u32[]{:S(2)}) async-start(f32[32,1,1024]{2,1,0:T(1,128)} %reshape.87), calls=%async_computation.1 | async-start | bytes 262144 | tf_op jit(solution)/shard_map/all_to_all | solution.py:120
  218.8 5.0 %collective-permute-start.1 = (f32[32,1024]{1,0:T(8,128)S(1)}, f32[32,1024]{1,0:T(8,128)S(1)}, u32[]{:S(2)}, u32[]{:S(2)}) collective-permute-start(f32[32,1024]{1,0:T(8,128)S(1)} %bitcast_select_fusion.1), channel_id=1, source_target_pairs={{64,0},{96,32},{0,64},{32,96},{65,1},{97,33},{1,65},{33,97},{66,2}... | collective-permute-start | bytes 393224 | tf_op jit(solution)/shard_map/ppermute | solution.py:14

commit v5 on v1

--- a/solution.py
+++ b/solution.py
@@ -1,13 +1,161 @@
+import functools
+
 import jax
 import jax.numpy as jnp
 from jax import lax
 from jax.sharding import PartitionSpec as P
+from jax.experimental import pallas as pl
+from jax.experimental.pallas import tpu as pltpu
 
 
 def passed_along(block, axis, distance):
     devices = range(lax.axis_size(axis))
     route = [((i - distance) % len(devices), i) for i in devices]
     return lax.ppermute(block, axis, route)
+
+
+def _exchange_kernel(layout, *refs):
+    count = len(layout)
+    sources, targets = refs[:count], refs[count:2 * count]
+    send_sems, recv_sems = refs[2 * count:3 * count], refs[3 * count:4 * count]
+    local_sems = refs[4 * count]
+    me = lax.axis_index("vir")
+    group = lax.axis_index("occ")
+
+    def peer_of(mine, coord, stride):
+        return me + (coord - mine) * stride
+
+    barrier = pltpu.get_barrier_semaphore()
+    greetings = 0
+    coords = []
+    for stride, size, shared in layout:
+        mine = lax.rem(lax.div(me, stride), size)
+        coords.append(mine)
+        for step in range(1, size):
+            coord = lax.rem(mine + step, size)
+            pl.semaphore_signal(
+                barrier, inc=1, device_id=(group, peer_of(mine, coord, stride)),
+                device_id_type=pl.DeviceIdType.MESH,
+            )
+            greetings += 1
+    pl.semaphore_wait(barrier, greetings)
+
+    def remote(part, coord, slot):
+        stride, size, shared = layout[part]
+        mine = coords[part]
+        source = sources[part] if shared else sources[part].at[coord]
+        return pltpu.make_async_remote_copy(
+            src_ref=source,
+            dst_ref=targets[part].at[slot],
+            send_sem=send_sems[part].at[coord],
+            recv_sem=recv_sems[part].at[slot],
+            device_id=(group, peer_of(mine, coord, stride)),
+            device_id_type=pl.DeviceIdType.MESH,
+        )
+
+    locals_ = []
+    for part, (stride, size, shared) in enumerate(layout):
+        mine = coords[part]
+        source = sources[part] if shared else sources[part].at[mine]
+        local = pltpu.make_async_copy(source, targets[part].at[mine], local_sems.at[part])
+        local.start()
+        locals_.append(local)
+        for step in range(1, size):
+            remote(part, lax.rem(mine + step, size), mine).start()
+    for part, (stride, size, shared) in enumerate(layout):
+        mine = coords[part]
+        for step in range(1, size):
+            remote(part, lax.rem(mine + step, size), mine).wait_send()
+            origin = lax.rem(mine + size - step, size)
+            stride_ = stride
+            pltpu.make_async_remote_copy(
+                src_ref=sources[part] if shared else sources[part].at[origin],
+                dst_ref=targets[part].at[origin],
+                send_sem=send_sems[part].at[origin],
+                recv_sem=recv_sems[part].at[origin],
+                device_id=(group, peer_of(mine, origin, stride_)),
+                device_id_type=pl.DeviceIdType.MESH,
+            ).wait_recv()
+        locals_[part].wait()
+
+
+def exchange(parts, collective_id):
+    layout = tuple((stride, size, shared) for _, stride, size, shared in parts)
+    shapes = []
+    for array, stride, size, shared in parts:
+        block = array.shape if shared else array.shape[1:]
+        shapes.append(jax.ShapeDtypeStruct((size,) + tuple(block), array.dtype))
+    scratch = [pltpu.SemaphoreType.DMA((size,)) for _, _, size, _ in parts]
+    scratch += [pltpu.SemaphoreType.DMA((size,)) for _, _, size, _ in parts]
+    scratch.append(pltpu.SemaphoreType.DMA((len(parts),)))
+    return pl.pallas_call(
+        functools.partial(_exchange_kernel, layout),
+        out_shape=tuple(shapes),
+        in_specs=[pl.BlockSpec(memory_space=pl.ANY)] * len(parts),
+        out_specs=tuple(pl.BlockSpec(memory_space=pl.ANY) for _ in parts),
+        scratch_shapes=scratch,
+        compiler_params=pltpu.CompilerParams(collective_id=collective_id, has_side_effects=True),
+    )(*[array for array, _, _, _ in parts])
+
+
+def _axis_sizes(n):
+    y_size = 2
+    x_size = 4
+    z_size = n // (x_size * y_size)
+    return z_size, x_size, y_size
+
+
+def _column_cuts(width):
+    lanes = width // 128
+    first = (lanes + 2) // 3
+    second = (lanes - first + 1) // 2
+    return [0, first * 128, (first + second) * 128, width]
+
+
+def reduce_rows(c, occ_axis, vir_axis):
+    n = lax.axis_size(vir_axis)
+    z_size, x_size, y_size = _axis_sizes(n)
+    rows = c.shape[0] // n
+    cuts = _column_cuts(c.shape[1])
+    grid = c.reshape(z_size, x_size, y_size, rows, c.shape[1])
+    axes = {"z": (x_size * y_size, z_size), "x": (y_size, x_size), "y": (1, y_size)}
+    orders = [("z", "x", "y"), ("x", "y", "z"), ("y", "z", "x")]
+    current = []
+    for part, order in enumerate(orders):
+        piece = grid[..., cuts[part]:cuts[part + 1]]
+        perm = ["zxy".index(name) for name in order]
+        current.append(jnp.transpose(piece, perm + [3, 4]))
+    for stage in range(3):
+        parts = []
+        for part, order in enumerate(orders):
+            stride, size = axes[order[stage]]
+            parts.append((current[part], stride, size, False))
+        arrived = exchange(parts, stage)
+        current = [jnp.sum(block, axis=0) for block in arrived]
+    return jnp.concatenate(current, axis=-1)
+
+
+def gather_rows(block, occ_axis, vir_axis):
+    n = lax.axis_size(vir_axis)
+    z_size, x_size, y_size = _axis_sizes(n)
+    cuts = _column_cuts(block.shape[-1])
+    axes = {"z": (x_size * y_size, z_size), "x": (y_size, x_size), "y": (1, y_size)}
+    orders = [("y", "x", "z"), ("z", "y", "x"), ("x", "z", "y")]
+    current = [block[..., cuts[part]:cuts[part + 1]] for part in range(3)]
+    for stage in range(3):
+        parts = []
+        for part, order in enumerate(orders):
+            stride, size = axes[order[stage]]
+            parts.append((current[part], stride, size, True))
+        current = list(exchange(parts, 3 + stage))
+    pieces = []
+    for part, order in enumerate(orders):
+        held = [order[2], order[1], order[0]]
+        perm = [held.index(name) for name in "zxy"]
+        arranged = jnp.transpose(current[part], [3] + perm + [4, 5])
+        pairs, rows, cols = block.shape[0], block.shape[1], arranged.shape[-1]
+        pieces.append(arranged.reshape(pairs, n * rows, cols))
+    return jnp.concatenate(pieces, axis=-1)
 
 
 def per_device(amplitudes, factors, occ_energy, vir_energy, occ_irrep, vir_irrep, pair_orbitals):
@@ -25,7 +173,7 @@
     first = jnp.where(lower_half, amplitudes[0], incoming)
     second = jnp.where(lower_half, incoming, amplitudes[1])
     couple = jnp.stack([first, second], axis=0)
-    gathered = lax.all_gather(couple, "vir", axis=1, tiled=True)
+    gathered = gather_rows(couple, "occ", "vir")
 
     def half_product(factor):
         product = jnp.einsum("pcd,bd->pbc", gathered, factor, preferred_element_type=jnp.float32)
@@ -35,7 +183,7 @@
     direct = jnp.einsum("qac,qbc->ab", factors, halves[:, 0], preferred_element_type=jnp.float32)
     turned_term = jnp.einsum("qac,qbc->ab", halves[:, 1], factors, preferred_element_type=jnp.float32)
     combined = direct + turned_term
-    own_rows = lax.psum_scatter(combined, "vir", scatter_dimension=0, tiled=True)
+    own_rows = reduce_rows(combined, "occ", "vir")
     cols = lax.all_to_all(own_rows, "vir", split_axis=1, concat_axis=0, tiled=True)
     own_cols = jnp.transpose(cols, (1, 0))
     outgoing_block = jnp.where(lower_half, own_cols, own_rows)

time: 381 us -> 238 us (0.62)
  waiting for transfers between devices: 289 us -> 14.7 us
  Pallas kernels: 0 us -> 136 us
  other arithmetic: 5.14 us -> 22.4 us
  between operations: 13.5 us -> 0.25 us
  local copies, waits for them, and re-layouts: 15.1 us -> 9.89 us
  matrix products: 50.1 us -> 45.9 us
    reduce_scatter x1 -> x0, waiting for transfers between devices: 190 us -> none  [per_device(): lax.psum_scatter(combined, 'vir', scatter_dimension=0, tiled=True)]
    pallas_call x0 -> x6, Pallas kernels: none -> 136 us  [exchange(): pl.pallas_call(functools.partial(_exchange_kernel, layout), out_shape=tup...]
    all_gather x1 -> x0, waiting for transfers between devices: 82.9 us -> none  [per_device(): gathered = lax.all_gather(couple, 'vir', axis=1, tiled=True)]
    reduce_sum x0 -> x9, other arithmetic: none -> 13.3 us  [reduce_rows(): current = [jnp.sum(block, axis=0) for block in arrived]]
    while x1 -> x0, local copies, waits for them, and re-layouts: 5.44 us -> none  [per_device(): halves = lax.map(half_product, factors)]
    unnamed x18 -> x19, local copies, waits for them, and re-layouts: 7.57 us -> 2.4 us
  transfers between devices with their start and end apart: 5 -> 3, of which waited for: 5 -> 2; matrix products, arithmetic and copies ran while one was open for 0% -> 1% of each run, Pallas kernels for 0% -> 0%
where the time goes in v5:
time: 238 us
  Pallas kernels  136 us (57%)
  matrix products  45.9 us (19%)
  other arithmetic  22.4 us (9%)
  waiting for transfers between devices  14.7 us (6%)
  local copies, waits for them, and re-layouts  9.89 us (4%)
  starting transfers between devices  8.22 us (3%)
    pallas_call x6, Pallas kernels, exchange(): pl.pallas_call(functools.partial(_exchange_kernel, layout), out_shape=tup...  136 us
    dot_general x3, matrix products, half_product(): jnp.einsum('pcd,bd->pbc', gathered, factor, preferred_element_type=jnp.fl...  28.2 us
    reduce_sum x9, other arithmetic, reduce_rows(): current = [jnp.sum(block, axis=0) for block in arrived]  13.3 us
    dot_general x1, matrix products, per_device(): jnp.einsum('qac,qbc->ab', halves[:, 1], factors, preferred_element_type=j...  11 us
    all_to_all x1, waiting for transfers between devices, per_device(): lax.all_to_all(own_rows, 'vir', split_axis=1, concat_axis=0, tiled=True)  10.1 us
    dot_general x1, matrix products, per_device(): jnp.einsum('qac,qbc->ab', factors, halves[:, 0], preferred_element_type=j...  6.73 us
    all_to_all x1, starting transfers between devices, per_device(): lax.all_to_all(own_rows, 'vir', split_axis=1, concat_axis=0, tiled=True)  6.12 us
  transfers between devices with their start and end apart: 3, of which 2 were waited for; matrix products, arithmetic and copies ran while one was open for 1% of the time, Pallas kernels for 0%

profile of v5, /device:TPU:0, one launch (start us, length us, event | category | flops | bytes accessed | tf_op | source)
XLA Modules:
  0.0 237.7 jit_solution(3469320505787002791)
XLA Ops:
  0.9 1.7 collective-permute-start
  8.2 10.2 %shard_map.73 = (bf16[2,2,32,384]{3,2,1,0:T(8,128)(2,1)}, bf16[4,2,32,384]{3,2,1,0:T(8,128)(2,1)}, bf16[4,2,32,256]{3,2,1,0:T(8,128)(2,1)}) custom-call(bf16[2,32,384]{2,1,0:T(8,128)(2,1)} %get-tuple-element.83.refs_0_, bf16[2,32,384]{2,1,0:T(8,128)(2,1)} %get-tuple-element.82.refs_1_, bf16[2,32,256]{2,1,0:T(8,128)(2,1)} %pad_maximum_fusion.2.refs_2_), custom_call_target="tpu_custom_call" | custom-call | tf_op jit(solution)/shard_map/pallas_call | solution.py:91
  18.4 17.2 %shard_map.74 = (bf16[4,2,2,32,384]{4,3,2,1,0:T(8,128)(2,1)}, bf16[2,4,2,32,384]{4,3,2,1,0:T(8,128)(2,1)}, bf16[4,4,2,32,256]{4,3,2,1,0:T(8,128)(2,1)}) custom-call(bf16[2,2,32,384]{3,2,1,0:T(8,128)(2,1)} %get-tuple-element.45.refs_0_, bf16[4,2,32,384]{3,2,1,0:T(8,128)(2,1)} %get-tuple-element.46.refs_1_, bf16[4,2,32,256]{3,2,1,0:T(8,128)(2,1)} %get-tuple-element.47.refs_2_), custom_call_target="tpu_custom_call" | custom-call | tf_op jit(solution)/shard_map/pallas_call | solution.py:91
  35.6 43.3 %shard_map.75 = (bf16[4,4,2,2,32,384]{5,4,3,2,1,0:T(8,128)(2,1)}, bf16[4,2,4,2,32,384]{5,4,3,2,1,0:T(8,128)(2,1)}, bf16[2,4,4,2,32,256]{5,4,3,2,1,0:T(8,128)(2,1)}) custom-call(bf16[4,2,2,32,384]{4,3,2,1,0:T(8,128)(2,1)} %get-tuple-element.48.refs_0_, bf16[2,4,2,32,384]{4,3,2,1,0:T(8,128)(2,1)} %get-tuple-element.49.refs_1_, ...), custom_call_target="tpu_custom_call" | custom-call | tf_op jit(solution)/shard_map/pallas_call | solution.py:91
  79.0 1.9 copy.30
  81.2 2.3 pad_maximum_fusion
  83.5 28.2 %while.10 = (s32[]{:T(128)}, bf16[3,2,1024,1024]{3,2,0,1:T(8,128)(2,1)}, bf16[3,1024,1024]{2,1,0:T(8,128)(2,1)}, bf16[2,1024,1024]{2,1,0:T(8,128)(2,1)}, s32[]{:T(128)}) while((s32[]{:T(128)}, bf16[3,2,1024,1024]{3,2,0,1:T(8,128)(2,1)}, bf16[3,1024,1024]{2,1,0:T(8,128)(2,1)}, bf16[2,1024,1024]{2,1,0:T(8,128)(2,1)}, s32[]{:T(128)}) %tuple.25), condition=%wide.region_3.4_spmd, body=%wide.region_2.3_spmd.sunk | while | flops 4297064448 | bytes 10486845 | solution.py:182
  83.5 9.4 %bitcast_dynamic-update-slice_fusion.2 = bf16[3,2,1024,1024]{3,2,0,1:T(8,128)(2,1)} fusion(bf16[3,2,1024,1024]{3,2,0,1:T(8,128)(2,1)} %get-tuple-element.117, s32[]{:T(128)} %get-tuple-element.116, bf16[2,1024,1024]{2,1,0:T(8,128)(2,1)} %get-tuple-element.124, bf16[3,1024,1024]{2,1,0:T(8,128)(2,1)} %get-tuple-element.123), kind=kOutput, calls=%fused_computation.clone.1 | convolution fusion | flops 4297064448 | bytes 10486784 | tf_op jit(solution)/shard_map/while/body/eval_jaxpr/pcd,bd->pbc/dot_general | solution.py:179
  92.9 9.5 %bitcast_dynamic-update-slice_fusion.2 = bf16[3,2,1024,1024]{3,2,0,1:T(8,128)(2,1)} fusion(bf16[3,2,1024,1024]{3,2,0,1:T(8,128)(2,1)} %get-tuple-element.117, s32[]{:T(128)} %get-tuple-element.116, bf16[2,1024,1024]{2,1,0:T(8,128)(2,1)} %get-tuple-element.124, bf16[3,1024,1024]{2,1,0:T(8,128)(2,1)} %get-tuple-element.123), kind=kOutput, calls=%fused_computation.clone.1 | convolution fusion | flops 4297064448 | bytes 10486784 | tf_op jit(solution)/shard_map/while/body/eval_jaxpr/pcd,bd->pbc/dot_general | solution.py:179
  102.3 9.4 %bitcast_dynamic-update-slice_fusion.2 = bf16[3,2,1024,1024]{3,2,0,1:T(8,128)(2,1)} fusion(bf16[3,2,1024,1024]{3,2,0,1:T(8,128)(2,1)} %get-tuple-element.117, s32[]{:T(128)} %get-tuple-element.116, bf16[2,1024,1024]{2,1,0:T(8,128)(2,1)} %get-tuple-element.124, bf16[3,1024,1024]{2,1,0:T(8,128)(2,1)} %get-tuple-element.123), kind=kOutput, calls=%fused_computation.clone.1 | convolution fusion | flops 4297064448 | bytes 10486784 | tf_op jit(solution)/shard_map/while/body/eval_jaxpr/pcd,bd->pbc/dot_general | solution.py:179
  111.7 11.0 %fusion.3 = f32[1024,1024,1]{1,0,2:T(8,128)S(1)} fusion(bf16[3,1024,1024]{2,1,0:T(8,128)(2,1)} %get-tuple-element.131, bf16[3,2,1024,1024]{3,2,0,1:T(8,128)(2,1)} %get-tuple-element.54), kind=kOutput, calls=%fused_computation.4 | convolution fusion | flops 6442450944 | bytes 16777216 | tf_op jit(solution)/shard_map/qac,qbc->ab/dot_general | solution.py:184
  122.7 6.7 %bitcast_add_fusion = f32[1024,1024]{1,0:T(8,128)S(1)} fusion(f32[1024,1024,1]{1,0,2:T(8,128)S(1)} %fusion.3, bf16[3,1024,1024]{2,1,0:T(8,128)(2,1)S(1)} %copy-done.6, bf16[3,2,1024,1024]{3,2,0,1:T(8,128)(2,1)S(1)} %copy-done.7), kind=kOutput, calls=%fused_computation.11 | convolution fusion | flops 6443499520 | bytes 20971520 | tf_op jit(solution)/shard_map/qac,qbc->ab/dot_general | solution.py:183
  129.5 1.4 fusion.17
  133.3 42.5 %shard_map.76 = (f32[4,4,2,32,384]{4,3,2,1,0:T(8,128)}, f32[4,2,4,32,384]{4,3,2,1,0:T(8,128)}, f32[2,4,4,32,256]{4,3,2,1,0:T(8,128)}) custom-call(f32[4,4,2,32,384]{4,3,2,1,0:T(8,128)} %get-tuple-element.77.refs_0_, f32[4,2,4,32,384]{4,3,2,1,0:T(8,128)} %bitcast.81, f32[2,4,4,32,256]{4,3,2,1,0:T(8,128)} %copy_bitcast_fusion.1.refs_2_), custom_call_target="tpu_custom_call" | custom-call | tf_op jit(solution)/shard_map/pallas_call | solution.py:91
  175.8 2.3 reduce_sum.121.refs_2_
  178.0 2.3 reduce_sum.119.refs_0_
  181.2 16.3 %shard_map.77 = (f32[4,2,32,384]{3,2,1,0:T(8,128)}, f32[2,4,32,384]{3,2,1,0:T(8,128)}, f32[4,4,32,256]{3,2,1,0:T(8,128)}) custom-call(f32[4,2,32,384]{3,2,1,0:T(8,128)} %reduce_sum.119.refs_0_, f32[2,4,32,384]{3,2,1,0:T(8,128)} %reduce_sum.120.refs_1_, f32[4,4,32,256]{3,2,1,0:T(8,128)} %reduce_sum.121.refs_2_), custom_call_target="tpu_custom_call" | custom-call | tf_op jit(solution)/shard_map/pallas_call | solution.py:91
  197.5 1.7 reduce_sum.123.refs_1_
  199.2 1.7 reduce_sum.124.refs_2_
  201.0 1.7 reduce_sum.122.refs_0_
  202.6 6.8 %shard_map.78 = (f32[2,32,384]{2,1,0:T(8,128)}, f32[4,32,384]{2,1,0:T(8,128)}, f32[4,32,256]{2,1,0:T(8,128)}) custom-call(f32[2,32,384]{2,1,0:T(8,128)} %reduce_sum.122.refs_0_, f32[4,32,384]{2,1,0:T(8,128)} %reduce_sum.123.refs_1_, f32[4,32,256]{2,1,0:T(8,128)} %reduce_sum.124.refs_2_), custom_call_target="tpu_custom_call" | custom-call | tf_op jit(solution)/shard_map/pallas_call | solution.py:91
  213.6 6.1 %all-to-all-start = ((f32[32,1,1024]{2,1,0:T(1,128)}), f32[32,1,1024]{2,1,0:T(1,128)S(1)}, u32[]{:S(2)}, u32[]{:S(2)}) async-start(f32[32,1,1024]{2,1,0:T(1,128)} %reshape.98), calls=%async_computation | async-start | bytes 262144 | tf_op jit(solution)/shard_map/all_to_all | solution.py:187
  219.8 10.1 %all-to-all-done = f32[32,1,1024]{2,1,0:T(1,128)S(1)} async-done(((f32[32,1,1024]{2,1,0:T(1,128)}), f32[32,1,1024]{2,1,0:T(1,128)S(1)}, u32[]{:S(2)}, u32[]{:S(2)}) %all-to-all-start) | async-done | bytes 131104 | tf_op jit(solution)/shard_map/all_to_all | solution.py:187
  232.2 4.6 %collective-permute-done.1 = f32[32,1024]{1,0:T(8,128)S(1)} collective-permute-done((f32[32,1024]{1,0:T(8,128)S(1)}, f32[32,1024]{1,0:T(8,128)S(1)}, u32[]{:S(2)}, u32[]{:S(2)}) %collective-permute-start.1) | collective-permute-done | bytes 131104 | tf_op jit(solution)/shard_map/ppermute | solution.py:14
  (52 shorter events, 17.4 us)
Async XLA Ops:
  0.0 2.6 %copy-start = (s32[8,2]{0,1:T(2,128)S(1)}, s32[8,2]{0,1:T(2,128)}, u32[]{:S(2)}) copy-start(s32[8,2]{0,1:T(2,128)} %param.15) | copy-start | bytes 196
  0.9 5.1 %collective-permute-start = (bf16[32,1024]{1,0:T(8,128)(2,1)S(1)}, bf16[32,1024]{1,0:T(8,128)(2,1)S(1)}, u32[]{:S(2)}, u32[]{:S(2)}) collective-permute-start(bf16[32,1024]{1,0:T(8,128)(2,1)S(1)} %bitcast_select_fusion.3), channel_id=1, source_target_pairs={{64,0},{96,32},{0,64},{32,96},{65,1},{97,33},{1,65},{33,97},{66,2}... | collective-permute-start | bytes 196616 | tf_op jit(solution)/shard_map/ppermute | solution.py:14
  79.0 1.9 copy-start.1
  79.0 2.2 copy-start.3
  111.7 11.0 %copy-start.6 = (bf16[3,1024,1024]{2,1,0:T(8,128)(2,1)S(1)}, bf16[3,1024,1024]{2,1,0:T(8,128)(2,1)}, u32[]{:S(2)}) copy-start(bf16[3,1024,1024]{2,1,0:T(8,128)(2,1)} %get-tuple-element.131) | copy-start | bytes 18874372
  111.7 11.0 %copy-start.7 = (bf16[3,2,1024,1024]{3,2,0,1:T(8,128)(2,1)S(1)}, bf16[3,2,1024,1024]{3,2,0,1:T(8,128)(2,1)}, u32[]{:S(2)}) copy-start(bf16[3,2,1024,1024]{3,2,0,1:T(8,128)(2,1)} %get-tuple-element.54) | copy-start | bytes 37748740
  175.8 4.6 %copy-start.2 = (f32[4,2,4,32,384]{4,3,2,1,0:T(8,128)S(1)}, f32[4,2,4,32,384]{4,3,2,1,0:T(8,128)}, u32[]{:S(2)}) copy-start(f32[4,2,4,32,384]{4,3,2,1,0:T(8,128)} %get-tuple-element.56) | copy-start | bytes 4718596
  180.3 39.4 %copy-start.5 = (f32[1024]{0:T(1024)S(1)}, f32[1024]{0:T(1024)}, u32[]{:S(2)}) copy-start(f32[1024]{0:T(1024)} %param.12) | copy-start | bytes 12292
  197.5 39.4 %copy-start.4 = (s32[1024]{0:T(1024)S(1)}, s32[1024]{0:T(1024)}, u32[]{:S(2)}) copy-start(s32[1024]{0:T(1024)} %param.14) | copy-start | bytes 12292
  213.6 16.3 %all-to-all-start = ((f32[32,1,1024]{2,1,0:T(1,128)}), f32[32,1,1024]{2,1,0:T(1,128)S(1)}, u32[]{:S(2)}, u32[]{:S(2)}) async-start(f32[32,1,1024]{2,1,0:T(1,128)} %reshape.98), calls=%async_computation | async-start | bytes 262144 | tf_op jit(solution)/shard_map/all_to_all | solution.py:187
  231.8 5.0 %collective-permute-start.1 = (f32[32,1024]{1,0:T(8,128)S(1)}, f32[32,1024]{1,0:T(8,128)S(1)}, u32[]{:S(2)}, u32[]{:S(2)}) collective-permute-start(f32[32,1024]{1,0:T(8,128)S(1)} %bitcast_select_fusion.1), channel_id=1, source_target_pairs={{64,0},{96,32},{0,64},{32,96},{65,1},{97,33},{1,65},{33,97},{66,2}... | collective-permute-start | bytes 393224 | tf_op jit(solution)/shard_map/ppermute | solution.py:14

commit v6 on v3

--- a/solution.py
+++ b/solution.py
@@ -24,6 +24,7 @@
     incoming = passed_along(outgoing, "occ", occ_devices // 2)
     first = jnp.where(lower_half, amplitudes[0], incoming)
     second = jnp.where(lower_half, incoming, amplitudes[1])
+
     def gather_rows(block):
         spread = jnp.broadcast_to(block[None], (vir_devices,) + block.shape)
         pieces = lax.all_to_all(spread, "vir", split_axis=0, concat_axis=0, tiled=True)
@@ -38,21 +39,12 @@
 
     halves_first = half_products(gather_rows(first))
     halves_second = half_products(gather_rows(second))
-    width = factors.shape[1]
-    chunks = 4
-    chunk = width // chunks
-    own_parts = []
-    for part in range(chunks):
-        cut = slice(part * chunk, (part + 1) * chunk)
-        direct = jnp.einsum("qac,qbc->ab", factors, halves_first[:, cut], preferred_element_type=jnp.float32)
-        turned_term = jnp.einsum(
-            "qac,qbc->ab", halves_second, factors[:, cut], preferred_element_type=jnp.float32
-        )
-        combined = direct + turned_term
-        blocks = combined.reshape(vir_devices, row_count, chunk)
-        arrived = lax.all_to_all(blocks, "vir", split_axis=0, concat_axis=0, tiled=True)
-        own_parts.append(jnp.sum(arrived, axis=0))
-    own_rows = jnp.concatenate(own_parts, axis=1)
+    direct = jnp.einsum("qac,qbc->ab", factors, halves_first, preferred_element_type=jnp.float32)
+    turned_term = jnp.einsum("qac,qbc->ab", halves_second, factors, preferred_element_type=jnp.float32)
+    combined = direct + turned_term
+    blocks = combined.reshape(vir_devices, row_count, combined.shape[-1])
+    arrived = lax.all_to_all(blocks, "vir", split_axis=0, concat_axis=0, tiled=True)
+    own_rows = jnp.sum(arrived, axis=0)
     cols = lax.all_to_all(own_rows, "vir", split_axis=1, concat_axis=0, tiled=True)
     own_cols = jnp.transpose(cols, (1, 0))
     outgoing_block = jnp.where(lower_half, own_cols, own_rows)

time: 224 us -> 214 us (0.955)
  waiting for transfers between devices: 77 us -> 104 us
  matrix products: 72.4 us -> 58.3 us
  starting transfers between devices: 44.3 us -> 31.6 us
  local copies, waits for them, and re-layouts: 22 us -> 13 us
    all_to_all x4 -> x1, waiting for transfers between devices: 26.4 us -> 56.5 us  [per_device(): lax.all_to_all(blocks, 'vir', split_axis=0, concat_axis=0, tiled=True)]
    dot_general x8 -> x2, matrix products: 38.6 us -> 24.7 us  [the longest x1 12.7 us: per_device(): jnp.einsum('qac,qbc->ab', halves_second, factors, preferred_element_type=...]
    all_to_all x4 -> x1, starting transfers between devices: 21.8 us -> 10.2 us  [per_device(): lax.all_to_all(blocks, 'vir', split_axis=0, concat_axis=0, tiled=True)]
    add x4 -> x0, local copies, waits for them, and re-layouts: 9.01 us -> none  [per_device(): combined = direct + turned_term]
    all_to_all x2, waiting for transfers between devices: 34.7 us -> 30.4 us  [gather_rows(): lax.all_to_all(spread, 'vir', split_axis=0, concat_axis=0, tiled=True)]
  transfers between devices with their start and end apart: 9 -> 6, of which waited for: 9 -> 5; matrix products, arithmetic and copies ran while one was open for 30% -> 16% of each run, Pallas kernels for 0% -> 0%
where the time goes in v6:
time: 214 us
  waiting for transfers between devices  104 us (49%)
  matrix products  58.3 us (27%)
  starting transfers between devices  31.6 us (15%)
  local copies, waits for them, and re-layouts  13 us (6%)
  other arithmetic  6.63 us (3%)
    all_to_all x1, waiting for transfers between devices, per_device(): lax.all_to_all(blocks, 'vir', split_axis=0, concat_axis=0, tiled=True)  56.5 us
    dot_general x6, matrix products, half_product(): jnp.einsum('cd,bd->bc', rows, factor, preferred_element_type=jnp.float32)  33.6 us
    all_to_all x2, waiting for transfers between devices, gather_rows(): lax.all_to_all(spread, 'vir', split_axis=0, concat_axis=0, tiled=True)  30.4 us
    all_to_all x2, starting transfers between devices, gather_rows(): lax.all_to_all(spread, 'vir', split_axis=0, concat_axis=0, tiled=True)  14.9 us
    dot_general x1, matrix products, per_device(): jnp.einsum('qac,qbc->ab', halves_second, factors, preferred_element_type=...  12.7 us
    dot_general x1, matrix products, per_device(): jnp.einsum('qac,qbc->ab', factors, halves_first, preferred_element_type=j...  12 us
    all_to_all x1, starting transfers between devices, per_device(): lax.all_to_all(blocks, 'vir', split_axis=0, concat_axis=0, tiled=True)  10.2 us
    all_to_all x1, waiting for transfers between devices, per_device(): lax.all_to_all(own_rows, 'vir', split_axis=1, concat_axis=0, tiled=True)  10.1 us
  transfers between devices with their start and end apart: 6, of which 5 were waited for; matrix products, arithmetic and copies ran while one was open for 16% of the time, Pallas kernels for 0%

profile of v6, /device:TPU:0, one launch (start us, length us, event | category | flops | bytes accessed | tf_op | source)
XLA Modules:
  0.0 213.6 jit_solution(11857537725229320154)
XLA Ops:
  0.9 1.7 collective-permute-start
  2.6 2.6 %collective-permute-done = bf16[32,1024]{1,0:T(8,128)(2,1)S(1)} collective-permute-done((bf16[32,1024]{1,0:T(8,128)(2,1)S(1)}, bf16[32,1024]{1,0:T(8,128)(2,1)S(1)}, u32[]{:S(2)}, u32[]{:S(2)}) %collective-permute-start) | collective-permute-done | bytes 65568 | tf_op jit(solution)/shard_map/ppermute | solution.py:10
  7.7 10.9 %all-to-all-start = ((bf16[32,32,1024]{2,1,0:T(8,128)(2,1)}), bf16[32,32,1024]{2,1,0:T(8,128)(2,1)S(1)}, u32[]{:S(2)}, u32[]{:S(2)}) async-start(bf16[32,32,1024]{2,1,0:T(8,128)(2,1)} %broadcast_in_dim.69), calls=%async_computation | async-start | bytes 4194304 | tf_op jit(solution)/shard_map/all_to_all | solution.py:30
  18.6 30.4 %all-to-all-done = bf16[32,32,1024]{2,1,0:T(8,128)(2,1)S(1)} async-done(((bf16[32,32,1024]{2,1,0:T(8,128)(2,1)}), bf16[32,32,1024]{2,1,0:T(8,128)(2,1)S(1)}, u32[]{:S(2)}, u32[]{:S(2)}) %all-to-all-start) | async-done | bytes 2097184 | tf_op jit(solution)/shard_map/all_to_all | solution.py:30
  49.0 1.8 broadcast_in_dim.70
  51.0 4.0 %all-to-all-start.1 = ((bf16[32,32,1024]{2,1,0:T(8,128)(2,1)}), bf16[32,32,1024]{2,1,0:T(8,128)(2,1)S(1)}, u32[]{:S(2)}, u32[]{:S(2)}) async-start(bf16[32,32,1024]{2,1,0:T(8,128)(2,1)} %broadcast_in_dim.70), calls=%async_computation.1 | async-start | bytes 4194304 | tf_op jit(solution)/shard_map/all_to_all | solution.py:30
  55.1 3.5 %broadcast.53.clone = bf16[3,1024,1024]{2,1,0:T(8,128)(2,1)} broadcast(bf16[]{:T(256)} %constant.38.clone.1), dimensions={} | broadcast | bytes 6291458 | tf_op jit(solution)/shard_map/broadcast.1
  58.5 17.7 %while.20 = (s32[]{:T(128)}, bf16[3,1024,1024]{2,1,0:T(8,128)(2,1)}, bf16[3,1024,1024]{2,1,0:T(8,128)(2,1)}, bf16[1024,1024]{1,0:T(8,128)(2,1)}, s32[]{:T(128)}) while((s32[]{:T(128)}, bf16[3,1024,1024]{2,1,0:T(8,128)(2,1)}, bf16[3,1024,1024]{2,1,0:T(8,128)(2,1)}, bf16[1024,1024]{1,0:T(8,128)(2,1)}, s32[]{:T(128)}) %tuple.43), condition=%wide.region_3.4_spmd, body=%wide.region_2.3_spmd.sunk | while | flops 2148532224 | bytes 6292541 | solution.py:38
  58.5 5.9 %bitcast_dynamic-update-slice_fusion.4 = bf16[3,1024,1024]{2,1,0:T(8,128)(2,1)} fusion(bf16[3,1024,1024]{2,1,0:T(8,128)(2,1)} %get-tuple-element.133, s32[]{:T(128)} %get-tuple-element.132, bf16[1024,1024]{1,0:T(8,128)(2,1)} %get-tuple-element.140, bf16[3,1024,1024]{2,1,0:T(8,128)(2,1)} %get-tuple-element.139), kind=kOutput, calls=%fused_computation.clone.1 | convolution fusion | flops 2148532224 | bytes 6292480 | tf_op jit(solution)/shard_map/while/body/eval_jaxpr/cd,bd->bc/dot_general | solution.py:35
  64.5 5.9 %bitcast_dynamic-update-slice_fusion.4 = bf16[3,1024,1024]{2,1,0:T(8,128)(2,1)} fusion(bf16[3,1024,1024]{2,1,0:T(8,128)(2,1)} %get-tuple-element.133, s32[]{:T(128)} %get-tuple-element.132, bf16[1024,1024]{1,0:T(8,128)(2,1)} %get-tuple-element.140, bf16[3,1024,1024]{2,1,0:T(8,128)(2,1)} %get-tuple-element.139), kind=kOutput, calls=%fused_computation.clone.1 | convolution fusion | flops 2148532224 | bytes 6292480 | tf_op jit(solution)/shard_map/while/body/eval_jaxpr/cd,bd->bc/dot_general | solution.py:35
  70.3 5.9 %bitcast_dynamic-update-slice_fusion.4 = bf16[3,1024,1024]{2,1,0:T(8,128)(2,1)} fusion(bf16[3,1024,1024]{2,1,0:T(8,128)(2,1)} %get-tuple-element.133, s32[]{:T(128)} %get-tuple-element.132, bf16[1024,1024]{1,0:T(8,128)(2,1)} %get-tuple-element.140, bf16[3,1024,1024]{2,1,0:T(8,128)(2,1)} %get-tuple-element.139), kind=kOutput, calls=%fused_computation.clone.1 | convolution fusion | flops 2148532224 | bytes 6292480 | tf_op jit(solution)/shard_map/while/body/eval_jaxpr/cd,bd->bc/dot_general | solution.py:35
  76.3 12.0 %fusion.14 = f32[1024,1024,1]{0,1,2:T(8,128)} fusion(bf16[3,1024,1024]{2,1,0:T(8,128)(2,1)} %get-tuple-element.49, bf16[3,1024,1024]{2,1,0:T(8,128)(2,1)} %get-tuple-element.166), kind=kOutput, calls=%fused_computation.33 | convolution fusion | flops 6442450944 | bytes 16777216 | tf_op jit(solution)/shard_map/qac,qbc->ab/dot_general | solution.py:42
  88.3 3.5 %broadcast.53.clone.1 = bf16[3,1024,1024]{2,1,0:T(8,128)(2,1)} broadcast(bf16[]{:T(256)} %constant.38.clone.1), dimensions={} | broadcast | bytes 6291458 | tf_op jit(solution)/shard_map/broadcast.1
  91.7 15.9 %while.21 = (s32[]{:T(128)}, bf16[3,1024,1024]{2,1,0:T(8,128)(2,1)}, bf16[3,1024,1024]{2,1,0:T(8,128)(2,1)}, bf16[1024,1024]{1,0:T(8,128)(2,1)S(1)}, s32[]{:T(128)}) while((s32[]{:T(128)}, bf16[3,1024,1024]{2,1,0:T(8,128)(2,1)}, bf16[3,1024,1024]{2,1,0:T(8,128)(2,1)}, bf16[1024,1024]{1,0:T(8,128)(2,1)S(1)}, s32[]{:T(128)}) %tuple.44), condition=%wide.region_5.6_spmd, body=%wide.region_4.5_spmd.sunk | while | flops 2148532224 | bytes 6292541 | solution.py:38
  91.7 5.3 %bitcast_dynamic-update-slice_fusion.5 = bf16[3,1024,1024]{2,1,0:T(8,128)(2,1)} fusion(bf16[3,1024,1024]{2,1,0:T(8,128)(2,1)} %get-tuple-element.148, s32[]{:T(128)} %get-tuple-element.147, bf16[1024,1024]{1,0:T(8,128)(2,1)S(1)} %get-tuple-element.155, bf16[3,1024,1024]{2,1,0:T(8,128)(2,1)} %get-tuple-element.154), kind=kOutput, calls=%fused_computation.5.clone.1 | convolution fusion | flops 2148532224 | bytes 6292480 | tf_op jit(solution)/shard_map/while/body/eval_jaxpr/cd,bd->bc/dot_general | solution.py:35
  97.0 5.3 %bitcast_dynamic-update-slice_fusion.5 = bf16[3,1024,1024]{2,1,0:T(8,128)(2,1)} fusion(bf16[3,1024,1024]{2,1,0:T(8,128)(2,1)} %get-tuple-element.148, s32[]{:T(128)} %get-tuple-element.147, bf16[1024,1024]{1,0:T(8,128)(2,1)S(1)} %get-tuple-element.155, bf16[3,1024,1024]{2,1,0:T(8,128)(2,1)} %get-tuple-element.154), kind=kOutput, calls=%fused_computation.5.clone.1 | convolution fusion | flops 2148532224 | bytes 6292480 | tf_op jit(solution)/shard_map/while/body/eval_jaxpr/cd,bd->bc/dot_general | solution.py:35
  102.3 5.3 %bitcast_dynamic-update-slice_fusion.5 = bf16[3,1024,1024]{2,1,0:T(8,128)(2,1)} fusion(bf16[3,1024,1024]{2,1,0:T(8,128)(2,1)} %get-tuple-element.148, s32[]{:T(128)} %get-tuple-element.147, bf16[1024,1024]{1,0:T(8,128)(2,1)S(1)} %get-tuple-element.155, bf16[3,1024,1024]{2,1,0:T(8,128)(2,1)} %get-tuple-element.154), kind=kOutput, calls=%fused_computation.5.clone.1 | convolution fusion | flops 2148532224 | bytes 6292480 | tf_op jit(solution)/shard_map/while/body/eval_jaxpr/cd,bd->bc/dot_general | solution.py:35
  107.6 12.7 %bitcast_add_fusion = f32[1024,1024]{1,0:T(8,128)} fusion(f32[1024,1024,1]{0,1,2:T(8,128)} %fusion.14, bf16[3,1024,1024]{2,1,0:T(8,128)(2,1)} %get-tuple-element.50, bf16[3,1024,1024]{2,1,0:T(8,128)(2,1)} %get-tuple-element.167), kind=kOutput, calls=%fused_computation.10 | convolution fusion | flops 6443499520 | bytes 20971520 | tf_op jit(solution)/shard_map/qac,qbc->ab/dot_general | solution.py:43
  120.3 10.2 %all-to-all-start.2 = ((f32[32,32,1024]{2,1,0:T(8,128)}), f32[32,32,1024]{2,1,0:T(8,128)}, u32[]{:S(2)}, u32[]{:S(2)}) async-start(f32[32,32,1024]{2,1,0:T(8,128)} %bitcast.67), calls=%async_computation.2 | async-start | bytes 8388608 | tf_op jit(solution)/shard_map/all_to_all | solution.py:46
  131.3 56.5 %all-to-all-done.2 = f32[32,32,1024]{2,1,0:T(8,128)} async-done(((f32[32,32,1024]{2,1,0:T(8,128)}), f32[32,32,1024]{2,1,0:T(8,128)}, u32[]{:S(2)}, u32[]{:S(2)}) %all-to-all-start.2) | async-done | bytes 4194336 | tf_op jit(solution)/shard_map/all_to_all | solution.py:46
  187.8 2.4 %reduce_sum.47 = f32[32,1024]{1,0:T(8,128)S(1)} reduce(f32[32,32,1024]{2,1,0:T(8,128)} %all-to-all-done.2, f32[]{:T(128)} %constant.39.clone.1), dimensions={0}, to_apply=%region_6.7 | reduce | flops 1015808 | bytes 4325380 | tf_op jit(solution)/shard_map/reduce_sum | solution.py:47
  191.6 4.0 %all-to-all-start.3 = ((f32[32,1,1024]{2,1,0:T(1,128)}), f32[32,1,1024]{2,1,0:T(1,128)S(1)}, u32[]{:S(2)}, u32[]{:S(2)}) async-start(f32[32,1,1024]{2,1,0:T(1,128)} %reshape.95), calls=%async_computation.3 | async-start | bytes 262144 | tf_op jit(solution)/shard_map/all_to_all | solution.py:48
  195.7 10.1 %all-to-all-done.3 = f32[32,1,1024]{2,1,0:T(1,128)S(1)} async-done(((f32[32,1,1024]{2,1,0:T(1,128)}), f32[32,1,1024]{2,1,0:T(1,128)S(1)}, u32[]{:S(2)}, u32[]{:S(2)}) %all-to-all-start.3) | async-done | bytes 131104 | tf_op jit(solution)/shard_map/all_to_all | solution.py:48
  208.4 4.3 %collective-permute-done.1 = f32[32,1024]{1,0:T(8,128)S(1)} collective-permute-done((f32[32,1024]{1,0:T(8,128)S(1)}, f32[32,1024]{1,0:T(8,128)S(1)}, u32[]{:S(2)}, u32[]{:S(2)}) %collective-permute-start.1) | collective-permute-done | bytes 131104 | tf_op jit(solution)/shard_map/ppermute | solution.py:10
  (37 shorter events, 9.2 us)
Async XLA Ops:
  0.0 130.8 %copy-start = (s32[8,2]{0,1:T(2,128)S(1)}, s32[8,2]{0,1:T(2,128)}, u32[]{:S(2)}) copy-start(s32[8,2]{0,1:T(2,128)} %param.17) | copy-start | bytes 196
  0.9 4.3 %collective-permute-start = (bf16[32,1024]{1,0:T(8,128)(2,1)S(1)}, bf16[32,1024]{1,0:T(8,128)(2,1)S(1)}, u32[]{:S(2)}, u32[]{:S(2)}) collective-permute-start(bf16[32,1024]{1,0:T(8,128)(2,1)S(1)} %bitcast_select_fusion.3), channel_id=1, source_target_pairs={{64,0},{96,32},{0,64},{32,96},{65,1},{97,33},{1,65},{33,97},{66,2}... | collective-permute-start | bytes 196616 | tf_op jit(solution)/shard_map/ppermute | solution.py:10
  7.7 41.3 %all-to-all-start = ((bf16[32,32,1024]{2,1,0:T(8,128)(2,1)}), bf16[32,32,1024]{2,1,0:T(8,128)(2,1)S(1)}, u32[]{:S(2)}, u32[]{:S(2)}) async-start(bf16[32,32,1024]{2,1,0:T(8,128)(2,1)} %broadcast_in_dim.69), calls=%async_computation | async-start | bytes 4194304 | tf_op jit(solution)/shard_map/all_to_all | solution.py:30
  49.0 2.0 copy-start.1
  51.0 37.2 %all-to-all-start.1 = ((bf16[32,32,1024]{2,1,0:T(8,128)(2,1)}), bf16[32,32,1024]{2,1,0:T(8,128)(2,1)S(1)}, u32[]{:S(2)}, u32[]{:S(2)}) async-start(bf16[32,32,1024]{2,1,0:T(8,128)(2,1)} %broadcast_in_dim.70), calls=%async_computation.1 | async-start | bytes 4194304 | tf_op jit(solution)/shard_map/all_to_all | solution.py:30
  120.3 10.3 %copy-start.2 = (s32[1024]{0:T(1024)S(1)}, s32[1024]{0:T(1024)}, u32[]{:S(2)}) copy-start(s32[1024]{0:T(1024)} %param.16) | copy-start | bytes 12292
  120.3 10.4 %copy-start.3 = (f32[1024]{0:T(1024)S(1)}, f32[1024]{0:T(1024)}, u32[]{:S(2)}) copy-start(f32[1024]{0:T(1024)} %param.14) | copy-start | bytes 12292
  120.3 10.5 %copy-start.4 = (s32[100]{0:T(128)S(1)}, s32[100]{0:T(128)}, u32[]{:S(2)}) copy-start(s32[100]{0:T(128)} %param.15) | copy-start | bytes 1204
  120.3 10.7 %copy-start.5 = (f32[100]{0:T(128)S(1)}, f32[100]{0:T(128)}, u32[]{:S(2)}) copy-start(f32[100]{0:T(128)} %param.13) | copy-start | bytes 1204
  120.3 67.4 %all-to-all-start.2 = ((f32[32,32,1024]{2,1,0:T(8,128)}), f32[32,32,1024]{2,1,0:T(8,128)}, u32[]{:S(2)}, u32[]{:S(2)}) async-start(f32[32,32,1024]{2,1,0:T(8,128)} %bitcast.67), calls=%async_computation.2 | async-start | bytes 8388608 | tf_op jit(solution)/shard_map/all_to_all | solution.py:46
  191.6 14.2 %all-to-all-start.3 = ((f32[32,1,1024]{2,1,0:T(1,128)}), f32[32,1,1024]{2,1,0:T(1,128)S(1)}, u32[]{:S(2)}, u32[]{:S(2)}) async-start(f32[32,1,1024]{2,1,0:T(1,128)} %reshape.95), calls=%async_computation.3 | async-start | bytes 262144 | tf_op jit(solution)/shard_map/all_to_all | solution.py:48
  207.7 5.0 %collective-permute-start.1 = (f32[32,1024]{1,0:T(8,128)S(1)}, f32[32,1024]{1,0:T(8,128)S(1)}, u32[]{:S(2)}, u32[]{:S(2)}) collective-permute-start(f32[32,1024]{1,0:T(8,128)S(1)} %bitcast_select_fusion.1), channel_id=1, source_target_pairs={{64,0},{96,32},{0,64},{32,96},{65,1},{97,33},{1,65},{33,97},{66,2}... | collective-permute-start | bytes 393224 | tf_op jit(solution)/shard_map/ppermute | solution.py:10

commit v7 on v6

--- a/solution.py
+++ b/solution.py
@@ -1,13 +1,145 @@
+import functools
+
 import jax
 import jax.numpy as jnp
 from jax import lax
 from jax.sharding import PartitionSpec as P
+from jax.experimental import pallas as pl
+from jax.experimental.pallas import tpu as pltpu
 
 
 def passed_along(block, axis, distance):
     devices = range(lax.axis_size(axis))
     route = [((i - distance) % len(devices), i) for i in devices]
     return lax.ppermute(block, axis, route)
+
+
+def _ladder_scatter_kernel(n, groups, factors_ref, first_ref, second_ref, out_ref, cbuf, send_sems, recv_sems, own_sem):
+    me = lax.axis_index("vir")
+    group = lax.axis_index("occ")
+    q_count = factors_ref.shape[0]
+    rows = out_ref.shape[1]
+    width = out_ref.shape[2]
+    per_group = n // groups
+    span = per_group * rows
+    tile = min(256, width)
+    tiles = width // tile
+    dims = (((1,), (1,)), ((), ()))
+
+    barrier = pltpu.get_barrier_semaphore()
+
+    def greet(k, carry):
+        pl.semaphore_signal(
+            barrier, inc=1, device_id=(group, lax.rem(me + k, n)), device_id_type=pl.DeviceIdType.MESH
+        )
+        return carry
+
+    lax.fori_loop(1, n, greet, 0)
+    pl.semaphore_wait(barrier, n - 1)
+
+    def remote(slot, i, dest):
+        return pltpu.make_async_remote_copy(
+            src_ref=cbuf.at[slot, pl.ds(i * rows, rows)],
+            dst_ref=out_ref.at[me],
+            send_sem=send_sems.at[dest],
+            recv_sem=recv_sems.at[me],
+            device_id=(group, dest),
+            device_id_type=pl.DeviceIdType.MESH,
+        )
+
+    def local(slot, i):
+        return pltpu.make_async_copy(cbuf.at[slot, pl.ds(i * rows, rows)], out_ref.at[me], own_sem)
+
+    def group_at(step):
+        return lax.rem(me // per_group + 1 + step, groups)
+
+    def settle(step):
+        slot = step % 2
+        chosen = group_at(step)
+        for i in range(per_group):
+            dest = chosen * per_group + i
+
+            @pl.when(dest != me)
+            def _():
+                remote(slot, i, dest).wait_send()
+
+            @pl.when(dest == me)
+            def _():
+                local(slot, i).wait()
+
+    for step in range(groups):
+        slot = step % 2
+        if step >= 2:
+            settle(step - 2)
+        chosen = group_at(step)
+        row0 = pl.multiple_of(chosen * span, span)
+
+        def product(t, carry):
+            col0 = pl.multiple_of(t * tile, tile)
+            acc = jnp.zeros((span, tile), jnp.float32)
+            for q in range(q_count):
+                acc += lax.dot_general(
+                    factors_ref[q, pl.ds(row0, span), :], first_ref[q, pl.ds(col0, tile), :],
+                    dims, preferred_element_type=jnp.float32,
+                )
+                acc += lax.dot_general(
+                    second_ref[q, pl.ds(row0, span), :], factors_ref[q, pl.ds(col0, tile), :],
+                    dims, preferred_element_type=jnp.float32,
+                )
+            cbuf[slot, :, pl.ds(col0, tile)] = acc
+            return carry
+
+        lax.fori_loop(0, tiles, product, 0)
+        for i in range(per_group):
+            dest = chosen * per_group + i
+
+            @pl.when(dest != me)
+            def _():
+                remote(slot, i, dest).start()
+
+            @pl.when(dest == me)
+            def _():
+                local(slot, i).start()
+
+    for step in range(max(groups - 2, 0), groups):
+        settle(step)
+
+    def arrive(k, carry):
+        source = lax.rem(me + k, n)
+        pltpu.make_async_remote_copy(
+            src_ref=cbuf.at[0, pl.ds(0, rows)],
+            dst_ref=out_ref.at[source],
+            send_sem=send_sems.at[source],
+            recv_sem=recv_sems.at[source],
+            device_id=(group, source),
+            device_id_type=pl.DeviceIdType.MESH,
+        ).wait_recv()
+        return carry
+
+    lax.fori_loop(1, n, arrive, 0)
+
+
+def ladder_rows(factors, first_halves, second_halves, vir_axis):
+    n = lax.axis_size(vir_axis)
+    width = factors.shape[1]
+    rows = width // n
+    groups = 4
+    arrived = pl.pallas_call(
+        functools.partial(_ladder_scatter_kernel, n, groups),
+        out_shape=jax.ShapeDtypeStruct((n, rows, width), jnp.float32),
+        in_specs=[pl.BlockSpec(memory_space=pltpu.VMEM)] * 3,
+        out_specs=pl.BlockSpec(memory_space=pl.ANY),
+        scratch_shapes=[
+            pltpu.VMEM((2, (n // groups) * rows, width), jnp.float32),
+            pltpu.SemaphoreType.DMA((n,)),
+            pltpu.SemaphoreType.DMA((n,)),
+            pltpu.SemaphoreType.DMA,
+        ],
+        compiler_params=pltpu.CompilerParams(
+            collective_id=0, has_side_effects=True, vmem_limit_bytes=48 * 1024 * 1024
+        ),
+    )(factors, first_halves, second_halves)
+    return jnp.sum(arrived, axis=0)
 
 
 def per_device(amplitudes, factors, occ_energy, vir_energy, occ_irrep, vir_irrep, pair_orbitals):
@@ -39,12 +171,7 @@
 
     halves_first = half_products(gather_rows(first))
     halves_second = half_products(gather_rows(second))
-    direct = jnp.einsum("qac,qbc->ab", factors, halves_first, preferred_element_type=jnp.float32)
-    turned_term = jnp.einsum("qac,qbc->ab", halves_second, factors, preferred_element_type=jnp.float32)
-    combined = direct + turned_term
-    blocks = combined.reshape(vir_devices, row_count, combined.shape[-1])
-    arrived = lax.all_to_all(blocks, "vir", split_axis=0, concat_axis=0, tiled=True)
-    own_rows = jnp.sum(arrived, axis=0)
+    own_rows = ladder_rows(factors, halves_first, halves_second, "vir")
     cols = lax.all_to_all(own_rows, "vir", split_axis=1, concat_axis=0, tiled=True)
     own_cols = jnp.transpose(cols, (1, 0))
     outgoing_block = jnp.where(lower_half, own_cols, own_rows)

time: 214 us -> 225 us (1.051)
  Pallas kernels: 0 us -> 78 us
  waiting for transfers between devices: 104 us -> 56.5 us
  matrix products: 58.3 us -> 33.7 us
  starting transfers between devices: 31.6 us -> 34.8 us
    pallas_call x0 -> x1, Pallas kernels: none -> 78 us  [ladder_rows(): pl.pallas_call(functools.partial(_ladder_scatter_kernel, n, groups), out_...]
    all_to_all x1 -> x0, waiting for transfers between devices: 56.5 us -> none  [per_device(): lax.all_to_all(blocks, 'vir', split_axis=0, concat_axis=0, tiled=True)]
    dot_general x2 -> x0, matrix products: 24.7 us -> none  [the longest x1 12.7 us: per_device(): jnp.einsum('qac,qbc->ab', halves_second, factors, preferred_element_type=...]
    all_to_all x1, starting transfers between devices: 3.99 us -> 17.8 us  [per_device(): lax.all_to_all(own_rows, 'vir', split_axis=1, concat_axis=0, tiled=True)]
    all_to_all x1 -> x0, starting transfers between devices: 10.2 us -> none  [per_device(): lax.all_to_all(blocks, 'vir', split_axis=0, concat_axis=0, tiled=True)]
    all_to_all x2, waiting for transfers between devices: 30.4 us -> 39.2 us  [gather_rows(): lax.all_to_all(spread, 'vir', split_axis=0, concat_axis=0, tiled=True)]
  transfers between devices with their start and end apart: 6 -> 5, of which waited for: 5 -> 5; matrix products, arithmetic and copies ran while one was open for 16% -> 10% of each run, Pallas kernels for 0% -> 0%
where the time goes in v7:
time: 225 us
  Pallas kernels  78 us (35%)
  waiting for transfers between devices  56.5 us (25%)
  starting transfers between devices  34.8 us (15%)
  matrix products  33.7 us (15%)
  local copies, waits for them, and re-layouts  14.9 us (7%)
  other arithmetic  6.63 us (3%)
    pallas_call x1, Pallas kernels, ladder_rows(): pl.pallas_call(functools.partial(_ladder_scatter_kernel, n, groups), out_...  78 us
    all_to_all x2, waiting for transfers between devices, gather_rows(): lax.all_to_all(spread, 'vir', split_axis=0, concat_axis=0, tiled=True)  39.2 us
    dot_general x6, matrix products, half_product(): jnp.einsum('cd,bd->bc', rows, factor, preferred_element_type=jnp.float32)  33.7 us
    all_to_all x1, starting transfers between devices, per_device(): lax.all_to_all(own_rows, 'vir', split_axis=1, concat_axis=0, tiled=True)  17.8 us
    all_to_all x2, starting transfers between devices, gather_rows(): lax.all_to_all(spread, 'vir', split_axis=0, concat_axis=0, tiled=True)  14.9 us
    all_to_all x1, waiting for transfers between devices, per_device(): lax.all_to_all(own_rows, 'vir', split_axis=1, concat_axis=0, tiled=True)  10.1 us
    ppermute x2, waiting for transfers between devices, passed_along(): return lax.ppermute(block, axis, route)  7.23 us
    another operation x2, local copies, waits for them, and re-layouts  6.91 us
  transfers between devices with their start and end apart: 5, of which 5 were waited for; matrix products, arithmetic and copies ran while one was open for 10% of the time, Pallas kernels for 0%

profile of v7, /device:TPU:0, one launch (start us, length us, event | category | flops | bytes accessed | tf_op | source)
XLA Modules:
  0.0 224.7 jit_solution(9038025253520603054)
XLA Ops:
  0.9 1.7 collective-permute-start
  2.6 2.6 %collective-permute-done = bf16[32,1024]{1,0:T(8,128)(2,1)S(1)} collective-permute-done((bf16[32,1024]{1,0:T(8,128)(2,1)S(1)}, bf16[32,1024]{1,0:T(8,128)(2,1)S(1)}, u32[]{:S(2)}, u32[]{:S(2)}) %collective-permute-start) | collective-permute-done | bytes 65568 | tf_op jit(solution)/shard_map/ppermute | solution.py:14
  6.2 1.6 broadcast_in_dim.70
  7.8 10.9 %all-to-all-start.1 = ((bf16[32,32,1024]{2,1,0:T(8,128)(2,1)}), bf16[32,32,1024]{2,1,0:T(8,128)(2,1)S(1)}, u32[]{:S(2)}, u32[]{:S(2)}) async-start(bf16[32,32,1024]{2,1,0:T(8,128)(2,1)} %broadcast_in_dim.70), calls=%async_computation.1 | async-start | bytes 4194304 | tf_op jit(solution)/shard_map/all_to_all | solution.py:162
  18.7 30.4 %all-to-all-done.1 = bf16[32,32,1024]{2,1,0:T(8,128)(2,1)S(1)} async-done(((bf16[32,32,1024]{2,1,0:T(8,128)(2,1)}), bf16[32,32,1024]{2,1,0:T(8,128)(2,1)S(1)}, u32[]{:S(2)}, u32[]{:S(2)}) %all-to-all-start.1) | async-done | bytes 2097184 | tf_op jit(solution)/shard_map/all_to_all | solution.py:162
  49.1 1.8 broadcast_in_dim.69
  51.0 4.0 %all-to-all-start = ((bf16[32,32,1024]{2,1,0:T(8,128)(2,1)}), bf16[32,32,1024]{2,1,0:T(8,128)(2,1)S(1)}, u32[]{:S(2)}, u32[]{:S(2)}) async-start(bf16[32,32,1024]{2,1,0:T(8,128)(2,1)} %broadcast_in_dim.69), calls=%async_computation | async-start | bytes 4194304 | tf_op jit(solution)/shard_map/all_to_all | solution.py:162
  55.7 3.5 %broadcast.53.clone.1 = bf16[3,1024,1024]{2,1,0:T(8,128)(2,1)} broadcast(bf16[]{:T(256)} %constant.38.clone.1), dimensions={} | broadcast | bytes 6291458 | tf_op jit(solution)/shard_map/broadcast.1
  59.2 17.7 %while.21 = (s32[]{:T(128)}, bf16[3,1024,1024]{2,1,0:T(8,128)(2,1)}, bf16[3,1024,1024]{2,1,0:T(8,128)(2,1)}, bf16[1024,1024]{1,0:T(8,128)(2,1)}, s32[]{:T(128)}) while((s32[]{:T(128)}, bf16[3,1024,1024]{2,1,0:T(8,128)(2,1)}, bf16[3,1024,1024]{2,1,0:T(8,128)(2,1)}, bf16[1024,1024]{1,0:T(8,128)(2,1)}, s32[]{:T(128)}) %tuple.44), condition=%wide.region_5.6_spmd, body=%wide.region_4.5_spmd.sunk | while | flops 2148532224 | bytes 6292541 | solution.py:170
  59.2 5.9 %bitcast_dynamic-update-slice_fusion.5 = bf16[3,1024,1024]{2,1,0:T(8,128)(2,1)} fusion(bf16[3,1024,1024]{2,1,0:T(8,128)(2,1)} %get-tuple-element.148, s32[]{:T(128)} %get-tuple-element.147, bf16[1024,1024]{1,0:T(8,128)(2,1)} %get-tuple-element.155, bf16[3,1024,1024]{2,1,0:T(8,128)(2,1)} %get-tuple-element.154), kind=kOutput, calls=%fused_computation.5.clone.1 | convolution fusion | flops 2148532224 | bytes 6292480 | tf_op jit(solution)/shard_map/while/body/eval_jaxpr/cd,bd->bc/dot_general | solution.py:167
  65.1 5.9 %bitcast_dynamic-update-slice_fusion.5 = bf16[3,1024,1024]{2,1,0:T(8,128)(2,1)} fusion(bf16[3,1024,1024]{2,1,0:T(8,128)(2,1)} %get-tuple-element.148, s32[]{:T(128)} %get-tuple-element.147, bf16[1024,1024]{1,0:T(8,128)(2,1)} %get-tuple-element.155, bf16[3,1024,1024]{2,1,0:T(8,128)(2,1)} %get-tuple-element.154), kind=kOutput, calls=%fused_computation.5.clone.1 | convolution fusion | flops 2148532224 | bytes 6292480 | tf_op jit(solution)/shard_map/while/body/eval_jaxpr/cd,bd->bc/dot_general | solution.py:167
  71.0 5.9 %bitcast_dynamic-update-slice_fusion.5 = bf16[3,1024,1024]{2,1,0:T(8,128)(2,1)} fusion(bf16[3,1024,1024]{2,1,0:T(8,128)(2,1)} %get-tuple-element.148, s32[]{:T(128)} %get-tuple-element.147, bf16[1024,1024]{1,0:T(8,128)(2,1)} %get-tuple-element.155, bf16[3,1024,1024]{2,1,0:T(8,128)(2,1)} %get-tuple-element.154), kind=kOutput, calls=%fused_computation.5.clone.1 | convolution fusion | flops 2148532224 | bytes 6292480 | tf_op jit(solution)/shard_map/while/body/eval_jaxpr/cd,bd->bc/dot_general | solution.py:167
  76.9 8.8 %all-to-all-done = bf16[32,32,1024]{2,1,0:T(8,128)(2,1)S(1)} async-done(((bf16[32,32,1024]{2,1,0:T(8,128)(2,1)}), bf16[32,32,1024]{2,1,0:T(8,128)(2,1)S(1)}, u32[]{:S(2)}, u32[]{:S(2)}) %all-to-all-start) | async-done | bytes 2097184 | tf_op jit(solution)/shard_map/all_to_all | solution.py:162
  85.7 3.5 %broadcast.53.clone = bf16[3,1024,1024]{2,1,0:T(8,128)(2,1)} broadcast(bf16[]{:T(256)} %constant.38.clone.1), dimensions={} | broadcast | bytes 6291458 | tf_op jit(solution)/shard_map/broadcast.1
  89.2 15.9 %while.20 = (s32[]{:T(128)}, bf16[3,1024,1024]{2,1,0:T(8,128)(2,1)}, bf16[3,1024,1024]{2,1,0:T(8,128)(2,1)}, bf16[1024,1024]{1,0:T(8,128)(2,1)S(1)}, s32[]{:T(128)}) while((s32[]{:T(128)}, bf16[3,1024,1024]{2,1,0:T(8,128)(2,1)}, bf16[3,1024,1024]{2,1,0:T(8,128)(2,1)}, bf16[1024,1024]{1,0:T(8,128)(2,1)S(1)}, s32[]{:T(128)}) %tuple.43), condition=%wide.region_3.4_spmd, body=%wide.region_2.3_spmd.sunk | while | flops 2148532224 | bytes 6292541 | solution.py:170
  89.2 5.3 %bitcast_dynamic-update-slice_fusion.4 = bf16[3,1024,1024]{2,1,0:T(8,128)(2,1)} fusion(bf16[3,1024,1024]{2,1,0:T(8,128)(2,1)} %get-tuple-element.133, s32[]{:T(128)} %get-tuple-element.132, bf16[1024,1024]{1,0:T(8,128)(2,1)S(1)} %get-tuple-element.140, bf16[3,1024,1024]{2,1,0:T(8,128)(2,1)} %get-tuple-element.139), kind=kOutput, calls=%fused_computation.clone.1 | convolution fusion | flops 2148532224 | bytes 6292480 | tf_op jit(solution)/shard_map/while/body/eval_jaxpr/cd,bd->bc/dot_general | solution.py:167
  94.5 5.3 %bitcast_dynamic-update-slice_fusion.4 = bf16[3,1024,1024]{2,1,0:T(8,128)(2,1)} fusion(bf16[3,1024,1024]{2,1,0:T(8,128)(2,1)} %get-tuple-element.133, s32[]{:T(128)} %get-tuple-element.132, bf16[1024,1024]{1,0:T(8,128)(2,1)S(1)} %get-tuple-element.140, bf16[3,1024,1024]{2,1,0:T(8,128)(2,1)} %get-tuple-element.139), kind=kOutput, calls=%fused_computation.clone.1 | convolution fusion | flops 2148532224 | bytes 6292480 | tf_op jit(solution)/shard_map/while/body/eval_jaxpr/cd,bd->bc/dot_general | solution.py:167
  99.8 5.3 %bitcast_dynamic-update-slice_fusion.4 = bf16[3,1024,1024]{2,1,0:T(8,128)(2,1)} fusion(bf16[3,1024,1024]{2,1,0:T(8,128)(2,1)} %get-tuple-element.133, s32[]{:T(128)} %get-tuple-element.132, bf16[1024,1024]{1,0:T(8,128)(2,1)S(1)} %get-tuple-element.140, bf16[3,1024,1024]{2,1,0:T(8,128)(2,1)} %get-tuple-element.139), kind=kOutput, calls=%fused_computation.clone.1 | convolution fusion | flops 2148532224 | bytes 6292480 | tf_op jit(solution)/shard_map/while/body/eval_jaxpr/cd,bd->bc/dot_general | solution.py:167
  105.1 78.0 %shard_map.73 = f32[32,32,1024]{2,1,0:T(8,128)S(1)} custom-call(bf16[3,1024,1024]{2,1,0:T(8,128)(2,1)} %get-tuple-element.158, bf16[3,1024,1024]{2,1,0:T(8,128)(2,1)} %get-tuple-element.49.first_ref, bf16[3,1024,1024]{2,1,0:T(8,128)(2,1)} %get-tuple-element.50.second_ref), custom_call_target="tpu_custom_call" | custom-call | tf_op jit(solution)/shard_map/pallas_call | solution.py:127
  183.1 1.9 copy-done.1
  185.0 2.4 %reduce_sum.47 = f32[32,1024]{1,0:T(8,128)S(1)} reduce(f32[32,32,1024]{2,1,0:T(8,128)} %copy-done.1, f32[]{:T(128)} %constant.39.clone.1), dimensions={0}, to_apply=%region_6.7 | reduce | flops 1015808 | bytes 4325380 | tf_op jit(solution)/shard_map/reduce_sum | solution.py:142
  188.8 17.8 %all-to-all-start.2 = ((f32[32,1,1024]{2,1,0:T(1,128)}), f32[32,1,1024]{2,1,0:T(1,128)S(1)}, u32[]{:S(2)}, u32[]{:S(2)}) async-start(f32[32,1,1024]{2,1,0:T(1,128)} %reshape.89), calls=%async_computation.2 | async-start | bytes 262144 | tf_op jit(solution)/shard_map/all_to_all | solution.py:175
  206.8 10.1 %all-to-all-done.2 = f32[32,1,1024]{2,1,0:T(1,128)S(1)} async-done(((f32[32,1,1024]{2,1,0:T(1,128)}), f32[32,1,1024]{2,1,0:T(1,128)S(1)}, u32[]{:S(2)}, u32[]{:S(2)}) %all-to-all-start.2) | async-done | bytes 131104 | tf_op jit(solution)/shard_map/all_to_all | solution.py:175
  219.2 4.6 %collective-permute-done.1 = f32[32,1024]{1,0:T(8,128)S(1)} collective-permute-done((f32[32,1024]{1,0:T(8,128)S(1)}, f32[32,1024]{1,0:T(8,128)S(1)}, u32[]{:S(2)}, u32[]{:S(2)}) %collective-permute-start.1) | collective-permute-done | bytes 131104 | tf_op jit(solution)/shard_map/ppermute | solution.py:14
  (36 shorter events, 7.2 us)
Async XLA Ops:
  0.0 55.0 %copy-start = (s32[8,2]{0,1:T(2,128)S(1)}, s32[8,2]{0,1:T(2,128)}, u32[]{:S(2)}) copy-start(s32[8,2]{0,1:T(2,128)} %param.17) | copy-start | bytes 196
  0.9 4.3 %collective-permute-start = (bf16[32,1024]{1,0:T(8,128)(2,1)S(1)}, bf16[32,1024]{1,0:T(8,128)(2,1)S(1)}, u32[]{:S(2)}, u32[]{:S(2)}) collective-permute-start(bf16[32,1024]{1,0:T(8,128)(2,1)S(1)} %bitcast_select_fusion.3), channel_id=1, source_target_pairs={{64,0},{96,32},{0,64},{32,96},{65,1},{97,33},{1,65},{33,97},{66,2}... | collective-permute-start | bytes 196616 | tf_op jit(solution)/shard_map/ppermute | solution.py:14
  6.1 49.0 %copy-start.3 = (s32[1024]{0:T(1024)S(1)}, s32[1024]{0:T(1024)}, u32[]{:S(2)}) copy-start(s32[1024]{0:T(1024)} %param.16) | copy-start | bytes 12292
  6.1 49.1 %copy-start.4 = (f32[1024]{0:T(1024)S(1)}, f32[1024]{0:T(1024)}, u32[]{:S(2)}) copy-start(f32[1024]{0:T(1024)} %param.14) | copy-start | bytes 12292
  6.2 49.1 %copy-start.5 = (s32[100]{0:T(128)S(1)}, s32[100]{0:T(128)}, u32[]{:S(2)}) copy-start(s32[100]{0:T(128)} %param.15) | copy-start | bytes 1204
  6.2 49.3 %copy-start.6 = (f32[100]{0:T(128)S(1)}, f32[100]{0:T(128)}, u32[]{:S(2)}) copy-start(f32[100]{0:T(128)} %param.13) | copy-start | bytes 1204
  7.8 41.3 %all-to-all-start.1 = ((bf16[32,32,1024]{2,1,0:T(8,128)(2,1)}), bf16[32,32,1024]{2,1,0:T(8,128)(2,1)S(1)}, u32[]{:S(2)}, u32[]{:S(2)}) async-start(bf16[32,32,1024]{2,1,0:T(8,128)(2,1)} %broadcast_in_dim.70), calls=%async_computation.1 | async-start | bytes 4194304 | tf_op jit(solution)/shard_map/all_to_all | solution.py:162
  49.1 2.0 copy-start.2
  51.0 34.7 %all-to-all-start = ((bf16[32,32,1024]{2,1,0:T(8,128)(2,1)}), bf16[32,32,1024]{2,1,0:T(8,128)(2,1)S(1)}, u32[]{:S(2)}, u32[]{:S(2)}) async-start(bf16[32,32,1024]{2,1,0:T(8,128)(2,1)} %broadcast_in_dim.69), calls=%async_computation | async-start | bytes 4194304 | tf_op jit(solution)/shard_map/all_to_all | solution.py:162
  183.1 1.9 copy-start.1
  188.8 28.1 %all-to-all-start.2 = ((f32[32,1,1024]{2,1,0:T(1,128)}), f32[32,1,1024]{2,1,0:T(1,128)S(1)}, u32[]{:S(2)}, u32[]{:S(2)}) async-start(f32[32,1,1024]{2,1,0:T(1,128)} %reshape.89), calls=%async_computation.2 | async-start | bytes 262144 | tf_op jit(solution)/shard_map/all_to_all | solution.py:175
  218.8 5.0 %collective-permute-start.1 = (f32[32,1024]{1,0:T(8,128)S(1)}, f32[32,1024]{1,0:T(8,128)S(1)}, u32[]{:S(2)}, u32[]{:S(2)}) collective-permute-start(f32[32,1024]{1,0:T(8,128)S(1)} %bitcast_select_fusion.1), channel_id=1, source_target_pairs={{64,0},{96,32},{0,64},{32,96},{65,1},{97,33},{1,65},{33,97},{66,2}... | collective-permute-start | bytes 393224 | tf_op jit(solution)/shard_map/ppermute | solution.py:14

commit v8 on v6

--- a/solution.py
+++ b/solution.py
@@ -20,10 +20,9 @@
     vir_index = lax.axis_index("vir")
     lower_half = occ_index < occ_devices // 2
 
+    own = jnp.where(lower_half, amplitudes[0], amplitudes[1])
     outgoing = jnp.where(lower_half, amplitudes[1], amplitudes[0])
-    incoming = passed_along(outgoing, "occ", occ_devices // 2)
-    first = jnp.where(lower_half, amplitudes[0], incoming)
-    second = jnp.where(lower_half, incoming, amplitudes[1])
+    other = passed_along(outgoing, "occ", occ_devices // 2)
 
     def gather_rows(block):
         spread = jnp.broadcast_to(block[None], (vir_devices,) + block.shape)
@@ -31,14 +30,11 @@
         return pieces.reshape(vir_devices * row_count, block.shape[-1])
 
     def half_products(rows):
-        def half_product(factor):
-            product = jnp.einsum("cd,bd->bc", rows, factor, preferred_element_type=jnp.float32)
-            return product.astype(jnp.bfloat16)
+        product = jnp.einsum("cd,qbd->qbc", rows, factors, preferred_element_type=jnp.float32)
+        return product.astype(jnp.bfloat16)
 
-        return lax.map(half_product, factors)
-
-    halves_first = half_products(gather_rows(first))
-    halves_second = half_products(gather_rows(second))
+    halves_first = half_products(gather_rows(own))
+    halves_second = half_products(gather_rows(other))
     direct = jnp.einsum("qac,qbc->ab", factors, halves_first, preferred_element_type=jnp.float32)
     turned_term = jnp.einsum("qac,qbc->ab", halves_second, factors, preferred_element_type=jnp.float32)
     combined = direct + turned_term
@@ -47,10 +43,9 @@
     own_rows = jnp.sum(arrived, axis=0)
     cols = lax.all_to_all(own_rows, "vir", split_axis=1, concat_axis=0, tiled=True)
     own_cols = jnp.transpose(cols, (1, 0))
-    outgoing_block = jnp.where(lower_half, own_cols, own_rows)
-    incoming_block = passed_along(outgoing_block, "occ", occ_devices // 2)
-    first_out = jnp.where(lower_half, own_rows, incoming_block)
-    second_out = jnp.where(lower_half, incoming_block, own_cols)
+    partner_cols = passed_along(own_cols, "occ", occ_devices // 2)
+    first_out = jnp.where(lower_half, own_rows, partner_cols)
+    second_out = jnp.where(lower_half, partner_cols, own_rows)
     summed_pair = jnp.stack([first_out, second_out], axis=0)
 
     pair_ids = lax.dynamic_slice_in_dim(pair_orbitals, occ_index * local_pairs, local_pairs, 0)

time: 214 us -> 193 us (0.902)
  matrix products: 58.3 us -> 39.5 us
  waiting for transfers between devices: 104 us -> 114 us
  local copies, waits for them, and re-layouts: 13 us -> 5.79 us
  starting transfers between devices: 31.6 us -> 26.6 us
    dot_general x6 -> x0, matrix products: 33.6 us -> none  [half_product(): jnp.einsum('cd,bd->bc', rows, factor, preferred_element_type=jnp.float32)]
    ppermute x2, waiting for transfers between devices: 6.88 us -> 19.4 us  [passed_along(): return lax.ppermute(block, axis, route)]
    dot_general x1, matrix products: 12 us -> 19.8 us  [per_device(): jnp.einsum('qac,qbc->ab', factors, halves_first, preferred_element_type=j...]
    dot_general x1, matrix products: 12.7 us -> 19.7 us  [per_device(): jnp.einsum('qac,qbc->ab', halves_second, factors, preferred_element_type=...]
    another operation x2 -> x0, local copies, waits for them, and re-layouts: 6.9 us -> none
    all_to_all x1, starting transfers between devices: 10.2 us -> 5 us  [per_device(): lax.all_to_all(blocks, 'vir', split_axis=0, concat_axis=0, tiled=True)]
    all_to_all x2, waiting for transfers between devices: 30.4 us -> 28.2 us  [gather_rows(): lax.all_to_all(spread, 'vir', split_axis=0, concat_axis=0, tiled=True)]
  transfers between devices with their start and end apart: 6 -> 6, of which waited for: 5 -> 6; matrix products, arithmetic and copies ran while one was open for 16% -> 11% of each run, Pallas kernels for 0% -> 0%
where the time goes in v8:
time: 193 us; the launch traced here: 192 us
  waiting for transfers between devices  114 us (59%)
  matrix products  39.5 us (20%)
  starting transfers between devices  26.6 us (14%)
  local copies, waits for them, and re-layouts  5.79 us (3%)
  other arithmetic  5.73 us (3%)
    all_to_all x1, waiting for transfers between devices, per_device(): lax.all_to_all(blocks, 'vir', split_axis=0, concat_axis=0, tiled=True)  56.6 us
    all_to_all x2, waiting for transfers between devices, gather_rows(): lax.all_to_all(spread, 'vir', split_axis=0, concat_axis=0, tiled=True)  28.2 us
    dot_general x1, matrix products, per_device(): jnp.einsum('qac,qbc->ab', factors, halves_first, preferred_element_type=j...  19.8 us
    dot_general x1, matrix products, per_device(): jnp.einsum('qac,qbc->ab', halves_second, factors, preferred_element_type=...  19.7 us
    ppermute x2, waiting for transfers between devices, passed_along(): return lax.ppermute(block, axis, route)  19.4 us
    all_to_all x2, starting transfers between devices, gather_rows(): lax.all_to_all(spread, 'vir', split_axis=0, concat_axis=0, tiled=True)  16.4 us
    all_to_all x1, waiting for transfers between devices, per_device(): lax.all_to_all(own_rows, 'vir', split_axis=1, concat_axis=0, tiled=True)  10.1 us
    all_to_all x1, starting transfers between devices, per_device(): lax.all_to_all(blocks, 'vir', split_axis=0, concat_axis=0, tiled=True)  5 us
  transfers between devices with their start and end apart: 6, of which 6 were waited for; matrix products, arithmetic and copies ran while one was open for 11% of the time, Pallas kernels for 0%

profile of v8, /device:TPU:0, one launch (start us, length us, event | category | flops | bytes accessed | tf_op | source)
XLA Modules:
  0.0 192.1 jit_solution(1124551243768346370)
XLA Ops:
  0.0 0.9 select_bitcast_fusion.2
  0.9 1.6 broadcast_in_dim.65
  2.5 10.9 %all-to-all-start = ((bf16[32,32,1024]{2,1,0:T(8,128)(2,1)}), bf16[32,32,1024]{2,1,0:T(8,128)(2,1)S(1)}, u32[]{:S(2)}, u32[]{:S(2)}) async-start(bf16[32,32,1024]{2,1,0:T(8,128)(2,1)} %broadcast_in_dim.65), calls=%async_computation | async-start | bytes 4194304 | tf_op jit(solution)/shard_map/all_to_all | solution.py:29
  13.4 0.8 collective-permute-start
  14.1 15.1 %collective-permute-done = bf16[32,1024]{1,0:T(8,128)(2,1)S(1)} collective-permute-done((bf16[32,1024]{1,0:T(8,128)(2,1)S(1)}, bf16[32,1024]{1,0:T(8,128)(2,1)S(1)}, u32[]{:S(2)}, u32[]{:S(2)}) %collective-permute-start) | collective-permute-done | bytes 65568 | tf_op jit(solution)/shard_map/ppermute | solution.py:10
  29.2 16.1 %all-to-all-done = bf16[32,32,1024]{2,1,0:T(8,128)(2,1)S(1)} async-done(((bf16[32,32,1024]{2,1,0:T(8,128)(2,1)}), bf16[32,32,1024]{2,1,0:T(8,128)(2,1)S(1)}, u32[]{:S(2)}, u32[]{:S(2)}) %all-to-all-start) | async-done | bytes 2097184 | tf_op jit(solution)/shard_map/all_to_all | solution.py:29
  45.3 1.6 broadcast_in_dim.66
  46.9 5.5 %all-to-all-start.1 = ((bf16[32,32,1024]{2,1,0:T(8,128)(2,1)}), bf16[32,32,1024]{2,1,0:T(8,128)(2,1)}, u32[]{:S(2)}, u32[]{:S(2)}) async-start(bf16[32,32,1024]{2,1,0:T(8,128)(2,1)} %broadcast_in_dim.66), calls=%async_computation.1 | async-start | bytes 4194304 | tf_op jit(solution)/shard_map/all_to_all | solution.py:29
  52.4 19.8 %fusion.2 = f32[1024,1024,1]{0,1,2:T(8,128)} fusion(bf16[3,1024,1024]{2,1,0:T(8,128)(2,1)} %param.8, bf16[1024,1024,1]{1,0,2:T(8,128)(2,1)S(1)} %bitcast.50), kind=kOutput, calls=%fused_computation.2 | convolution fusion | flops 12888047616 | bytes 12582912 | tf_op jit(solution)/shard_map/qac,qbc->ab/dot_general | solution.py:38
  72.1 12.1 %all-to-all-done.1 = bf16[32,32,1024]{2,1,0:T(8,128)(2,1)} async-done(((bf16[32,32,1024]{2,1,0:T(8,128)(2,1)}), bf16[32,32,1024]{2,1,0:T(8,128)(2,1)}, u32[]{:S(2)}, u32[]{:S(2)}) %all-to-all-start.1) | async-done | bytes 2097184 | tf_op jit(solution)/shard_map/all_to_all | solution.py:29
  84.2 19.7 %bitcast_add_fusion = f32[1024,1024]{1,0:T(8,128)} fusion(f32[1024,1024,1]{0,1,2:T(8,128)} %fusion.2, bf16[3,1024,1024]{2,1,0:T(8,128)(2,1)} %param.8, bf16[1024,1024,1]{1,0,2:T(8,128)(2,1)} %bitcast.10), kind=kOutput, calls=%fused_computation.6 | convolution fusion | flops 12889096192 | bytes 16777216 | tf_op jit(solution)/shard_map/qac,qbc->ab/dot_general | solution.py:39
  104.0 5.0 %all-to-all-start.2 = ((f32[32,32,1024]{2,1,0:T(8,128)}), f32[32,32,1024]{2,1,0:T(8,128)}, u32[]{:S(2)}, u32[]{:S(2)}) async-start(f32[32,32,1024]{2,1,0:T(8,128)} %bitcast.48), calls=%async_computation.2 | async-start | bytes 8388608 | tf_op jit(solution)/shard_map/all_to_all | solution.py:42
  109.7 56.6 %all-to-all-done.2 = f32[32,32,1024]{2,1,0:T(8,128)} async-done(((f32[32,32,1024]{2,1,0:T(8,128)}), f32[32,32,1024]{2,1,0:T(8,128)}, u32[]{:S(2)}, u32[]{:S(2)}) %all-to-all-start.2) | async-done | bytes 4194336 | tf_op jit(solution)/shard_map/all_to_all | solution.py:42
  166.3 2.4 %reduce_sum.47 = f32[32,1024]{1,0:T(8,128)S(1)} reduce(f32[32,32,1024]{2,1,0:T(8,128)} %all-to-all-done.2, f32[]{:T(128)} %constant.21.clone.1), dimensions={0}, to_apply=%region_2.3 | reduce | flops 1015808 | bytes 4325380 | tf_op jit(solution)/shard_map/reduce_sum | solution.py:43
  169.0 0.9 reshape.98
  169.9 3.9 %all-to-all-start.3 = ((f32[32,1,1024]{2,1,0:T(1,128)}), f32[32,1,1024]{2,1,0:T(1,128)S(1)}, u32[]{:S(2)}, u32[]{:S(2)}) async-start(f32[32,1,1024]{2,1,0:T(1,128)} %reshape.98), calls=%async_computation.3 | async-start | bytes 262144 | tf_op jit(solution)/shard_map/all_to_all | solution.py:44
  173.9 10.1 %all-to-all-done.3 = f32[32,1,1024]{2,1,0:T(1,128)S(1)} async-done(((f32[32,1,1024]{2,1,0:T(1,128)}), f32[32,1,1024]{2,1,0:T(1,128)S(1)}, u32[]{:S(2)}, u32[]{:S(2)}) %all-to-all-start.3) | async-done | bytes 131104 | tf_op jit(solution)/shard_map/all_to_all | solution.py:44
  184.0 0.5 broadcast.52
  184.5 1.0 reduce
  185.7 0.3 copy.17
  186.0 0.2 all_to_all.29
  186.2 0.6 collective-permute-start.1
  186.9 4.4 %collective-permute-done.1 = f32[32,1024]{1,0:T(8,128)S(1)} collective-permute-done((f32[32,1024]{1,0:T(8,128)S(1)}, f32[32,1024]{1,0:T(8,128)S(1)}, u32[]{:S(2)}, u32[]{:S(2)}) %collective-permute-start.1) | collective-permute-done | bytes 131104 | tf_op jit(solution)/shard_map/ppermute | solution.py:10
  191.3 0.8 fusion.12
  (24 shorter events, 1.3 us)
Async XLA Ops:
  0.0 109.2 %copy-start = (s32[8,2]{0,1:T(2,128)S(1)}, s32[8,2]{0,1:T(2,128)}, u32[]{:S(2)}) copy-start(s32[8,2]{0,1:T(2,128)} %param.13) | copy-start | bytes 196
  2.5 42.8 %all-to-all-start = ((bf16[32,32,1024]{2,1,0:T(8,128)(2,1)}), bf16[32,32,1024]{2,1,0:T(8,128)(2,1)S(1)}, u32[]{:S(2)}, u32[]{:S(2)}) async-start(bf16[32,32,1024]{2,1,0:T(8,128)(2,1)} %broadcast_in_dim.65), calls=%async_computation | async-start | bytes 4194304 | tf_op jit(solution)/shard_map/all_to_all | solution.py:29
  13.4 15.8 %collective-permute-start = (bf16[32,1024]{1,0:T(8,128)(2,1)S(1)}, bf16[32,1024]{1,0:T(8,128)(2,1)S(1)}, u32[]{:S(2)}, u32[]{:S(2)}) collective-permute-start(bf16[32,1024]{1,0:T(8,128)(2,1)S(1)} %get-tuple-element.11), channel_id=1, source_target_pairs={{64,0},{96,32},{0,64},{32,96},{65,1},{97,33},{1,65},{33,97},{66,2}... | collective-permute-start | bytes 196616 | tf_op jit(solution)/shard_map/ppermute | solution.py:10
  46.9 37.3 %all-to-all-start.1 = ((bf16[32,32,1024]{2,1,0:T(8,128)(2,1)}), bf16[32,32,1024]{2,1,0:T(8,128)(2,1)}, u32[]{:S(2)}, u32[]{:S(2)}) async-start(bf16[32,32,1024]{2,1,0:T(8,128)(2,1)} %broadcast_in_dim.66), calls=%async_computation.1 | async-start | bytes 4194304 | tf_op jit(solution)/shard_map/all_to_all | solution.py:29
  104.0 5.0 %copy-start.2 = (f32[1024]{0:T(1024)S(1)}, f32[1024]{0:T(1024)}, u32[]{:S(2)}) copy-start(f32[1024]{0:T(1024)} %param.10) | copy-start | bytes 12292
  104.0 5.1 %copy-start.1 = (s32[1024]{0:T(1024)S(1)}, s32[1024]{0:T(1024)}, u32[]{:S(2)}) copy-start(s32[1024]{0:T(1024)} %param.12) | copy-start | bytes 12292
  104.0 5.3 %copy-start.3 = (f32[100]{0:T(128)S(1)}, f32[100]{0:T(128)}, u32[]{:S(2)}) copy-start(f32[100]{0:T(128)} %param.9) | copy-start | bytes 1204
  104.0 5.5 %copy-start.4 = (s32[100]{0:T(128)S(1)}, s32[100]{0:T(128)}, u32[]{:S(2)}) copy-start(s32[100]{0:T(128)} %param.11) | copy-start | bytes 1204
  104.0 62.4 %all-to-all-start.2 = ((f32[32,32,1024]{2,1,0:T(8,128)}), f32[32,32,1024]{2,1,0:T(8,128)}, u32[]{:S(2)}, u32[]{:S(2)}) async-start(f32[32,32,1024]{2,1,0:T(8,128)} %bitcast.48), calls=%async_computation.2 | async-start | bytes 8388608 | tf_op jit(solution)/shard_map/all_to_all | solution.py:42
  169.9 14.1 %all-to-all-start.3 = ((f32[32,1,1024]{2,1,0:T(1,128)}), f32[32,1,1024]{2,1,0:T(1,128)S(1)}, u32[]{:S(2)}, u32[]{:S(2)}) async-start(f32[32,1,1024]{2,1,0:T(1,128)} %reshape.98), calls=%async_computation.3 | async-start | bytes 262144 | tf_op jit(solution)/shard_map/all_to_all | solution.py:44
  186.2 5.0 %collective-permute-start.1 = (f32[32,1024]{1,0:T(8,128)S(1)}, f32[32,1024]{1,0:T(8,128)S(1)}, u32[]{:S(2)}, u32[]{:S(2)}) collective-permute-start(f32[32,1024]{1,0:T(8,128)S(1)} %bitcast.51), channel_id=1, source_target_pairs={{64,0},{96,32},{0,64},{32,96},{65,1},{97,33},{1,65},{33,97},{66,2}... | collective-permute-start | bytes 393224 | tf_op jit(solution)/shard_map/ppermute | solution.py:10

commit v9 on v8

--- a/solution.py
+++ b/solution.py
@@ -1,13 +1,79 @@
+import functools
+
 import jax
 import jax.numpy as jnp
 from jax import lax
 from jax.sharding import PartitionSpec as P
+from jax.experimental import pallas as pl
+from jax.experimental.pallas import tpu as pltpu
 
 
 def passed_along(block, axis, distance):
     devices = range(lax.axis_size(axis))
     route = [((i - distance) % len(devices), i) for i in devices]
     return lax.ppermute(block, axis, route)
+
+
+def _turn_kernel(n, blocks_ref, out_ref, send_sems, recv_sems):
+    me = lax.axis_index("vir")
+    group = lax.axis_index("occ")
+    partner = lax.rem(group + lax.axis_size("occ") // 2, lax.axis_size("occ"))
+
+    barrier = pltpu.get_barrier_semaphore()
+
+    def greet(k, carry):
+        pl.semaphore_signal(barrier, inc=1, device_id=(partner, k), device_id_type=pl.DeviceIdType.MESH)
+        return carry
+
+    lax.fori_loop(0, n, greet, 0)
+    pl.semaphore_wait(barrier, n)
+
+    def copy_to(k):
+        dest = lax.rem(me + k, n)
+        return pltpu.make_async_remote_copy(
+            src_ref=blocks_ref.at[dest],
+            dst_ref=out_ref.at[me],
+            send_sem=send_sems.at[dest],
+            recv_sem=recv_sems.at[me],
+            device_id=(partner, dest),
+            device_id_type=pl.DeviceIdType.MESH,
+        )
+
+    def send(k, carry):
+        copy_to(k).start()
+        return carry
+
+    lax.fori_loop(0, n, send, 0)
+
+    def finish(k, carry):
+        copy_to(k).wait_send()
+        source = lax.rem(me + n - k, n)
+        pltpu.make_async_remote_copy(
+            src_ref=blocks_ref.at[source],
+            dst_ref=out_ref.at[source],
+            send_sem=send_sems.at[source],
+            recv_sem=recv_sems.at[source],
+            device_id=(partner, source),
+            device_id_type=pl.DeviceIdType.MESH,
+        ).wait_recv()
+        return carry
+
+    lax.fori_loop(0, n, finish, 0)
+
+
+def partner_transpose(own_rows, vir_axis):
+    n = lax.axis_size(vir_axis)
+    rows, width = own_rows.shape
+    blocks = jnp.transpose(own_rows.reshape(rows, n, width // n), (1, 2, 0))
+    arrived = pl.pallas_call(
+        functools.partial(_turn_kernel, n),
+        out_shape=jax.ShapeDtypeStruct(blocks.shape, blocks.dtype),
+        in_specs=[pl.BlockSpec(memory_space=pl.ANY)],
+        out_specs=pl.BlockSpec(memory_space=pl.ANY),
+        scratch_shapes=[pltpu.SemaphoreType.DMA((n,)), pltpu.SemaphoreType.DMA((n,))],
+        compiler_params=pltpu.CompilerParams(collective_id=1, has_side_effects=True),
+    )(blocks)
+    return jnp.transpose(arrived, (1, 0, 2)).reshape(width // n, n * rows)
 
 
 def per_device(amplitudes, factors, occ_energy, vir_energy, occ_irrep, vir_irrep, pair_orbitals):
@@ -23,6 +89,7 @@
     own = jnp.where(lower_half, amplitudes[0], amplitudes[1])
     outgoing = jnp.where(lower_half, amplitudes[1], amplitudes[0])
     other = passed_along(outgoing, "occ", occ_devices // 2)
+    own, other = lax.optimization_barrier((own, other))
 
     def gather_rows(block):
         spread = jnp.broadcast_to(block[None], (vir_devices,) + block.shape)
@@ -41,9 +108,7 @@
     blocks = combined.reshape(vir_devices, row_count, combined.shape[-1])
     arrived = lax.all_to_all(blocks, "vir", split_axis=0, concat_axis=0, tiled=True)
     own_rows = jnp.sum(arrived, axis=0)
-    cols = lax.all_to_all(own_rows, "vir", split_axis=1, concat_axis=0, tiled=True)
-    own_cols = jnp.transpose(cols, (1, 0))
-    partner_cols = passed_along(own_cols, "occ", occ_devices // 2)
+    partner_cols = partner_transpose(own_rows, "vir")
     first_out = jnp.where(lower_half, own_rows, partner_cols)
     second_out = jnp.where(lower_half, partner_cols, own_rows)
     summed_pair = jnp.stack([first_out, second_out], axis=0)

time: 193 us -> 180 us (0.933)
  waiting for transfers between devices: 114 us -> 67.6 us
  blocking collectives: 0 us -> 40.2 us
  starting transfers between devices: 26.6 us -> 10.8 us
  Pallas kernels: 0 us -> 12.1 us
    all_to_all x0 -> x1, blocking collectives: none -> 40.2 us  [gather_rows(): lax.all_to_all(spread, 'vir', split_axis=0, concat_axis=0, tiled=True)]
    all_to_all x2 -> x1, waiting for transfers between devices: 28.2 us -> 8.81 us  [gather_rows(): lax.all_to_all(spread, 'vir', split_axis=0, concat_axis=0, tiled=True)]
    ppermute x2 -> x1, waiting for transfers between devices: 19.4 us -> 2.61 us  [passed_along(): return lax.ppermute(block, axis, route)]
    all_to_all x2 -> x1, starting transfers between devices: 16.4 us -> 4.01 us  [gather_rows(): lax.all_to_all(spread, 'vir', split_axis=0, concat_axis=0, tiled=True)]
    pallas_call x0 -> x1, Pallas kernels: none -> 12.1 us  [partner_transpose(): pl.pallas_call(functools.partial(_turn_kernel, n), out_shape=jax.ShapeDty...]
    all_to_all x1 -> x0, waiting for transfers between devices: 10.1 us -> none  [per_device(): lax.all_to_all(own_rows, 'vir', split_axis=1, concat_axis=0, tiled=True)]
    all_to_all x1 -> x0, starting transfers between devices: 3.86 us -> none  [per_device(): lax.all_to_all(own_rows, 'vir', split_axis=1, concat_axis=0, tiled=True)]
  transfers between devices with their start and end apart: 6 -> 3, of which waited for: 6 -> 3; matrix products, arithmetic and copies ran while one was open for 11% -> 12% of each run, Pallas kernels for 0% -> 0%
where the time goes in v9:
time: 180 us
  waiting for transfers between devices  67.6 us (38%)
  blocking collectives  40.2 us (22%)
  matrix products  39.4 us (22%)
  Pallas kernels  12.1 us (7%)
  starting transfers between devices  10.8 us (6%)
  other arithmetic  4.78 us (3%)
  local copies, waits for them, and re-layouts  4.68 us (3%)
    all_to_all x1, waiting for transfers between devices, per_device(): lax.all_to_all(blocks, 'vir', split_axis=0, concat_axis=0, tiled=True)  56.2 us
    all_to_all x1, blocking collectives, gather_rows(): lax.all_to_all(spread, 'vir', split_axis=0, concat_axis=0, tiled=True)  40.2 us
    dot_general x1, matrix products, per_device(): jnp.einsum('qac,qbc->ab', factors, halves_first, preferred_element_type=j...  20.3 us
    dot_general x1, matrix products, per_device(): jnp.einsum('qac,qbc->ab', halves_second, factors, preferred_element_type=...  19.1 us
    pallas_call x1, Pallas kernels, partner_transpose(): pl.pallas_call(functools.partial(_turn_kernel, n), out_shape=jax.ShapeDty...  12.1 us
    all_to_all x1, waiting for transfers between devices, gather_rows(): lax.all_to_all(spread, 'vir', split_axis=0, concat_axis=0, tiled=True)  8.81 us
    all_to_all x1, starting transfers between devices, per_device(): lax.all_to_all(blocks, 'vir', split_axis=0, concat_axis=0, tiled=True)  5.01 us
    all_to_all x1, starting transfers between devices, gather_rows(): lax.all_to_all(spread, 'vir', split_axis=0, concat_axis=0, tiled=True)  4.01 us
  transfers between devices with their start and end apart: 3, of which 3 were waited for; matrix products, arithmetic and copies ran while one was open for 12% of the time, Pallas kernels for 0%

profile of v9, /device:TPU:0, one launch (start us, length us, event | category | flops | bytes accessed | tf_op | source)
XLA Modules:
  0.0 179.7 jit_solution(10991497910226555341)
XLA Ops:
  0.0 0.9 select_bitcast_fusion
  0.9 1.7 collective-permute-start
  2.6 2.6 %collective-permute-done = bf16[32,1024]{1,0:T(8,128)(2,1)S(1)} collective-permute-done((bf16[32,1024]{1,0:T(8,128)(2,1)S(1)}, bf16[32,1024]{1,0:T(8,128)(2,1)S(1)}, u32[]{:S(2)}, u32[]{:S(2)}) %collective-permute-start) | collective-permute-done | bytes 65568 | tf_op jit(solution)/shard_map/ppermute | solution.py:14
  5.2 0.2 broadcast_in_dim.62
  5.5 40.2 %all_to_all.15 = bf16[32,32,1024]{2,1,0:T(8,128)(2,1)} all-to-all(bf16[32,32,1024]{2,1,0:T(8,128)(2,1)S(1)} %broadcast_in_dim.62), channel_id=1, replica_groups=mesh['occ'=4,'vir'=32] {'vir'}, dimensions={0} | all-to-all | bytes 4194304 | tf_op jit(solution)/shard_map/all_to_all | solution.py:96
  45.7 1.6 broadcast_in_dim.63
  47.3 4.0 %all-to-all-start.1 = ((bf16[32,32,1024]{2,1,0:T(8,128)(2,1)}), bf16[32,32,1024]{2,1,0:T(8,128)(2,1)S(1)}, u32[]{:S(2)}, u32[]{:S(2)}) async-start(bf16[32,32,1024]{2,1,0:T(8,128)(2,1)} %broadcast_in_dim.63), calls=%async_computation.1 | async-start | bytes 4194304 | tf_op jit(solution)/shard_map/all_to_all | solution.py:96
  51.3 20.3 %fusion.2 = f32[1024,1024,1]{0,1,2:T(8,128)} fusion(bf16[3,1024,1024]{2,1,0:T(8,128)(2,1)} %param.8, bf16[1024,1024,1]{1,0,2:T(8,128)(2,1)} %bitcast.45), kind=kOutput, calls=%fused_computation.2 | convolution fusion | flops 12888047616 | bytes 12582912 | tf_op jit(solution)/shard_map/qac,qbc->ab/dot_general | solution.py:105
  71.7 8.8 %all-to-all-done.1 = bf16[32,32,1024]{2,1,0:T(8,128)(2,1)S(1)} async-done(((bf16[32,32,1024]{2,1,0:T(8,128)(2,1)}), bf16[32,32,1024]{2,1,0:T(8,128)(2,1)S(1)}, u32[]{:S(2)}, u32[]{:S(2)}) %all-to-all-start.1) | async-done | bytes 2097184 | tf_op jit(solution)/shard_map/all_to_all | solution.py:96
  80.5 19.1 %bitcast_add_fusion = f32[1024,1024]{1,0:T(8,128)} fusion(f32[1024,1024,1]{0,1,2:T(8,128)} %fusion.2, bf16[3,1024,1024]{2,1,0:T(8,128)(2,1)} %param.8, bf16[1024,1024,1]{1,0,2:T(8,128)(2,1)S(1)} %bitcast.44), kind=kOutput, calls=%fused_computation.6 | convolution fusion | flops 12889096192 | bytes 16777216 | tf_op jit(solution)/shard_map/qac,qbc->ab/dot_general | solution.py:106
  99.6 5.0 %all-to-all-start.2 = ((f32[32,32,1024]{2,1,0:T(8,128)}), f32[32,32,1024]{2,1,0:T(8,128)}, u32[]{:S(2)}, u32[]{:S(2)}) async-start(f32[32,32,1024]{2,1,0:T(8,128)} %bitcast.42), calls=%async_computation.2 | async-start | bytes 8388608 | tf_op jit(solution)/shard_map/all_to_all | solution.py:109
  104.6 0.1 dynamic_slice.11
  104.7 0.1 dynamic_slice.10
  104.8 0.1 constant_dynamic-slice_fusion
  104.9 0.2 select_reduce_fusion
  105.1 0.2 select_reduce_fusion.2
  105.4 0.1 broadcast_add_fusion
  105.5 56.2 %all-to-all-done.2 = f32[32,32,1024]{2,1,0:T(8,128)} async-done(((f32[32,32,1024]{2,1,0:T(8,128)}), f32[32,32,1024]{2,1,0:T(8,128)}, u32[]{:S(2)}, u32[]{:S(2)}) %all-to-all-start.2) | async-done | bytes 4194336 | tf_op jit(solution)/shard_map/all_to_all | solution.py:109
  161.7 2.4 %reduce_sum.49 = f32[32,1024]{1,0:T(8,128)S(1)} reduce(f32[32,32,1024]{2,1,0:T(8,128)} %all-to-all-done.2, f32[]{:T(128)} %constant.21.clone.1), dimensions={0}, to_apply=%region_2.3 | reduce | flops 1015808 | bytes 4325380 | tf_op jit(solution)/shard_map/reduce_sum | solution.py:110
  164.1 1.0 copy.13
  165.1 12.1 %shard_map.73 = f32[32,32,32]{2,1,0:T(8,128)} custom-call(f32[32,32,32]{2,1,0:T(8,128)} %bitcast.43), custom_call_target="tpu_custom_call" | custom-call | tf_op jit(solution)/shard_map/pallas_call | solution.py:68
  177.2 1.4 copy.14
  178.5 0.2 reshape.129
  178.8 0.8 fusion.12
  (15 shorter events, 0.1 us)
Async XLA Ops:
  0.0 104.8 %copy-start = (s32[8,2]{0,1:T(2,128)S(1)}, s32[8,2]{0,1:T(2,128)}, u32[]{:S(2)}) copy-start(s32[8,2]{0,1:T(2,128)} %param.13) | copy-start | bytes 196
  0.9 4.3 %collective-permute-start = (bf16[32,1024]{1,0:T(8,128)(2,1)S(1)}, bf16[32,1024]{1,0:T(8,128)(2,1)S(1)}, u32[]{:S(2)}, u32[]{:S(2)}) collective-permute-start(bf16[32,1024]{1,0:T(8,128)(2,1)S(1)} %get-tuple-element.15), channel_id=1, source_target_pairs={{64,0},{96,32},{0,64},{32,96},{65,1},{97,33},{1,65},{33,97},{66,2}... | collective-permute-start | bytes 196616 | tf_op jit(solution)/shard_map/ppermute | solution.py:14
  47.3 33.2 %all-to-all-start.1 = ((bf16[32,32,1024]{2,1,0:T(8,128)(2,1)}), bf16[32,32,1024]{2,1,0:T(8,128)(2,1)S(1)}, u32[]{:S(2)}, u32[]{:S(2)}) async-start(bf16[32,32,1024]{2,1,0:T(8,128)(2,1)} %broadcast_in_dim.63), calls=%async_computation.1 | async-start | bytes 4194304 | tf_op jit(solution)/shard_map/all_to_all | solution.py:96
  99.6 5.0 %copy-start.2 = (f32[1024]{0:T(1024)S(1)}, f32[1024]{0:T(1024)}, u32[]{:S(2)}) copy-start(f32[1024]{0:T(1024)} %param.10) | copy-start | bytes 12292
  99.6 5.1 %copy-start.1 = (s32[1024]{0:T(1024)S(1)}, s32[1024]{0:T(1024)}, u32[]{:S(2)}) copy-start(s32[1024]{0:T(1024)} %param.12) | copy-start | bytes 12292
  99.6 5.3 %copy-start.3 = (f32[100]{0:T(128)S(1)}, f32[100]{0:T(128)}, u32[]{:S(2)}) copy-start(f32[100]{0:T(128)} %param.9) | copy-start | bytes 1204
  99.6 5.5 %copy-start.4 = (s32[100]{0:T(128)S(1)}, s32[100]{0:T(128)}, u32[]{:S(2)}) copy-start(s32[100]{0:T(128)} %param.11) | copy-start | bytes 1204
  99.6 62.1 %all-to-all-start.2 = ((f32[32,32,1024]{2,1,0:T(8,128)}), f32[32,32,1024]{2,1,0:T(8,128)}, u32[]{:S(2)}, u32[]{:S(2)}) async-start(f32[32,32,1024]{2,1,0:T(8,128)} %bitcast.42), calls=%async_computation.2 | async-start | bytes 8388608 | tf_op jit(solution)/shard_map/all_to_all | solution.py:109

commit v10 on v9

--- a/solution.py
+++ b/solution.py
@@ -105,9 +105,9 @@
     direct = jnp.einsum("qac,qbc->ab", factors, halves_first, preferred_element_type=jnp.float32)
     turned_term = jnp.einsum("qac,qbc->ab", halves_second, factors, preferred_element_type=jnp.float32)
     combined = direct + turned_term
-    blocks = combined.reshape(vir_devices, row_count, combined.shape[-1])
+    blocks = combined.reshape(vir_devices, row_count, combined.shape[-1]).astype(jnp.bfloat16)
     arrived = lax.all_to_all(blocks, "vir", split_axis=0, concat_axis=0, tiled=True)
-    own_rows = jnp.sum(arrived, axis=0)
+    own_rows = jnp.sum(arrived.astype(jnp.float32), axis=0)
     partner_cols = partner_transpose(own_rows, "vir")
     first_out = jnp.where(lower_half, own_rows, partner_cols)
     second_out = jnp.where(lower_half, partner_cols, own_rows)

time: 180 us -> 150 us (0.83)
  waiting for transfers between devices: 67.6 us -> 41.1 us
  other arithmetic: 4.78 us -> 2.71 us
    all_to_all x1, waiting for transfers between devices: 56.2 us -> 29.7 us  [per_device(): lax.all_to_all(blocks, 'vir', split_axis=0, concat_axis=0, tiled=True)]
    reduce_sum x1, other arithmetic: 2.44 us -> 0.37 us  [per_device(): own_rows = jnp.sum(arrived.astype(jnp.float32), axis=0)]
  transfers between devices with their start and end apart: 3 -> 3, of which waited for: 3 -> 3; matrix products, arithmetic and copies ran while one was open for 12% -> 14% of each run, Pallas kernels for 0% -> 0%
where the time goes in v10:
time: 150 us
  waiting for transfers between devices  41.1 us (27%)
  blocking collectives  40.2 us (27%)
  matrix products  39.1 us (26%)
  Pallas kernels  12.1 us (8%)
  starting transfers between devices  9.91 us (7%)
  local copies, waits for them, and re-layouts  4.68 us (3%)
  other arithmetic  2.71 us (2%)
    all_to_all x1, blocking collectives, gather_rows(): lax.all_to_all(spread, 'vir', split_axis=0, concat_axis=0, tiled=True)  40.2 us
    all_to_all x1, waiting for transfers between devices, per_device(): lax.all_to_all(blocks, 'vir', split_axis=0, concat_axis=0, tiled=True)  29.7 us
    dot_general x1, matrix products, per_device(): jnp.einsum('qac,qbc->ab', factors, halves_first, preferred_element_type=j...  20.3 us
    dot_general x1, matrix products, per_device(): jnp.einsum('qac,qbc->ab', halves_second, factors, preferred_element_type=...  18.8 us
    pallas_call x1, Pallas kernels, partner_transpose(): pl.pallas_call(functools.partial(_turn_kernel, n), out_shape=jax.ShapeDty...  12.1 us
    all_to_all x1, waiting for transfers between devices, gather_rows(): lax.all_to_all(spread, 'vir', split_axis=0, concat_axis=0, tiled=True)  8.81 us
    all_to_all x1, starting transfers between devices, per_device(): lax.all_to_all(blocks, 'vir', split_axis=0, concat_axis=0, tiled=True)  4.15 us
    all_to_all x1, starting transfers between devices, gather_rows(): lax.all_to_all(spread, 'vir', split_axis=0, concat_axis=0, tiled=True)  4.01 us
  transfers between devices with their start and end apart: 3, of which 3 were waited for; matrix products, arithmetic and copies ran while one was open for 14% of the time, Pallas kernels for 0%

profile of v10, /device:TPU:0, one launch (start us, length us, event | category | flops | bytes accessed | tf_op | source)
XLA Modules:
  0.0 150.0 jit_solution(4888687774855270688)
XLA Ops:
  0.0 0.9 select_bitcast_fusion
  0.9 1.7 %collective-permute-start = (bf16[32,1024]{1,0:T(8,128)(2,1)S(1)}, bf16[32,1024]{1,0:T(8,128)(2,1)S(1)}, u32[]{:S(2)}, u32[]{:S(2)}) collective-permute-start(bf16[32,1024]{1,0:T(8,128)(2,1)S(1)} %get-tuple-element.15), channel_id=1, source_target_pairs={{64,0},{96,32},{0,64},{32,96},{65,1},{97,33},{1,65},{33,97},{66,2}... | collective-permute-start | bytes 196616 | tf_op jit(solution)/shard_map/ppermute | solution.py:14
  2.6 2.6 %collective-permute-done = bf16[32,1024]{1,0:T(8,128)(2,1)S(1)} collective-permute-done((bf16[32,1024]{1,0:T(8,128)(2,1)S(1)}, bf16[32,1024]{1,0:T(8,128)(2,1)S(1)}, u32[]{:S(2)}, u32[]{:S(2)}) %collective-permute-start) | collective-permute-done | bytes 65568 | tf_op jit(solution)/shard_map/ppermute | solution.py:14
  5.2 0.2 broadcast_in_dim.62
  5.5 40.2 %all_to_all.15 = bf16[32,32,1024]{2,1,0:T(8,128)(2,1)} all-to-all(bf16[32,32,1024]{2,1,0:T(8,128)(2,1)S(1)} %broadcast_in_dim.62), channel_id=1, replica_groups=mesh['occ'=4,'vir'=32] {'vir'}, dimensions={0} | all-to-all | bytes 4194304 | tf_op jit(solution)/shard_map/all_to_all | solution.py:96
  45.7 1.6 %broadcast_in_dim.63 = bf16[32,32,1024]{2,1,0:T(8,128)(2,1)} broadcast(bf16[32,1024]{1,0:T(8,128)(2,1)S(1)} %collective-permute-done), dimensions={1,2} | broadcast | bytes 2162688 | tf_op jit(solution)/shard_map/broadcast_in_dim | solution.py:95
  47.3 4.0 %all-to-all-start.1 = ((bf16[32,32,1024]{2,1,0:T(8,128)(2,1)}), bf16[32,32,1024]{2,1,0:T(8,128)(2,1)S(1)}, u32[]{:S(2)}, u32[]{:S(2)}) async-start(bf16[32,32,1024]{2,1,0:T(8,128)(2,1)} %broadcast_in_dim.63), calls=%async_computation.1 | async-start | bytes 4194304 | tf_op jit(solution)/shard_map/all_to_all | solution.py:96
  51.3 20.3 %fusion.2 = f32[1024,1024,1]{0,1,2:T(8,128)} fusion(bf16[3,1024,1024]{2,1,0:T(8,128)(2,1)} %param.8, bf16[1024,1024,1]{1,0,2:T(8,128)(2,1)} %bitcast.47), kind=kOutput, calls=%fused_computation.2 | convolution fusion | flops 12888047616 | bytes 12582912 | tf_op jit(solution)/shard_map/qac,qbc->ab/dot_general | solution.py:105
  71.7 8.8 %all-to-all-done.1 = bf16[32,32,1024]{2,1,0:T(8,128)(2,1)S(1)} async-done(((bf16[32,32,1024]{2,1,0:T(8,128)(2,1)}), bf16[32,32,1024]{2,1,0:T(8,128)(2,1)S(1)}, u32[]{:S(2)}, u32[]{:S(2)}) %all-to-all-start.1) | async-done | bytes 2097184 | tf_op jit(solution)/shard_map/all_to_all | solution.py:96
  80.5 18.8 %fusion.6 = bf16[1024,1024]{1,0:T(8,128)(2,1)} fusion(f32[1024,1024,1]{0,1,2:T(8,128)} %fusion.2, bf16[3,1024,1024]{2,1,0:T(8,128)(2,1)} %param.8, bf16[1024,1024,1]{1,0,2:T(8,128)(2,1)S(1)} %bitcast.46), kind=kOutput, calls=%fused_computation.7 | convolution fusion | flops 12890144768 | bytes 14680064 | tf_op jit(solution)/shard_map/qac,qbc->ab/dot_general | solution.py:106
  99.3 4.2 %all-to-all-start.2 = ((bf16[32,32,1024]{2,1,0:T(8,128)(2,1)}), bf16[32,32,1024]{2,1,0:T(8,128)(2,1)S(1)}, u32[]{:S(2)}, u32[]{:S(2)}) async-start(bf16[32,32,1024]{2,1,0:T(8,128)(2,1)} %bitcast.45), calls=%async_computation.2 | async-start | bytes 4194304 | tf_op jit(solution)/shard_map/all_to_all | solution.py:109
  103.5 0.1 dynamic_slice.11
  103.6 0.1 dynamic_slice.10
  103.6 0.1 constant_dynamic-slice_fusion
  103.7 0.2 select_reduce_fusion
  104.0 0.2 select_reduce_fusion.2
  104.3 0.1 broadcast_add_fusion
  104.3 29.7 %all-to-all-done.2 = bf16[32,32,1024]{2,1,0:T(8,128)(2,1)S(1)} async-done(((bf16[32,32,1024]{2,1,0:T(8,128)(2,1)}), bf16[32,32,1024]{2,1,0:T(8,128)(2,1)S(1)}, u32[]{:S(2)}, u32[]{:S(2)}) %all-to-all-start.2) | async-done | bytes 2097184 | tf_op jit(solution)/shard_map/all_to_all | solution.py:109
  134.1 0.4 convert_reduce_fusion
  134.4 1.0 copy.13
  135.4 12.1 %shard_map.73 = f32[32,32,32]{2,1,0:T(8,128)} custom-call(f32[32,32,32]{2,1,0:T(8,128)} %bitcast.44), custom_call_target="tpu_custom_call" | custom-call | tf_op jit(solution)/shard_map/pallas_call | solution.py:68
  147.5 1.4 copy.14
  148.9 0.2 reshape.127
  149.2 0.8 fusion.13
  (15 shorter events, 0.1 us)
Async XLA Ops:
  0.0 103.6 %copy-start = (s32[8,2]{0,1:T(2,128)S(1)}, s32[8,2]{0,1:T(2,128)}, u32[]{:S(2)}) copy-start(s32[8,2]{0,1:T(2,128)} %param.13) | copy-start | bytes 196
  0.9 4.3 %collective-permute-start = (bf16[32,1024]{1,0:T(8,128)(2,1)S(1)}, bf16[32,1024]{1,0:T(8,128)(2,1)S(1)}, u32[]{:S(2)}, u32[]{:S(2)}) collective-permute-start(bf16[32,1024]{1,0:T(8,128)(2,1)S(1)} %get-tuple-element.15), channel_id=1, source_target_pairs={{64,0},{96,32},{0,64},{32,96},{65,1},{97,33},{1,65},{33,97},{66,2}... | collective-permute-start | bytes 196616 | tf_op jit(solution)/shard_map/ppermute | solution.py:14
  47.3 33.2 %all-to-all-start.1 = ((bf16[32,32,1024]{2,1,0:T(8,128)(2,1)}), bf16[32,32,1024]{2,1,0:T(8,128)(2,1)S(1)}, u32[]{:S(2)}, u32[]{:S(2)}) async-start(bf16[32,32,1024]{2,1,0:T(8,128)(2,1)} %broadcast_in_dim.63), calls=%async_computation.1 | async-start | bytes 4194304 | tf_op jit(solution)/shard_map/all_to_all | solution.py:96
  99.3 4.2 %copy-start.2 = (f32[1024]{0:T(1024)S(1)}, f32[1024]{0:T(1024)}, u32[]{:S(2)}) copy-start(f32[1024]{0:T(1024)} %param.10) | copy-start | bytes 12292
  99.3 4.3 %copy-start.1 = (s32[1024]{0:T(1024)S(1)}, s32[1024]{0:T(1024)}, u32[]{:S(2)}) copy-start(s32[1024]{0:T(1024)} %param.12) | copy-start | bytes 12292
  99.3 4.4 %copy-start.3 = (f32[100]{0:T(128)S(1)}, f32[100]{0:T(128)}, u32[]{:S(2)}) copy-start(f32[100]{0:T(128)} %param.9) | copy-start | bytes 1204
  99.3 4.7 %copy-start.4 = (s32[100]{0:T(128)S(1)}, s32[100]{0:T(128)}, u32[]{:S(2)}) copy-start(s32[100]{0:T(128)} %param.11) | copy-start | bytes 1204
  99.3 34.8 %all-to-all-start.2 = ((bf16[32,32,1024]{2,1,0:T(8,128)(2,1)}), bf16[32,32,1024]{2,1,0:T(8,128)(2,1)S(1)}, u32[]{:S(2)}, u32[]{:S(2)}) async-start(bf16[32,32,1024]{2,1,0:T(8,128)(2,1)} %bitcast.45), calls=%async_computation.2 | async-start | bytes 4194304 | tf_op jit(solution)/shard_map/all_to_all | solution.py:109

commit v11 on v10

--- a/solution.py
+++ b/solution.py
@@ -89,7 +89,6 @@
     own = jnp.where(lower_half, amplitudes[0], amplitudes[1])
     outgoing = jnp.where(lower_half, amplitudes[1], amplitudes[0])
     other = passed_along(outgoing, "occ", occ_devices // 2)
-    own, other = lax.optimization_barrier((own, other))
 
     def gather_rows(block):
         spread = jnp.broadcast_to(block[None], (vir_devices,) + block.shape)
@@ -100,7 +99,7 @@
         product = jnp.einsum("cd,qbd->qbc", rows, factors, preferred_element_type=jnp.float32)
         return product.astype(jnp.bfloat16)
 
-    halves_first = half_products(gather_rows(own))
+    halves_first = half_products(lax.all_gather(own, "vir", axis=0, tiled=True))
     halves_second = half_products(gather_rows(other))
     direct = jnp.einsum("qac,qbc->ab", factors, halves_first, preferred_element_type=jnp.float32)
     turned_term = jnp.einsum("qac,qbc->ab", halves_second, factors, preferred_element_type=jnp.float32)

time: 150 us -> 197 us (1.31)
  waiting for transfers between devices: 41.1 us -> 107 us
  blocking collectives: 40.2 us -> 0 us
  between operations: 0.12 us -> 13.5 us
  starting transfers between devices: 9.91 us -> 17.4 us
    all_gather x0 -> x1, waiting for transfers between devices: none -> 74.6 us  [per_device(): halves_first = half_products(lax.all_gather(own, 'vir', axis=0, tiled=True))]
    all_to_all x1 -> x0, blocking collectives: 40.2 us -> none  [gather_rows(): lax.all_to_all(spread, 'vir', split_axis=0, concat_axis=0, tiled=True)]
    all_to_all x1, waiting for transfers between devices: 8.81 us -> 0.01 us  [gather_rows(): lax.all_to_all(spread, 'vir', split_axis=0, concat_axis=0, tiled=True)]
    all_to_all x1, starting transfers between devices: 4.01 us -> 10.9 us  [gather_rows(): lax.all_to_all(spread, 'vir', split_axis=0, concat_axis=0, tiled=True)]
  transfers between devices with their start and end apart: 3 -> 4, of which waited for: 3 -> 3; matrix products, arithmetic and copies ran while one was open for 14% -> 12% of each run, Pallas kernels for 0% -> 0%
where the time goes in v11:
time: 197 us
  waiting for transfers between devices  107 us (54%)
  matrix products  39.3 us (20%)
  starting transfers between devices  17.4 us (9%)
  between operations  13.5 us (7%)
  Pallas kernels  12.1 us (6%)
  local copies, waits for them, and re-layouts  4.44 us (2%)
  other arithmetic  3.32 us (2%)
    all_gather x1, waiting for transfers between devices, per_device(): halves_first = half_products(lax.all_gather(own, 'vir', axis=0, tiled=True))  74.6 us
    all_to_all x1, waiting for transfers between devices, per_device(): lax.all_to_all(blocks, 'vir', split_axis=0, concat_axis=0, tiled=True)  29.3 us
    dot_general x1, matrix products, per_device(): jnp.einsum('qac,qbc->ab', factors, halves_first, preferred_element_type=j...  20.3 us
    dot_general x1, matrix products, per_device(): jnp.einsum('qac,qbc->ab', halves_second, factors, preferred_element_type=...  19 us
    pallas_call x1, Pallas kernels, partner_transpose(): pl.pallas_call(functools.partial(_turn_kernel, n), out_shape=jax.ShapeDty...  12.1 us
    all_to_all x1, starting transfers between devices, gather_rows(): lax.all_to_all(spread, 'vir', split_axis=0, concat_axis=0, tiled=True)  10.9 us
    all_to_all x1, starting transfers between devices, per_device(): lax.all_to_all(blocks, 'vir', split_axis=0, concat_axis=0, tiled=True)  4.77 us
  transfers between devices with their start and end apart: 4, of which 3 were waited for; matrix products, arithmetic and copies ran while one was open for 12% of the time, Pallas kernels for 0%

profile of v11, /device:TPU:0, one launch (start us, length us, event | category | flops | bytes accessed | tf_op | source)
XLA Modules:
  0.0 196.6 jit_solution(8619089396341628393)
XLA Ops:
  6.5 1.5 select_bitcast_fusion
  8.1 0.0 all-gather.3.cloned.1.call-update
  8.1 1.7 collective-permute-start
  9.8 2.6 %collective-permute-done = bf16[32,1024]{1,0:T(8,128)(2,1)S(1)} collective-permute-done((bf16[32,1024]{1,0:T(8,128)(2,1)S(1)}, bf16[32,1024]{1,0:T(8,128)(2,1)S(1)}, u32[]{:S(2)}, u32[]{:S(2)}) %collective-permute-start) | collective-permute-done | bytes 65568 | tf_op jit(solution)/shard_map/ppermute | solution.py:14
  12.4 1.6 broadcast_in_dim.56
  14.0 10.9 %all-to-all-start = ((bf16[32,32,1024]{2,1,0:T(8,128)(2,1)}), bf16[32,32,1024]{2,1,0:T(8,128)(2,1)S(1)}, u32[]{:S(2)}, u32[]{:S(2)}) async-start(bf16[32,32,1024]{2,1,0:T(8,128)(2,1)} %broadcast_in_dim.56), calls=%async_computation | async-start | bytes 4194304 | tf_op jit(solution)/shard_map/all_to_all | solution.py:95
  24.9 74.6 %all-gather.3.cloned.1.call-done = bf16[1,1024,1024]{2,1,0:T(8,128)(2,1)} async-done(((bf16[1,32,1024]{2,1,0:T(8,128)(2,1)}), bf16[1,1024,1024]{2,1,0:T(8,128)(2,1)}) %all-gather.3.cloned.1.call-update) | async-done | bytes 2097168 | tf_op jit(solution)/shard_map/all_gather | solution.py:102
  99.5 20.3 %fusion.2 = f32[1024,1024,1]{0,1,2:T(8,128)} fusion(bf16[3,1024,1024]{2,1,0:T(8,128)(2,1)} %param.8, bf16[1,1024,1024]{2,1,0:T(8,128)(2,1)} %all-gather.3.cloned.1.call-done), kind=kOutput, calls=%fused_computation.2 | convolution fusion | flops 12888047616 | bytes 12582912 | tf_op jit(solution)/shard_map/qac,qbc->ab/dot_general | solution.py:104
  119.9 19.0 %fusion.6 = bf16[1024,1024]{1,0:T(8,128)(2,1)} fusion(f32[1024,1024,1]{0,1,2:T(8,128)} %fusion.2, bf16[3,1024,1024]{2,1,0:T(8,128)(2,1)} %param.8, bf16[1024,1024,1]{1,0,2:T(8,128)(2,1)S(1)} %bitcast.45), kind=kOutput, calls=%fused_computation.7 | convolution fusion | flops 12890144768 | bytes 14680064 | tf_op jit(solution)/shard_map/qac,qbc->ab/dot_general | solution.py:105
  138.9 4.8 %all-to-all-start.1 = ((bf16[32,32,1024]{2,1,0:T(8,128)(2,1)}), bf16[32,32,1024]{2,1,0:T(8,128)(2,1)S(1)}, u32[]{:S(2)}, u32[]{:S(2)}) async-start(bf16[32,32,1024]{2,1,0:T(8,128)(2,1)} %bitcast.44), calls=%async_computation.1 | async-start | bytes 4194304 | tf_op jit(solution)/shard_map/all_to_all | solution.py:108
  143.7 0.1 dynamic_slice.11
  143.8 0.1 dynamic_slice.10
  143.8 0.1 constant_dynamic-slice_fusion
  143.9 0.2 select_reduce_fusion
  144.2 0.2 select_reduce_fusion.2
  144.4 0.1 broadcast_xor_fusion
  144.5 0.1 broadcast_add_fusion
  144.5 29.3 %all-to-all-done.1 = bf16[32,32,1024]{2,1,0:T(8,128)(2,1)S(1)} async-done(((bf16[32,32,1024]{2,1,0:T(8,128)(2,1)}), bf16[32,32,1024]{2,1,0:T(8,128)(2,1)S(1)}, u32[]{:S(2)}, u32[]{:S(2)}) %all-to-all-start.1) | async-done | bytes 2097184 | tf_op jit(solution)/shard_map/all_to_all | solution.py:108
  173.9 0.4 convert_reduce_fusion
  174.2 1.0 copy.13
  175.2 12.1 %shard_map.73 = f32[32,32,32]{2,1,0:T(8,128)} custom-call(f32[32,32,32]{2,1,0:T(8,128)} %bitcast.43), custom_call_target="tpu_custom_call" | custom-call | tf_op jit(solution)/shard_map/pallas_call | solution.py:68
  187.3 1.4 copy.14
  188.7 0.2 reshape.122
  189.0 0.8 fusion.15
  (16 shorter events, 0.1 us)
Async XLA Ops:
  6.5 137.3 %copy-start = (s32[8,2]{0,1:T(2,128)S(1)}, s32[8,2]{0,1:T(2,128)}, u32[]{:S(2)}) copy-start(s32[8,2]{0,1:T(2,128)} %param.13) | copy-start | bytes 196
  6.5 93.0 %all-gather.3.cloned.1.call-start = ((), (), s32[]{:S(2)}) async-start(), calls=%async_computation.2 | async-start | bytes 2162688 | tf_op jit(solution)/shard_map/all_gather | solution.py:102
  8.1 4.3 %collective-permute-start = (bf16[32,1024]{1,0:T(8,128)(2,1)S(1)}, bf16[32,1024]{1,0:T(8,128)(2,1)S(1)}, u32[]{:S(2)}, u32[]{:S(2)}) collective-permute-start(bf16[32,1024]{1,0:T(8,128)(2,1)S(1)} %get-tuple-element.11), channel_id=1, source_target_pairs={{64,0},{96,32},{0,64},{32,96},{65,1},{97,33},{1,65},{33,97},{66,2}... | collective-permute-start | bytes 196616 | tf_op jit(solution)/shard_map/ppermute | solution.py:14
  14.0 105.8 %all-to-all-start = ((bf16[32,32,1024]{2,1,0:T(8,128)(2,1)}), bf16[32,32,1024]{2,1,0:T(8,128)(2,1)S(1)}, u32[]{:S(2)}, u32[]{:S(2)}) async-start(bf16[32,32,1024]{2,1,0:T(8,128)(2,1)} %broadcast_in_dim.56), calls=%async_computation | async-start | bytes 4194304 | tf_op jit(solution)/shard_map/all_to_all | solution.py:95
  138.9 4.8 %copy-start.2 = (f32[1024]{0:T(1024)S(1)}, f32[1024]{0:T(1024)}, u32[]{:S(2)}) copy-start(f32[1024]{0:T(1024)} %param.10) | copy-start | bytes 12292
  138.9 4.9 %copy-start.1 = (s32[1024]{0:T(1024)S(1)}, s32[1024]{0:T(1024)}, u32[]{:S(2)}) copy-start(s32[1024]{0:T(1024)} %param.12) | copy-start | bytes 12292
  138.9 5.1 %copy-start.3 = (f32[100]{0:T(128)S(1)}, f32[100]{0:T(128)}, u32[]{:S(2)}) copy-start(f32[100]{0:T(128)} %param.9) | copy-start | bytes 1204
  138.9 5.3 %copy-start.4 = (s32[100]{0:T(128)S(1)}, s32[100]{0:T(128)}, u32[]{:S(2)}) copy-start(s32[100]{0:T(128)} %param.11) | copy-start | bytes 1204
  138.9 35.0 %all-to-all-start.1 = ((bf16[32,32,1024]{2,1,0:T(8,128)(2,1)}), bf16[32,32,1024]{2,1,0:T(8,128)(2,1)S(1)}, u32[]{:S(2)}, u32[]{:S(2)}) async-start(bf16[32,32,1024]{2,1,0:T(8,128)(2,1)} %bitcast.44), calls=%async_computation.1 | async-start | bytes 4194304 | tf_op jit(solution)/shard_map/all_to_all | solution.py:108
Sparse Core Ops, SparseCore 0:
  10.3 89.1 all-gather.2

commit v12 on v10

--- a/solution.py
+++ b/solution.py
@@ -14,66 +14,126 @@
     return lax.ppermute(block, axis, route)
 
 
-def _turn_kernel(n, blocks_ref, out_ref, send_sems, recv_sems):
+def _scatter_turn_kernel(n, parts_ref, own_ref, turned_ref, slots, flipped, sems):
     me = lax.axis_index("vir")
     group = lax.axis_index("occ")
     partner = lax.rem(group + lax.axis_size("occ") // 2, lax.axis_size("occ"))
+    rs_send, rs_recv, local_sem, t_send, t_recv = sems
+    rows = own_ref.shape[0]
 
     barrier = pltpu.get_barrier_semaphore()
 
     def greet(k, carry):
         pl.semaphore_signal(barrier, inc=1, device_id=(partner, k), device_id_type=pl.DeviceIdType.MESH)
+
+        @pl.when(k != me)
+        def _():
+            pl.semaphore_signal(barrier, inc=1, device_id=(group, k), device_id_type=pl.DeviceIdType.MESH)
+
         return carry
 
     lax.fori_loop(0, n, greet, 0)
-    pl.semaphore_wait(barrier, n)
-
-    def copy_to(k):
-        dest = lax.rem(me + k, n)
+    pl.semaphore_wait(barrier, 2 * n - 1)
+
+    def part_copy(dest):
         return pltpu.make_async_remote_copy(
-            src_ref=blocks_ref.at[dest],
-            dst_ref=out_ref.at[me],
-            send_sem=send_sems.at[dest],
-            recv_sem=recv_sems.at[me],
-            device_id=(partner, dest),
+            src_ref=parts_ref.at[dest],
+            dst_ref=slots.at[me],
+            send_sem=rs_send.at[dest],
+            recv_sem=rs_recv.at[me],
+            device_id=(group, dest),
             device_id_type=pl.DeviceIdType.MESH,
         )
 
+    local = pltpu.make_async_copy(parts_ref.at[me], slots.at[me], local_sem)
+    local.start()
+
     def send(k, carry):
-        copy_to(k).start()
-        return carry
-
-    lax.fori_loop(0, n, send, 0)
-
-    def finish(k, carry):
-        copy_to(k).wait_send()
+        part_copy(lax.rem(me + k, n)).start()
+        return carry
+
+    lax.fori_loop(1, n, send, 0)
+
+    def settle(k, carry):
+        part_copy(lax.rem(me + k, n)).wait_send()
         source = lax.rem(me + n - k, n)
         pltpu.make_async_remote_copy(
-            src_ref=blocks_ref.at[source],
-            dst_ref=out_ref.at[source],
-            send_sem=send_sems.at[source],
-            recv_sem=recv_sems.at[source],
-            device_id=(partner, source),
+            src_ref=parts_ref.at[source],
+            dst_ref=slots.at[source],
+            send_sem=rs_send.at[source],
+            recv_sem=rs_recv.at[source],
+            device_id=(group, source),
             device_id_type=pl.DeviceIdType.MESH,
         ).wait_recv()
         return carry
 
+    lax.fori_loop(1, n, settle, 0)
+    local.wait()
+
+    def accumulate(w, total):
+        return total + slots[w].astype(jnp.float32)
+
+    total = lax.fori_loop(0, n, accumulate, jnp.zeros(own_ref.shape, jnp.float32))
+    own_ref[...] = total
+    flipped[...] = jnp.transpose(total, (1, 0))
+
+    def turn_copy(dest):
+        return pltpu.make_async_remote_copy(
+            src_ref=flipped.at[pl.ds(pl.multiple_of(dest * rows, rows), rows)],
+            dst_ref=turned_ref.at[me],
+            send_sem=t_send.at[dest],
+            recv_sem=t_recv.at[me],
+            device_id=(partner, dest),
+            device_id_type=pl.DeviceIdType.MESH,
+        )
+
+    def turn(k, carry):
+        turn_copy(k).start()
+        return carry
+
+    lax.fori_loop(0, n, turn, 0)
+
+    def finish(k, carry):
+        turn_copy(k).wait_send()
+        pltpu.make_async_remote_copy(
+            src_ref=flipped.at[pl.ds(pl.multiple_of(k * rows, rows), rows)],
+            dst_ref=turned_ref.at[k],
+            send_sem=t_send.at[k],
+            recv_sem=t_recv.at[k],
+            device_id=(partner, k),
+            device_id_type=pl.DeviceIdType.MESH,
+        ).wait_recv()
+        return carry
+
     lax.fori_loop(0, n, finish, 0)
 
 
-def partner_transpose(own_rows, vir_axis):
+def scatter_and_turn(parts, vir_axis):
     n = lax.axis_size(vir_axis)
-    rows, width = own_rows.shape
-    blocks = jnp.transpose(own_rows.reshape(rows, n, width // n), (1, 2, 0))
-    arrived = pl.pallas_call(
-        functools.partial(_turn_kernel, n),
-        out_shape=jax.ShapeDtypeStruct(blocks.shape, blocks.dtype),
+    rows, width = parts.shape[1], parts.shape[2]
+    own_rows, arrived = pl.pallas_call(
+        functools.partial(_scatter_turn_kernel, n),
+        out_shape=(
+            jax.ShapeDtypeStruct((rows, width), jnp.float32),
+            jax.ShapeDtypeStruct((n, rows, rows), jnp.float32),
+        ),
         in_specs=[pl.BlockSpec(memory_space=pl.ANY)],
-        out_specs=pl.BlockSpec(memory_space=pl.ANY),
-        scratch_shapes=[pltpu.SemaphoreType.DMA((n,)), pltpu.SemaphoreType.DMA((n,))],
+        out_specs=(pl.BlockSpec(memory_space=pltpu.VMEM), pl.BlockSpec(memory_space=pl.ANY)),
+        scratch_shapes=[
+            pltpu.VMEM((n, rows, width), parts.dtype),
+            pltpu.VMEM((width, rows), jnp.float32),
+            (
+                pltpu.SemaphoreType.DMA((n,)),
+                pltpu.SemaphoreType.DMA((n,)),
+                pltpu.SemaphoreType.DMA,
+                pltpu.SemaphoreType.DMA((n,)),
+                pltpu.SemaphoreType.DMA((n,)),
+            ),
+        ],
         compiler_params=pltpu.CompilerParams(collective_id=1, has_side_effects=True),
-    )(blocks)
-    return jnp.transpose(arrived, (1, 0, 2)).reshape(width // n, n * rows)
+    )(parts)
+    partner_cols = jnp.transpose(arrived, (1, 0, 2)).reshape(rows, n * rows)
+    return own_rows, partner_cols
 
 
 def per_device(amplitudes, factors, occ_energy, vir_energy, occ_irrep, vir_irrep, pair_orbitals):
@@ -106,9 +166,7 @@
     turned_term = jnp.einsum("qac,qbc->ab", halves_second, factors, preferred_element_type=jnp.float32)
     combined = direct + turned_term
     blocks = combined.reshape(vir_devices, row_count, combined.shape[-1]).astype(jnp.bfloat16)
-    arrived = lax.all_to_all(blocks, "vir", split_axis=0, concat_axis=0, tiled=True)
-    own_rows = jnp.sum(arrived.astype(jnp.float32), axis=0)
-    partner_cols = partner_transpose(own_rows, "vir")
+    own_rows, partner_cols = scatter_and_turn(blocks, "vir")
     first_out = jnp.where(lower_half, own_rows, partner_cols)
     second_out = jnp.where(lower_half, partner_cols, own_rows)
     summed_pair = jnp.stack([first_out, second_out], axis=0)

time: 150 us -> 153 us (1.020)
  blocking collectives: 40.2 us -> 0 us
  Pallas kernels: 12.1 us -> 44.9 us
  starting transfers between devices: 9.91 us -> 17.4 us
    all_to_all x1 -> x0, blocking collectives: 40.2 us -> none  [gather_rows(): lax.all_to_all(spread, 'vir', split_axis=0, concat_axis=0, tiled=True)]
    pallas_call x1, Pallas kernels: 12.1 us -> 44.9 us  [scatter_and_turn(): pl.pallas_call(functools.partial(_scatter_turn_kernel, n), out_shape=(jax...]
    all_to_all x1 -> x2, waiting for transfers between devices: 8.81 us -> 39.8 us  [gather_rows(): lax.all_to_all(spread, 'vir', split_axis=0, concat_axis=0, tiled=True)]
    all_to_all x1 -> x0, waiting for transfers between devices: 29.7 us -> none  [per_device(): lax.all_to_all(blocks, 'vir', split_axis=0, concat_axis=0, tiled=True)]
    all_to_all x1 -> x2, starting transfers between devices: 4.01 us -> 15.7 us  [gather_rows(): lax.all_to_all(spread, 'vir', split_axis=0, concat_axis=0, tiled=True)]
    all_to_all x1 -> x0, starting transfers between devices: 4.15 us -> none  [per_device(): lax.all_to_all(blocks, 'vir', split_axis=0, concat_axis=0, tiled=True)]
  transfers between devices with their start and end apart: 3 -> 3, of which waited for: 3 -> 3; matrix products, arithmetic and copies ran while one was open for 14% -> 13% of each run, Pallas kernels for 0% -> 0%
where the time goes in v12:
time: 153 us; the launch traced here: 152 us
  Pallas kernels  44.9 us (29%)
  waiting for transfers between devices  42.4 us (28%)
  matrix products  39.1 us (26%)
  starting transfers between devices  17.4 us (11%)
  local copies, waits for them, and re-layouts  5.01 us (3%)
  other arithmetic  3.25 us (2%)
    pallas_call x1, Pallas kernels, scatter_and_turn(): pl.pallas_call(functools.partial(_scatter_turn_kernel, n), out_shape=(jax...  44.9 us
    all_to_all x2, waiting for transfers between devices, gather_rows(): lax.all_to_all(spread, 'vir', split_axis=0, concat_axis=0, tiled=True)  39.8 us
    dot_general x1, matrix products, per_device(): jnp.einsum('qac,qbc->ab', factors, halves_first, preferred_element_type=j...  19.7 us
    dot_general x1, matrix products, per_device(): jnp.einsum('qac,qbc->ab', halves_second, factors, preferred_element_type=...  19.4 us
    all_to_all x2, starting transfers between devices, gather_rows(): lax.all_to_all(spread, 'vir', split_axis=0, concat_axis=0, tiled=True)  15.7 us
    broadcast_in_dim x2, local copies, waits for them, and re-layouts, gather_rows(): spread = jnp.broadcast_to(block[None], (vir_devices,) + block.shape)  3.18 us
  transfers between devices with their start and end apart: 3, of which 3 were waited for; matrix products, arithmetic and copies ran while one was open for 13% of the time, Pallas kernels for 0%

profile of v12, /device:TPU:0, one launch (start us, length us, event | category | flops | bytes accessed | tf_op | source)
XLA Modules:
  0.0 152.2 jit_solution(11970905397565446613)
XLA Ops:
  0.0 0.0 copy-start
  0.0 0.9 select_bitcast_fusion.2
  0.9 1.7 %collective-permute-start = (bf16[32,1024]{1,0:T(8,128)(2,1)S(1)}, bf16[32,1024]{1,0:T(8,128)(2,1)S(1)}, u32[]{:S(2)}, u32[]{:S(2)}) collective-permute-start(bf16[32,1024]{1,0:T(8,128)(2,1)S(1)} %get-tuple-element.19), channel_id=1, source_target_pairs={{64,0},{96,32},{0,64},{32,96},{65,1},{97,33},{1,65},{33,97},{66,2}... | collective-permute-start | bytes 196616 | tf_op jit(solution)/shard_map/ppermute | solution.py:14
  2.7 2.6 %collective-permute-done = bf16[32,1024]{1,0:T(8,128)(2,1)S(1)} collective-permute-done((bf16[32,1024]{1,0:T(8,128)(2,1)S(1)}, bf16[32,1024]{1,0:T(8,128)(2,1)S(1)}, u32[]{:S(2)}, u32[]{:S(2)}) %collective-permute-start) | collective-permute-done | bytes 65568 | tf_op jit(solution)/shard_map/ppermute | solution.py:14
  5.3 1.6 %broadcast_in_dim.62 = bf16[32,32,1024]{2,1,0:T(8,128)(2,1)} broadcast(bf16[32,1024]{1,0:T(8,128)(2,1)S(1)} %get-tuple-element.9), dimensions={1,2} | broadcast | bytes 2162688 | tf_op jit(solution)/shard_map/broadcast_in_dim | solution.py:155
  6.9 10.9 %all-to-all-start = ((bf16[32,32,1024]{2,1,0:T(8,128)(2,1)}), bf16[32,32,1024]{2,1,0:T(8,128)(2,1)S(1)}, u32[]{:S(2)}, u32[]{:S(2)}) async-start(bf16[32,32,1024]{2,1,0:T(8,128)(2,1)} %broadcast_in_dim.62), calls=%async_computation | async-start | bytes 4194304 | tf_op jit(solution)/shard_map/all_to_all | solution.py:156
  17.8 0.1 dynamic_slice.11
  17.8 0.1 dynamic_slice.10
  17.9 0.1 constant_dynamic-slice_fusion
  18.0 0.2 select_reduce_fusion
  18.2 0.2 select_reduce_fusion.2
  18.5 0.1 broadcast_xor_fusion
  18.5 0.1 broadcast_add_fusion
  18.6 29.5 %all-to-all-done = bf16[32,32,1024]{2,1,0:T(8,128)(2,1)S(1)} async-done(((bf16[32,32,1024]{2,1,0:T(8,128)(2,1)}), bf16[32,32,1024]{2,1,0:T(8,128)(2,1)S(1)}, u32[]{:S(2)}, u32[]{:S(2)}) %all-to-all-start) | async-done | bytes 2097184 | tf_op jit(solution)/shard_map/all_to_all | solution.py:156
  48.2 1.6 %broadcast_in_dim.63 = bf16[32,32,1024]{2,1,0:T(8,128)(2,1)} broadcast(bf16[32,1024]{1,0:T(8,128)(2,1)S(1)} %collective-permute-done), dimensions={1,2} | broadcast | bytes 2162688 | tf_op jit(solution)/shard_map/broadcast_in_dim | solution.py:155
  49.7 4.8 %all-to-all-start.1 = ((bf16[32,32,1024]{2,1,0:T(8,128)(2,1)}), bf16[32,32,1024]{2,1,0:T(8,128)(2,1)}, u32[]{:S(2)}, u32[]{:S(2)}) async-start(bf16[32,32,1024]{2,1,0:T(8,128)(2,1)} %broadcast_in_dim.63), calls=%async_computation.1 | async-start | bytes 4194304 | tf_op jit(solution)/shard_map/all_to_all | solution.py:156
  54.5 19.7 %fusion.2 = f32[1024,1024,1]{0,1,2:T(8,128)} fusion(bf16[3,1024,1024]{2,1,0:T(8,128)(2,1)} %param.8, bf16[1024,1024,1]{1,0,2:T(8,128)(2,1)S(1)} %bitcast.42), kind=kOutput, calls=%fused_computation.2 | convolution fusion | flops 12888047616 | bytes 12582912 | tf_op jit(solution)/shard_map/qac,qbc->ab/dot_general | solution.py:165
  74.3 10.3 %all-to-all-done.1 = bf16[32,32,1024]{2,1,0:T(8,128)(2,1)} async-done(((bf16[32,32,1024]{2,1,0:T(8,128)(2,1)}), bf16[32,32,1024]{2,1,0:T(8,128)(2,1)}, u32[]{:S(2)}, u32[]{:S(2)}) %all-to-all-start.1) | async-done | bytes 2097184 | tf_op jit(solution)/shard_map/all_to_all | solution.py:156
  84.6 19.4 %fusion.6 = bf16[1024,1024]{1,0:T(8,128)(2,1)} fusion(f32[1024,1024,1]{0,1,2:T(8,128)} %fusion.2, bf16[3,1024,1024]{2,1,0:T(8,128)(2,1)} %param.8, bf16[1024,1024,1]{1,0,2:T(8,128)(2,1)} %bitcast.10), kind=kOutput, calls=%fused_computation.7 | convolution fusion | flops 12890144768 | bytes 14680064 | tf_op jit(solution)/shard_map/qac,qbc->ab/dot_general | solution.py:166
  104.0 44.9 %shard_map.73 = (f32[32,1024]{1,0:T(8,128)}, f32[32,32,32]{2,1,0:T(8,128)}) custom-call(bf16[32,32,1024]{2,1,0:T(8,128)(2,1)} %bitcast.43), custom_call_target="tpu_custom_call" | custom-call | tf_op jit(solution)/shard_map/pallas_call | solution.py:114
  148.9 1.4 copy.11
  150.2 0.2 reshape.95
  150.4 0.9 select_bitcast_fusion.1
  151.4 0.8 fusion.13
  (12 shorter events, 0.0 us)
Async XLA Ops:
  0.0 17.9 %copy-start = (s32[8,2]{0,1:T(2,128)S(1)}, s32[8,2]{0,1:T(2,128)}, u32[]{:S(2)}) copy-start(s32[8,2]{0,1:T(2,128)} %param.13) | copy-start | bytes 196
  0.0 17.8 %copy-start.2 = (f32[1024]{0:T(1024)S(1)}, f32[1024]{0:T(1024)}, u32[]{:S(2)}) copy-start(f32[1024]{0:T(1024)} %param.10) | copy-start | bytes 12292
  0.0 17.8 %copy-start.1 = (s32[1024]{0:T(1024)S(1)}, s32[1024]{0:T(1024)}, u32[]{:S(2)}) copy-start(s32[1024]{0:T(1024)} %param.12) | copy-start | bytes 12292
  0.0 18.0 %copy-start.3 = (f32[100]{0:T(128)S(1)}, f32[100]{0:T(128)}, u32[]{:S(2)}) copy-start(f32[100]{0:T(128)} %param.9) | copy-start | bytes 1204
  0.0 18.2 %copy-start.4 = (s32[100]{0:T(128)S(1)}, s32[100]{0:T(128)}, u32[]{:S(2)}) copy-start(s32[100]{0:T(128)} %param.11) | copy-start | bytes 1204
  0.9 4.3 %collective-permute-start = (bf16[32,1024]{1,0:T(8,128)(2,1)S(1)}, bf16[32,1024]{1,0:T(8,128)(2,1)S(1)}, u32[]{:S(2)}, u32[]{:S(2)}) collective-permute-start(bf16[32,1024]{1,0:T(8,128)(2,1)S(1)} %get-tuple-element.19), channel_id=1, source_target_pairs={{64,0},{96,32},{0,64},{32,96},{65,1},{97,33},{1,65},{33,97},{66,2}... | collective-permute-start | bytes 196616 | tf_op jit(solution)/shard_map/ppermute | solution.py:14
  6.9 41.3 %all-to-all-start = ((bf16[32,32,1024]{2,1,0:T(8,128)(2,1)}), bf16[32,32,1024]{2,1,0:T(8,128)(2,1)S(1)}, u32[]{:S(2)}, u32[]{:S(2)}) async-start(bf16[32,32,1024]{2,1,0:T(8,128)(2,1)} %broadcast_in_dim.62), calls=%async_computation | async-start | bytes 4194304 | tf_op jit(solution)/shard_map/all_to_all | solution.py:156
  49.7 34.8 %all-to-all-start.1 = ((bf16[32,32,1024]{2,1,0:T(8,128)(2,1)}), bf16[32,32,1024]{2,1,0:T(8,128)(2,1)}, u32[]{:S(2)}, u32[]{:S(2)}) async-start(bf16[32,32,1024]{2,1,0:T(8,128)(2,1)} %broadcast_in_dim.63), calls=%async_computation.1 | async-start | bytes 4194304 | tf_op jit(solution)/shard_map/all_to_all | solution.py:156

commit v13 on v10

--- a/solution.py
+++ b/solution.py
@@ -89,7 +89,6 @@
     own = jnp.where(lower_half, amplitudes[0], amplitudes[1])
     outgoing = jnp.where(lower_half, amplitudes[1], amplitudes[0])
     other = passed_along(outgoing, "occ", occ_devices // 2)
-    own, other = lax.optimization_barrier((own, other))
 
     def gather_rows(block):
         spread = jnp.broadcast_to(block[None], (vir_devices,) + block.shape)

time: 150 us -> 155 us (1.033)
  blocking collectives: 40.2 us -> 0 us
  waiting for transfers between devices: 41.1 us -> 73 us
  starting transfers between devices: 9.91 us -> 21.3 us
    all_to_all x1 -> x0, blocking collectives: 40.2 us -> none  [gather_rows(): lax.all_to_all(spread, 'vir', split_axis=0, concat_axis=0, tiled=True)]
    all_to_all x1 -> x2, waiting for transfers between devices: 8.81 us -> 28.2 us  [gather_rows(): lax.all_to_all(spread, 'vir', split_axis=0, concat_axis=0, tiled=True)]
    ppermute x1, waiting for transfers between devices: 2.61 us -> 15.1 us  [passed_along(): return lax.ppermute(block, axis, route)]
    all_to_all x1 -> x2, starting transfers between devices: 4.01 us -> 16.4 us  [gather_rows(): lax.all_to_all(spread, 'vir', split_axis=0, concat_axis=0, tiled=True)]
  transfers between devices with their start and end apart: 3 -> 4, of which waited for: 3 -> 4; matrix products, arithmetic and copies ran while one was open for 14% -> 13% of each run, Pallas kernels for 0% -> 0%
where the time goes in v13:
time: 155 us; the launch traced here: 154 us
  waiting for transfers between devices  73 us (47%)
  matrix products  39.1 us (25%)
  starting transfers between devices  21.3 us (14%)
  Pallas kernels  12.1 us (8%)
  local copies, waits for them, and re-layouts  6.04 us (4%)
  other arithmetic  2.71 us (2%)
    all_to_all x1, waiting for transfers between devices, per_device(): lax.all_to_all(blocks, 'vir', split_axis=0, concat_axis=0, tiled=True)  29.7 us
    all_to_all x2, waiting for transfers between devices, gather_rows(): lax.all_to_all(spread, 'vir', split_axis=0, concat_axis=0, tiled=True)  28.2 us
    dot_general x1, matrix products, per_device(): jnp.einsum('qac,qbc->ab', factors, halves_first, preferred_element_type=j...  19.7 us
    dot_general x1, matrix products, per_device(): jnp.einsum('qac,qbc->ab', halves_second, factors, preferred_element_type=...  19.4 us
    all_to_all x2, starting transfers between devices, gather_rows(): lax.all_to_all(spread, 'vir', split_axis=0, concat_axis=0, tiled=True)  16.4 us
    ppermute x1, waiting for transfers between devices, passed_along(): return lax.ppermute(block, axis, route)  15.1 us
    pallas_call x1, Pallas kernels, partner_transpose(): pl.pallas_call(functools.partial(_turn_kernel, n), out_shape=jax.ShapeDty...  12.1 us
    all_to_all x1, starting transfers between devices, per_device(): lax.all_to_all(blocks, 'vir', split_axis=0, concat_axis=0, tiled=True)  4.16 us
  transfers between devices with their start and end apart: 4, of which 4 were waited for; matrix products, arithmetic and copies ran while one was open for 13% of the time, Pallas kernels for 0%

profile of v13, /device:TPU:0, one launch (start us, length us, event | category | flops | bytes accessed | tf_op | source)
XLA Modules:
  0.0 154.3 jit_solution(8365747179894356073)
XLA Ops:
  0.0 0.9 select_bitcast_fusion
  0.9 1.6 %broadcast_in_dim.65 = bf16[32,32,1024]{2,1,0:T(8,128)(2,1)} broadcast(bf16[32,1024]{1,0:T(8,128)(2,1)S(1)} %get-tuple-element.12), dimensions={1,2} | broadcast | bytes 2162688 | tf_op jit(solution)/shard_map/broadcast_in_dim | solution.py:94
  2.5 10.9 %all-to-all-start = ((bf16[32,32,1024]{2,1,0:T(8,128)(2,1)}), bf16[32,32,1024]{2,1,0:T(8,128)(2,1)S(1)}, u32[]{:S(2)}, u32[]{:S(2)}) async-start(bf16[32,32,1024]{2,1,0:T(8,128)(2,1)} %broadcast_in_dim.65), calls=%async_computation | async-start | bytes 4194304 | tf_op jit(solution)/shard_map/all_to_all | solution.py:95
  13.4 0.8 collective-permute-start
  14.1 15.1 %collective-permute-done = bf16[32,1024]{1,0:T(8,128)(2,1)S(1)} collective-permute-done((bf16[32,1024]{1,0:T(8,128)(2,1)S(1)}, bf16[32,1024]{1,0:T(8,128)(2,1)S(1)}, u32[]{:S(2)}, u32[]{:S(2)}) %collective-permute-start) | collective-permute-done | bytes 65568 | tf_op jit(solution)/shard_map/ppermute | solution.py:14
  29.2 16.1 %all-to-all-done = bf16[32,32,1024]{2,1,0:T(8,128)(2,1)S(1)} async-done(((bf16[32,32,1024]{2,1,0:T(8,128)(2,1)}), bf16[32,32,1024]{2,1,0:T(8,128)(2,1)S(1)}, u32[]{:S(2)}, u32[]{:S(2)}) %all-to-all-start) | async-done | bytes 2097184 | tf_op jit(solution)/shard_map/all_to_all | solution.py:95
  45.3 1.6 %broadcast_in_dim.66 = bf16[32,32,1024]{2,1,0:T(8,128)(2,1)} broadcast(bf16[32,1024]{1,0:T(8,128)(2,1)S(1)} %collective-permute-done), dimensions={1,2} | broadcast | bytes 2162688 | tf_op jit(solution)/shard_map/broadcast_in_dim | solution.py:94
  46.9 5.5 %all-to-all-start.1 = ((bf16[32,32,1024]{2,1,0:T(8,128)(2,1)}), bf16[32,32,1024]{2,1,0:T(8,128)(2,1)}, u32[]{:S(2)}, u32[]{:S(2)}) async-start(bf16[32,32,1024]{2,1,0:T(8,128)(2,1)} %broadcast_in_dim.66), calls=%async_computation.1 | async-start | bytes 4194304 | tf_op jit(solution)/shard_map/all_to_all | solution.py:95
  52.4 19.7 %fusion.2 = f32[1024,1024,1]{0,1,2:T(8,128)} fusion(bf16[3,1024,1024]{2,1,0:T(8,128)(2,1)} %param.8, bf16[1024,1024,1]{1,0,2:T(8,128)(2,1)S(1)} %bitcast.46), kind=kOutput, calls=%fused_computation.2 | convolution fusion | flops 12888047616 | bytes 12582912 | tf_op jit(solution)/shard_map/qac,qbc->ab/dot_general | solution.py:104
  72.1 12.1 %all-to-all-done.1 = bf16[32,32,1024]{2,1,0:T(8,128)(2,1)} async-done(((bf16[32,32,1024]{2,1,0:T(8,128)(2,1)}), bf16[32,32,1024]{2,1,0:T(8,128)(2,1)}, u32[]{:S(2)}, u32[]{:S(2)}) %all-to-all-start.1) | async-done | bytes 2097184 | tf_op jit(solution)/shard_map/all_to_all | solution.py:95
  84.3 19.4 %fusion.6 = bf16[1024,1024]{1,0:T(8,128)(2,1)} fusion(f32[1024,1024,1]{0,1,2:T(8,128)} %fusion.2, bf16[3,1024,1024]{2,1,0:T(8,128)(2,1)} %param.8, bf16[1024,1024,1]{1,0,2:T(8,128)(2,1)} %bitcast.10), kind=kOutput, calls=%fused_computation.7 | convolution fusion | flops 12890144768 | bytes 14680064 | tf_op jit(solution)/shard_map/qac,qbc->ab/dot_general | solution.py:105
  103.7 4.2 %all-to-all-start.2 = ((bf16[32,32,1024]{2,1,0:T(8,128)(2,1)}), bf16[32,32,1024]{2,1,0:T(8,128)(2,1)S(1)}, u32[]{:S(2)}, u32[]{:S(2)}) async-start(bf16[32,32,1024]{2,1,0:T(8,128)(2,1)} %bitcast.45), calls=%async_computation.2 | async-start | bytes 4194304 | tf_op jit(solution)/shard_map/all_to_all | solution.py:108
  107.8 0.1 dynamic_slice.11
  107.9 0.1 dynamic_slice.10
  108.1 0.2 select_reduce_fusion
  108.3 0.2 select_reduce_fusion.2
  108.6 0.1 broadcast_add_fusion
  108.7 29.7 %all-to-all-done.2 = bf16[32,32,1024]{2,1,0:T(8,128)(2,1)S(1)} async-done(((bf16[32,32,1024]{2,1,0:T(8,128)(2,1)}), bf16[32,32,1024]{2,1,0:T(8,128)(2,1)S(1)}, u32[]{:S(2)}, u32[]{:S(2)}) %all-to-all-start.2) | async-done | bytes 2097184 | tf_op jit(solution)/shard_map/all_to_all | solution.py:108
  138.4 0.4 convert_reduce_fusion
  138.8 1.0 copy.13
  139.8 12.1 %shard_map.73 = f32[32,32,32]{2,1,0:T(8,128)} custom-call(f32[32,32,32]{2,1,0:T(8,128)} %bitcast.44), custom_call_target="tpu_custom_call" | custom-call | tf_op jit(solution)/shard_map/pallas_call | solution.py:68
  151.9 1.4 copy.14
  153.2 0.2 reshape.124
  153.5 0.8 fusion.13
  (16 shorter events, 0.2 us)
Async XLA Ops:
  0.0 108.0 %copy-start = (s32[8,2]{0,1:T(2,128)S(1)}, s32[8,2]{0,1:T(2,128)}, u32[]{:S(2)}) copy-start(s32[8,2]{0,1:T(2,128)} %param.13) | copy-start | bytes 196
  2.5 42.8 %all-to-all-start = ((bf16[32,32,1024]{2,1,0:T(8,128)(2,1)}), bf16[32,32,1024]{2,1,0:T(8,128)(2,1)S(1)}, u32[]{:S(2)}, u32[]{:S(2)}) async-start(bf16[32,32,1024]{2,1,0:T(8,128)(2,1)} %broadcast_in_dim.65), calls=%async_computation | async-start | bytes 4194304 | tf_op jit(solution)/shard_map/all_to_all | solution.py:95
  13.4 15.8 %collective-permute-start = (bf16[32,1024]{1,0:T(8,128)(2,1)S(1)}, bf16[32,1024]{1,0:T(8,128)(2,1)S(1)}, u32[]{:S(2)}, u32[]{:S(2)}) collective-permute-start(bf16[32,1024]{1,0:T(8,128)(2,1)S(1)} %get-tuple-element.11), channel_id=1, source_target_pairs={{64,0},{96,32},{0,64},{32,96},{65,1},{97,33},{1,65},{33,97},{66,2}... | collective-permute-start | bytes 196616 | tf_op jit(solution)/shard_map/ppermute | solution.py:14
  46.9 37.3 %all-to-all-start.1 = ((bf16[32,32,1024]{2,1,0:T(8,128)(2,1)}), bf16[32,32,1024]{2,1,0:T(8,128)(2,1)}, u32[]{:S(2)}, u32[]{:S(2)}) async-start(bf16[32,32,1024]{2,1,0:T(8,128)(2,1)} %broadcast_in_dim.66), calls=%async_computation.1 | async-start | bytes 4194304 | tf_op jit(solution)/shard_map/all_to_all | solution.py:95
  103.6 4.2 %copy-start.2 = (f32[1024]{0:T(1024)S(1)}, f32[1024]{0:T(1024)}, u32[]{:S(2)}) copy-start(f32[1024]{0:T(1024)} %param.10) | copy-start | bytes 12292
  103.6 4.3 %copy-start.1 = (s32[1024]{0:T(1024)S(1)}, s32[1024]{0:T(1024)}, u32[]{:S(2)}) copy-start(s32[1024]{0:T(1024)} %param.12) | copy-start | bytes 12292
  103.6 4.4 %copy-start.3 = (f32[100]{0:T(128)S(1)}, f32[100]{0:T(128)}, u32[]{:S(2)}) copy-start(f32[100]{0:T(128)} %param.9) | copy-start | bytes 1204
  103.7 4.7 %copy-start.4 = (s32[100]{0:T(128)S(1)}, s32[100]{0:T(128)}, u32[]{:S(2)}) copy-start(s32[100]{0:T(128)} %param.11) | copy-start | bytes 1204
  103.7 34.7 %all-to-all-start.2 = ((bf16[32,32,1024]{2,1,0:T(8,128)(2,1)}), bf16[32,32,1024]{2,1,0:T(8,128)(2,1)S(1)}, u32[]{:S(2)}, u32[]{:S(2)}) async-start(bf16[32,32,1024]{2,1,0:T(8,128)(2,1)} %bitcast.45), calls=%async_computation.2 | async-start | bytes 4194304 | tf_op jit(solution)/shard_map/all_to_all | solution.py:108

commit v14 on v10

--- a/solution.py
+++ b/solution.py
@@ -12,6 +12,90 @@
     devices = range(lax.axis_size(axis))
     route = [((i - distance) % len(devices), i) for i in devices]
     return lax.ppermute(block, axis, route)
+
+
+def _exchange_kernel(layout, *refs):
+    count = len(layout)
+    sources, targets = refs[:count], refs[count:2 * count]
+    send_sems, recv_sems = refs[2 * count:3 * count], refs[3 * count:4 * count]
+    local_sems = refs[4 * count]
+    me = lax.axis_index("vir")
+    group = lax.axis_index("occ")
+
+    def peer_of(mine, coord, stride):
+        return me + (coord - mine) * stride
+
+    barrier = pltpu.get_barrier_semaphore()
+    greetings = 0
+    coords = []
+    for stride, size, shared in layout:
+        mine = lax.rem(lax.div(me, stride), size)
+        coords.append(mine)
+        for step in range(1, size):
+            coord = lax.rem(mine + step, size)
+            pl.semaphore_signal(
+                barrier, inc=1, device_id=(group, peer_of(mine, coord, stride)),
+                device_id_type=pl.DeviceIdType.MESH,
+            )
+            greetings += 1
+    pl.semaphore_wait(barrier, greetings)
+
+    def remote(part, coord, slot):
+        stride, size, shared = layout[part]
+        mine = coords[part]
+        source = sources[part] if shared else sources[part].at[coord]
+        return pltpu.make_async_remote_copy(
+            src_ref=source,
+            dst_ref=targets[part].at[slot],
+            send_sem=send_sems[part].at[coord],
+            recv_sem=recv_sems[part].at[slot],
+            device_id=(group, peer_of(mine, coord, stride)),
+            device_id_type=pl.DeviceIdType.MESH,
+        )
+
+    locals_ = []
+    for part, (stride, size, shared) in enumerate(layout):
+        mine = coords[part]
+        source = sources[part] if shared else sources[part].at[mine]
+        local = pltpu.make_async_copy(source, targets[part].at[mine], local_sems.at[part])
+        local.start()
+        locals_.append(local)
+        for step in range(1, size):
+            remote(part, lax.rem(mine + step, size), mine).start()
+    for part, (stride, size, shared) in enumerate(layout):
+        mine = coords[part]
+        for step in range(1, size):
+            remote(part, lax.rem(mine + step, size), mine).wait_send()
+            origin = lax.rem(mine + size - step, size)
+            stride_ = stride
+            pltpu.make_async_remote_copy(
+                src_ref=sources[part] if shared else sources[part].at[origin],
+                dst_ref=targets[part].at[origin],
+                send_sem=send_sems[part].at[origin],
+                recv_sem=recv_sems[part].at[origin],
+                device_id=(group, peer_of(mine, origin, stride_)),
+                device_id_type=pl.DeviceIdType.MESH,
+            ).wait_recv()
+        locals_[part].wait()
+
+
+def exchange(parts, collective_id):
+    layout = tuple((stride, size, shared) for _, stride, size, shared in parts)
+    shapes = []
+    for array, stride, size, shared in parts:
+        block = array.shape if shared else array.shape[1:]
+        shapes.append(jax.ShapeDtypeStruct((size,) + tuple(block), array.dtype))
+    scratch = [pltpu.SemaphoreType.DMA((size,)) for _, _, size, _ in parts]
+    scratch += [pltpu.SemaphoreType.DMA((size,)) for _, _, size, _ in parts]
+    scratch.append(pltpu.SemaphoreType.DMA((len(parts),)))
+    return pl.pallas_call(
+        functools.partial(_exchange_kernel, layout),
+        out_shape=tuple(shapes),
+        in_specs=[pl.BlockSpec(memory_space=pl.ANY)] * len(parts),
+        out_specs=tuple(pl.BlockSpec(memory_space=pl.ANY) for _ in parts),
+        scratch_shapes=scratch,
+        compiler_params=pltpu.CompilerParams(collective_id=collective_id, has_side_effects=True),
+    )(*[array for array, _, _, _ in parts])
 
 
 def _turn_kernel(n, blocks_ref, out_ref, send_sems, recv_sems):
@@ -100,7 +184,8 @@
         product = jnp.einsum("cd,qbd->qbc", rows, factors, preferred_element_type=jnp.float32)
         return product.astype(jnp.bfloat16)
 
-    halves_first = half_products(gather_rows(own))
+    (pieces,) = exchange([(own, 1, vir_devices, True)], 0)
+    halves_first = half_products(pieces.reshape(vir_devices * row_count, own.shape[-1]))
     halves_second = half_products(gather_rows(other))
     direct = jnp.einsum("qac,qbc->ab", factors, halves_first, preferred_element_type=jnp.float32)
     turned_term = jnp.einsum("qac,qbc->ab", halves_second, factors, preferred_element_type=jnp.float32)

time: 150 us -> 155 us (1.033)
  blocking collectives: 40.2 us -> 0 us
  Pallas kernels: 12.1 us -> 50.2 us
  starting transfers between devices: 9.91 us -> 13.9 us
  waiting for transfers between devices: 41.1 us -> 43 us
    all_to_all x1 -> x0, blocking collectives: 40.2 us -> none  [gather_rows(): lax.all_to_all(spread, 'vir', split_axis=0, concat_axis=0, tiled=True)]
    pallas_call x0 -> x1, Pallas kernels: none -> 38.1 us  [exchange(): pl.pallas_call(functools.partial(_exchange_kernel, layout), out_shape=tup...]
    all_to_all x1, starting transfers between devices: 4.01 us -> 8.08 us  [gather_rows(): lax.all_to_all(spread, 'vir', split_axis=0, concat_axis=0, tiled=True)]
where the time goes in v14:
time: 155 us; the launch traced here: 154 us
  Pallas kernels  50.2 us (32%)
  waiting for transfers between devices  43 us (28%)
  matrix products  39.1 us (25%)
  starting transfers between devices  13.9 us (9%)
  local copies, waits for them, and re-layouts  4.43 us (3%)
  other arithmetic  3.33 us (2%)
    pallas_call x1, Pallas kernels, exchange(): pl.pallas_call(functools.partial(_exchange_kernel, layout), out_shape=tup...  38.1 us
    all_to_all x1, waiting for transfers between devices, per_device(): lax.all_to_all(blocks, 'vir', split_axis=0, concat_axis=0, tiled=True)  30.7 us
    dot_general x1, matrix products, per_device(): jnp.einsum('qac,qbc->ab', factors, halves_first, preferred_element_type=j...  20.3 us
    dot_general x1, matrix products, per_device(): jnp.einsum('qac,qbc->ab', halves_second, factors, preferred_element_type=...  18.8 us
    pallas_call x1, Pallas kernels, partner_transpose(): pl.pallas_call(functools.partial(_turn_kernel, n), out_shape=jax.ShapeDty...  12.1 us
    all_to_all x1, waiting for transfers between devices, gather_rows(): lax.all_to_all(spread, 'vir', split_axis=0, concat_axis=0, tiled=True)  9.71 us
    all_to_all x1, starting transfers between devices, gather_rows(): lax.all_to_all(spread, 'vir', split_axis=0, concat_axis=0, tiled=True)  8.08 us
    all_to_all x1, starting transfers between devices, per_device(): lax.all_to_all(blocks, 'vir', split_axis=0, concat_axis=0, tiled=True)  4.16 us
  transfers between devices with their start and end apart: 3, of which 3 were waited for; matrix products, arithmetic and copies ran while one was open for 14% of the time, Pallas kernels for 0%

profile of v14, /device:TPU:0, one launch (start us, length us, event | category | flops | bytes accessed | tf_op | source)
XLA Modules:
  0.0 154.2 jit_solution(10697815333917656185)
XLA Ops:
  0.0 1.5 select_bitcast_fusion
  1.5 1.7 %collective-permute-start = (bf16[32,1024]{1,0:T(8,128)(2,1)S(1)}, bf16[32,1024]{1,0:T(8,128)(2,1)S(1)}, u32[]{:S(2)}, u32[]{:S(2)}) collective-permute-start(bf16[32,1024]{1,0:T(8,128)(2,1)S(1)} %get-tuple-element.15), channel_id=1, source_target_pairs={{64,0},{96,32},{0,64},{32,96},{65,1},{97,33},{1,65},{33,97},{66,2}... | collective-permute-start | bytes 196616 | tf_op jit(solution)/shard_map/ppermute | solution.py:14
  3.2 2.6 %collective-permute-done = bf16[32,1024]{1,0:T(8,128)(2,1)S(1)} collective-permute-done((bf16[32,1024]{1,0:T(8,128)(2,1)S(1)}, bf16[32,1024]{1,0:T(8,128)(2,1)S(1)}, u32[]{:S(2)}, u32[]{:S(2)}) %collective-permute-start) | collective-permute-done | bytes 65568 | tf_op jit(solution)/shard_map/ppermute | solution.py:14
  5.8 38.1 %shard_map.73 = bf16[32,32,1024]{2,1,0:T(8,128)(2,1)} custom-call(bf16[32,1024]{1,0:T(8,128)(2,1)} %get-tuple-element.7.refs_0_), custom_call_target="tpu_custom_call" | custom-call | tf_op jit(solution)/shard_map/pallas_call | solution.py:91
  43.9 1.6 %broadcast_in_dim.56 = bf16[32,32,1024]{2,1,0:T(8,128)(2,1)} broadcast(bf16[32,1024]{1,0:T(8,128)(2,1)S(1)} %collective-permute-done), dimensions={1,2} | broadcast | bytes 2162688 | tf_op jit(solution)/shard_map/broadcast_in_dim | solution.py:179
  45.5 8.1 %all-to-all-start = ((bf16[32,32,1024]{2,1,0:T(8,128)(2,1)}), bf16[32,32,1024]{2,1,0:T(8,128)(2,1)S(1)}, u32[]{:S(2)}, u32[]{:S(2)}) async-start(bf16[32,32,1024]{2,1,0:T(8,128)(2,1)} %broadcast_in_dim.56), calls=%async_computation | async-start | bytes 4194304 | tf_op jit(solution)/shard_map/all_to_all | solution.py:180
  53.6 20.3 %fusion.2 = f32[1024,1024,1]{0,1,2:T(8,128)} fusion(bf16[3,1024,1024]{2,1,0:T(8,128)(2,1)} %param.8, bf16[1024,1024,1]{1,0,2:T(8,128)(2,1)} %bitcast.47), kind=kOutput, calls=%fused_computation.2 | convolution fusion | flops 12888047616 | bytes 12582912 | tf_op jit(solution)/shard_map/qac,qbc->ab/dot_general | solution.py:190
  73.9 9.7 %all-to-all-done = bf16[32,32,1024]{2,1,0:T(8,128)(2,1)S(1)} async-done(((bf16[32,32,1024]{2,1,0:T(8,128)(2,1)}), bf16[32,32,1024]{2,1,0:T(8,128)(2,1)S(1)}, u32[]{:S(2)}, u32[]{:S(2)}) %all-to-all-start) | async-done | bytes 2097184 | tf_op jit(solution)/shard_map/all_to_all | solution.py:180
  83.6 18.8 %fusion.6 = bf16[1024,1024]{1,0:T(8,128)(2,1)} fusion(f32[1024,1024,1]{0,1,2:T(8,128)} %fusion.2, bf16[3,1024,1024]{2,1,0:T(8,128)(2,1)} %param.8, bf16[1024,1024,1]{1,0,2:T(8,128)(2,1)S(1)} %bitcast.46), kind=kOutput, calls=%fused_computation.7 | convolution fusion | flops 12890144768 | bytes 14680064 | tf_op jit(solution)/shard_map/qac,qbc->ab/dot_general | solution.py:191
  102.5 4.2 %all-to-all-start.1 = ((bf16[32,32,1024]{2,1,0:T(8,128)(2,1)}), bf16[32,32,1024]{2,1,0:T(8,128)(2,1)S(1)}, u32[]{:S(2)}, u32[]{:S(2)}) async-start(bf16[32,32,1024]{2,1,0:T(8,128)(2,1)} %bitcast.45), calls=%async_computation.1 | async-start | bytes 4194304 | tf_op jit(solution)/shard_map/all_to_all | solution.py:194
  106.7 0.1 dynamic_slice.11
  106.7 0.1 dynamic_slice.10
  106.8 0.1 constant_dynamic-slice_fusion
  106.9 0.2 select_reduce_fusion
  107.1 0.2 select_reduce_fusion.2
  107.3 0.1 broadcast_xor_fusion
  107.4 0.1 broadcast_add_fusion
  107.5 30.7 %all-to-all-done.1 = bf16[32,32,1024]{2,1,0:T(8,128)(2,1)S(1)} async-done(((bf16[32,32,1024]{2,1,0:T(8,128)(2,1)}), bf16[32,32,1024]{2,1,0:T(8,128)(2,1)S(1)}, u32[]{:S(2)}, u32[]{:S(2)}) %all-to-all-start.1) | async-done | bytes 2097184 | tf_op jit(solution)/shard_map/all_to_all | solution.py:194
  138.2 0.4 convert_reduce_fusion
  138.6 1.0 copy.13
  139.6 12.1 %shard_map.74 = f32[32,32,32]{2,1,0:T(8,128)} custom-call(f32[32,32,32]{2,1,0:T(8,128)} %bitcast.44), custom_call_target="tpu_custom_call" | custom-call | tf_op jit(solution)/shard_map/pallas_call | solution.py:152
  151.7 1.4 copy.14
  153.1 0.2 reshape.126
  153.3 0.8 fusion.13
  (14 shorter events, 0.1 us)
Async XLA Ops:
  0.0 106.8 %copy-start = (s32[8,2]{0,1:T(2,128)S(1)}, s32[8,2]{0,1:T(2,128)}, u32[]{:S(2)}) copy-start(s32[8,2]{0,1:T(2,128)} %param.13) | copy-start | bytes 196
  1.5 4.3 %collective-permute-start = (bf16[32,1024]{1,0:T(8,128)(2,1)S(1)}, bf16[32,1024]{1,0:T(8,128)(2,1)S(1)}, u32[]{:S(2)}, u32[]{:S(2)}) collective-permute-start(bf16[32,1024]{1,0:T(8,128)(2,1)S(1)} %get-tuple-element.15), channel_id=1, source_target_pairs={{64,0},{96,32},{0,64},{32,96},{65,1},{97,33},{1,65},{33,97},{66,2}... | collective-permute-start | bytes 196616 | tf_op jit(solution)/shard_map/ppermute | solution.py:14
  45.5 38.1 %all-to-all-start = ((bf16[32,32,1024]{2,1,0:T(8,128)(2,1)}), bf16[32,32,1024]{2,1,0:T(8,128)(2,1)S(1)}, u32[]{:S(2)}, u32[]{:S(2)}) async-start(bf16[32,32,1024]{2,1,0:T(8,128)(2,1)} %broadcast_in_dim.56), calls=%async_computation | async-start | bytes 4194304 | tf_op jit(solution)/shard_map/all_to_all | solution.py:180
  102.5 4.2 %copy-start.2 = (f32[1024]{0:T(1024)S(1)}, f32[1024]{0:T(1024)}, u32[]{:S(2)}) copy-start(f32[1024]{0:T(1024)} %param.10) | copy-start | bytes 12292
  102.5 4.3 %copy-start.1 = (s32[1024]{0:T(1024)S(1)}, s32[1024]{0:T(1024)}, u32[]{:S(2)}) copy-start(s32[1024]{0:T(1024)} %param.12) | copy-start | bytes 12292
  102.5 4.4 %copy-start.3 = (f32[100]{0:T(128)S(1)}, f32[100]{0:T(128)}, u32[]{:S(2)}) copy-start(f32[100]{0:T(128)} %param.9) | copy-start | bytes 1204
  102.5 4.7 %copy-start.4 = (s32[100]{0:T(128)S(1)}, s32[100]{0:T(128)}, u32[]{:S(2)}) copy-start(s32[100]{0:T(128)} %param.11) | copy-start | bytes 1204
  102.5 35.8 %all-to-all-start.1 = ((bf16[32,32,1024]{2,1,0:T(8,128)(2,1)}), bf16[32,32,1024]{2,1,0:T(8,128)(2,1)S(1)}, u32[]{:S(2)}, u32[]{:S(2)}) async-start(bf16[32,32,1024]{2,1,0:T(8,128)(2,1)} %bitcast.45), calls=%async_computation.1 | async-start | bytes 4194304 | tf_op jit(solution)/shard_map/all_to_all | solution.py:194

commit v15 on v10

--- a/solution.py
+++ b/solution.py
@@ -14,8 +14,10 @@
     return lax.ppermute(block, axis, route)
 
 
-def _turn_kernel(n, blocks_ref, out_ref, send_sems, recv_sems):
+def _turn_kernel(n, rows_ref, out_ref, flipped, send_sems, recv_sems):
     me = lax.axis_index("vir")
+    rows = rows_ref.shape[0]
+    flipped[...] = jnp.transpose(rows_ref[...], (1, 0))
     group = lax.axis_index("occ")
     partner = lax.rem(group + lax.axis_size("occ") // 2, lax.axis_size("occ"))
 
@@ -31,7 +33,7 @@
     def copy_to(k):
         dest = lax.rem(me + k, n)
         return pltpu.make_async_remote_copy(
-            src_ref=blocks_ref.at[dest],
+            src_ref=flipped.at[pl.ds(pl.multiple_of(dest * rows, rows), rows)],
             dst_ref=out_ref.at[me],
             send_sem=send_sems.at[dest],
             recv_sem=recv_sems.at[me],
@@ -49,7 +51,7 @@
         copy_to(k).wait_send()
         source = lax.rem(me + n - k, n)
         pltpu.make_async_remote_copy(
-            src_ref=blocks_ref.at[source],
+            src_ref=flipped.at[pl.ds(pl.multiple_of(source * rows, rows), rows)],
             dst_ref=out_ref.at[source],
             send_sem=send_sems.at[source],
             recv_sem=recv_sems.at[source],
@@ -64,15 +66,18 @@
 def partner_transpose(own_rows, vir_axis):
     n = lax.axis_size(vir_axis)
     rows, width = own_rows.shape
-    blocks = jnp.transpose(own_rows.reshape(rows, n, width // n), (1, 2, 0))
     arrived = pl.pallas_call(
         functools.partial(_turn_kernel, n),
-        out_shape=jax.ShapeDtypeStruct(blocks.shape, blocks.dtype),
-        in_specs=[pl.BlockSpec(memory_space=pl.ANY)],
+        out_shape=jax.ShapeDtypeStruct((n, rows, rows), own_rows.dtype),
+        in_specs=[pl.BlockSpec(memory_space=pltpu.VMEM)],
         out_specs=pl.BlockSpec(memory_space=pl.ANY),
-        scratch_shapes=[pltpu.SemaphoreType.DMA((n,)), pltpu.SemaphoreType.DMA((n,))],
+        scratch_shapes=[
+            pltpu.VMEM((width, rows), own_rows.dtype),
+            pltpu.SemaphoreType.DMA((n,)),
+            pltpu.SemaphoreType.DMA((n,)),
+        ],
         compiler_params=pltpu.CompilerParams(collective_id=1, has_side_effects=True),
-    )(blocks)
+    )(own_rows)
     return jnp.transpose(arrived, (1, 0, 2)).reshape(width // n, n * rows)
 
 

time: 150 us -> 152 us (1.013)
  other arithmetic: 2.71 us -> 4.28 us
    dot_general x1, matrix products: 18.8 us -> 20.4 us  [per_device(): jnp.einsum('qac,qbc->ab', halves_second, factors, preferred_element_type=...]
where the time goes in v15:
time: 152 us
  waiting for transfers between devices  41.1 us (27%)
  blocking collectives  40.2 us (26%)
  matrix products  39.3 us (26%)
  Pallas kernels  13.2 us (9%)
  starting transfers between devices  9.91 us (7%)
  other arithmetic  4.28 us (3%)
  local copies, waits for them, and re-layouts  3.69 us (2%)
    all_to_all x1, blocking collectives, gather_rows(): lax.all_to_all(spread, 'vir', split_axis=0, concat_axis=0, tiled=True)  40.2 us
    all_to_all x1, waiting for transfers between devices, per_device(): lax.all_to_all(blocks, 'vir', split_axis=0, concat_axis=0, tiled=True)  29.7 us
    dot_general x1, matrix products, per_device(): jnp.einsum('qac,qbc->ab', halves_second, factors, preferred_element_type=...  20.4 us
    dot_general x1, matrix products, per_device(): jnp.einsum('qac,qbc->ab', factors, halves_first, preferred_element_type=j...  18.9 us
    pallas_call x1, Pallas kernels, partner_transpose(): pl.pallas_call(functools.partial(_turn_kernel, n), out_shape=jax.ShapeDty...  13.2 us
    all_to_all x1, waiting for transfers between devices, gather_rows(): lax.all_to_all(spread, 'vir', split_axis=0, concat_axis=0, tiled=True)  8.78 us
    all_to_all x1, starting transfers between devices, per_device(): lax.all_to_all(blocks, 'vir', split_axis=0, concat_axis=0, tiled=True)  4.15 us
    all_to_all x1, starting transfers between devices, gather_rows(): lax.all_to_all(spread, 'vir', split_axis=0, concat_axis=0, tiled=True)  4.01 us
  transfers between devices with their start and end apart: 3, of which 3 were waited for; matrix products, arithmetic and copies ran while one was open for 14% of the time, Pallas kernels for 0%

profile of v15, /device:TPU:0, one launch (start us, length us, event | category | flops | bytes accessed | tf_op | source)
XLA Modules:
  0.0 151.7 jit_solution(3364986958134047685)
XLA Ops:
  0.0 0.9 select_bitcast_fusion
  0.9 1.7 %collective-permute-start = (bf16[32,1024]{1,0:T(8,128)(2,1)S(1)}, bf16[32,1024]{1,0:T(8,128)(2,1)S(1)}, u32[]{:S(2)}, u32[]{:S(2)}) collective-permute-start(bf16[32,1024]{1,0:T(8,128)(2,1)S(1)} %get-tuple-element.15), channel_id=1, source_target_pairs={{64,0},{96,32},{0,64},{32,96},{65,1},{97,33},{1,65},{33,97},{66,2}... | collective-permute-start | bytes 196616 | tf_op jit(solution)/shard_map/ppermute | solution.py:14
  2.6 2.6 %collective-permute-done = bf16[32,1024]{1,0:T(8,128)(2,1)S(1)} collective-permute-done((bf16[32,1024]{1,0:T(8,128)(2,1)S(1)}, bf16[32,1024]{1,0:T(8,128)(2,1)S(1)}, u32[]{:S(2)}, u32[]{:S(2)}) %collective-permute-start) | collective-permute-done | bytes 65568 | tf_op jit(solution)/shard_map/ppermute | solution.py:14
  5.2 0.2 broadcast_in_dim.63
  5.5 40.2 %all_to_all.15 = bf16[32,32,1024]{2,1,0:T(8,128)(2,1)} all-to-all(bf16[32,32,1024]{2,1,0:T(8,128)(2,1)S(1)} %broadcast_in_dim.63), channel_id=1, replica_groups=mesh['occ'=4,'vir'=32] {'vir'}, dimensions={0} | all-to-all | bytes 4194304 | tf_op jit(solution)/shard_map/all_to_all | solution.py:101
  45.7 1.6 %broadcast_in_dim.62 = bf16[32,32,1024]{2,1,0:T(8,128)(2,1)} broadcast(bf16[32,1024]{1,0:T(8,128)(2,1)S(1)} %get-tuple-element.7), dimensions={1,2} | broadcast | bytes 2162688 | tf_op jit(solution)/shard_map/broadcast_in_dim | solution.py:100
  47.3 4.0 %all-to-all-start = ((bf16[32,32,1024]{2,1,0:T(8,128)(2,1)}), bf16[32,32,1024]{2,1,0:T(8,128)(2,1)S(1)}, u32[]{:S(2)}, u32[]{:S(2)}) async-start(bf16[32,32,1024]{2,1,0:T(8,128)(2,1)} %broadcast_in_dim.62), calls=%async_computation | async-start | bytes 4194304 | tf_op jit(solution)/shard_map/all_to_all | solution.py:101
  51.3 20.4 %fusion = f32[1024,1024,1]{1,0,2:T(8,128)} fusion(bf16[3,1024,1024]{2,1,0:T(8,128)(2,1)} %param.8, bf16[1024,1024,1]{1,0,2:T(8,128)(2,1)} %bitcast.52), kind=kOutput, calls=%fused_computation | convolution fusion | flops 12888047616 | bytes 12582912 | tf_op jit(solution)/shard_map/qac,qbc->ab/dot_general | solution.py:111
  71.7 8.8 %all-to-all-done = bf16[32,32,1024]{2,1,0:T(8,128)(2,1)S(1)} async-done(((bf16[32,32,1024]{2,1,0:T(8,128)(2,1)}), bf16[32,32,1024]{2,1,0:T(8,128)(2,1)S(1)}, u32[]{:S(2)}, u32[]{:S(2)}) %all-to-all-start) | async-done | bytes 2097184 | tf_op jit(solution)/shard_map/all_to_all | solution.py:101
  80.5 18.9 %fusion.6 = bf16[1024,1024]{1,0:T(8,128)(2,1)} fusion(f32[1024,1024,1]{1,0,2:T(8,128)} %fusion, bf16[3,1024,1024]{2,1,0:T(8,128)(2,1)} %param.8, bf16[1024,1024,1]{1,0,2:T(8,128)(2,1)S(1)} %bitcast.51), kind=kOutput, calls=%fused_computation.7 | convolution fusion | flops 12886999040 | bytes 14680064 | tf_op jit(solution)/shard_map/qac,qbc->ab/dot_general | solution.py:110
  99.4 4.2 %all-to-all-start.2 = ((bf16[32,32,1024]{2,1,0:T(8,128)(2,1)}), bf16[32,32,1024]{2,1,0:T(8,128)(2,1)S(1)}, u32[]{:S(2)}, u32[]{:S(2)}) async-start(bf16[32,32,1024]{2,1,0:T(8,128)(2,1)} %bitcast.50), calls=%async_computation.2 | async-start | bytes 4194304 | tf_op jit(solution)/shard_map/all_to_all | solution.py:114
  103.6 0.1 dynamic_slice.11
  103.7 0.1 dynamic_slice.10
  103.8 0.1 constant_dynamic-slice_fusion
  103.8 0.2 select_reduce_fusion
  104.1 0.2 select_reduce_fusion.2
  104.4 0.1 broadcast_add_fusion
  104.5 29.7 %all-to-all-done.2 = bf16[32,32,1024]{2,1,0:T(8,128)(2,1)S(1)} async-done(((bf16[32,32,1024]{2,1,0:T(8,128)(2,1)}), bf16[32,32,1024]{2,1,0:T(8,128)(2,1)S(1)}, u32[]{:S(2)}, u32[]{:S(2)}) %all-to-all-start.2) | async-done | bytes 2097184 | tf_op jit(solution)/shard_map/all_to_all | solution.py:114
  134.2 1.0 convert_reduce_fusion.rows_ref
  135.2 13.2 %shard_map.73 = f32[32,32,32]{2,1,0:T(8,128)} custom-call(f32[32,1024]{1,0:T(8,128)} %convert_reduce_fusion.rows_ref), custom_call_target="tpu_custom_call" | custom-call | tf_op jit(solution)/shard_map/pallas_call | solution.py:69
  148.4 1.4 copy.9
  149.7 0.2 reshape.123
  150.0 0.9 bitcast_select_fusion.1
  150.9 0.8 fusion.11
  (14 shorter events, 0.1 us)
Async XLA Ops:
  0.0 103.8 %copy-start = (s32[8,2]{0,1:T(2,128)S(1)}, s32[8,2]{0,1:T(2,128)}, u32[]{:S(2)}) copy-start(s32[8,2]{0,1:T(2,128)} %param.13) | copy-start | bytes 196
  0.9 4.3 %collective-permute-start = (bf16[32,1024]{1,0:T(8,128)(2,1)S(1)}, bf16[32,1024]{1,0:T(8,128)(2,1)S(1)}, u32[]{:S(2)}, u32[]{:S(2)}) collective-permute-start(bf16[32,1024]{1,0:T(8,128)(2,1)S(1)} %get-tuple-element.15), channel_id=1, source_target_pairs={{64,0},{96,32},{0,64},{32,96},{65,1},{97,33},{1,65},{33,97},{66,2}... | collective-permute-start | bytes 196616 | tf_op jit(solution)/shard_map/ppermute | solution.py:14
  47.3 33.2 %all-to-all-start = ((bf16[32,32,1024]{2,1,0:T(8,128)(2,1)}), bf16[32,32,1024]{2,1,0:T(8,128)(2,1)S(1)}, u32[]{:S(2)}, u32[]{:S(2)}) async-start(bf16[32,32,1024]{2,1,0:T(8,128)(2,1)} %broadcast_in_dim.62), calls=%async_computation | async-start | bytes 4194304 | tf_op jit(solution)/shard_map/all_to_all | solution.py:101
  99.4 4.2 %copy-start.2 = (f32[1024]{0:T(1024)S(1)}, f32[1024]{0:T(1024)}, u32[]{:S(2)}) copy-start(f32[1024]{0:T(1024)} %param.10) | copy-start | bytes 12292
  99.4 4.3 %copy-start.1 = (s32[1024]{0:T(1024)S(1)}, s32[1024]{0:T(1024)}, u32[]{:S(2)}) copy-start(s32[1024]{0:T(1024)} %param.12) | copy-start | bytes 12292
  99.4 4.4 %copy-start.3 = (f32[100]{0:T(128)S(1)}, f32[100]{0:T(128)}, u32[]{:S(2)}) copy-start(f32[100]{0:T(128)} %param.9) | copy-start | bytes 1204
  99.4 4.7 %copy-start.4 = (s32[100]{0:T(128)S(1)}, s32[100]{0:T(128)}, u32[]{:S(2)}) copy-start(s32[100]{0:T(128)} %param.11) | copy-start | bytes 1204
  99.4 34.8 %all-to-all-start.2 = ((bf16[32,32,1024]{2,1,0:T(8,128)(2,1)}), bf16[32,32,1024]{2,1,0:T(8,128)(2,1)S(1)}, u32[]{:S(2)}, u32[]{:S(2)}) async-start(bf16[32,32,1024]{2,1,0:T(8,128)(2,1)} %bitcast.50), calls=%async_computation.2 | async-start | bytes 4194304 | tf_op jit(solution)/shard_map/all_to_all | solution.py:114

commit v16 on v7

--- a/solution.py
+++ b/solution.py
@@ -14,7 +14,7 @@
     return lax.ppermute(block, axis, route)
 
 
-def _ladder_scatter_kernel(n, groups, factors_ref, first_ref, second_ref, out_ref, cbuf, send_sems, recv_sems, own_sem):
+def _turned_scatter_kernel(n, groups, factors_ref, other_ref, direct_ref, out_ref, hbuf, cbuf, send_sems, recv_sems, own_sem):
     me = lax.axis_index("vir")
     group = lax.axis_index("occ")
     q_count = factors_ref.shape[0]
@@ -74,19 +74,27 @@
         chosen = group_at(step)
         row0 = pl.multiple_of(chosen * span, span)
 
+        def halves(t, carry):
+            col0 = pl.multiple_of(t * tile, tile)
+            for q in range(q_count):
+                product = lax.dot_general(
+                    factors_ref[q, pl.ds(row0, span), :], other_ref[pl.ds(col0, tile), :],
+                    dims, preferred_element_type=jnp.float32,
+                )
+                hbuf[q, :, pl.ds(col0, tile)] = product.astype(hbuf.dtype)
+            return carry
+
+        lax.fori_loop(0, tiles, halves, 0)
+
         def product(t, carry):
             col0 = pl.multiple_of(t * tile, tile)
-            acc = jnp.zeros((span, tile), jnp.float32)
+            acc = direct_ref[pl.ds(row0, span), pl.ds(col0, tile)]
             for q in range(q_count):
                 acc += lax.dot_general(
-                    factors_ref[q, pl.ds(row0, span), :], first_ref[q, pl.ds(col0, tile), :],
+                    hbuf[q], factors_ref[q, pl.ds(col0, tile), :],
                     dims, preferred_element_type=jnp.float32,
                 )
-                acc += lax.dot_general(
-                    second_ref[q, pl.ds(row0, span), :], factors_ref[q, pl.ds(col0, tile), :],
-                    dims, preferred_element_type=jnp.float32,
-                )
-            cbuf[slot, :, pl.ds(col0, tile)] = acc
+            cbuf[slot, :, pl.ds(col0, tile)] = acc.astype(cbuf.dtype)
             return carry
 
         lax.fori_loop(0, tiles, product, 0)
@@ -119,18 +127,20 @@
     lax.fori_loop(1, n, arrive, 0)
 
 
-def ladder_rows(factors, first_halves, second_halves, vir_axis):
+def turned_rows(factors, other_rows, direct, vir_axis):
     n = lax.axis_size(vir_axis)
     width = factors.shape[1]
     rows = width // n
     groups = 4
+    span = (n // groups) * rows
     arrived = pl.pallas_call(
-        functools.partial(_ladder_scatter_kernel, n, groups),
-        out_shape=jax.ShapeDtypeStruct((n, rows, width), jnp.float32),
+        functools.partial(_turned_scatter_kernel, n, groups),
+        out_shape=jax.ShapeDtypeStruct((n, rows, width), jnp.bfloat16),
         in_specs=[pl.BlockSpec(memory_space=pltpu.VMEM)] * 3,
         out_specs=pl.BlockSpec(memory_space=pl.ANY),
         scratch_shapes=[
-            pltpu.VMEM((2, (n // groups) * rows, width), jnp.float32),
+            pltpu.VMEM((factors.shape[0], span, width), jnp.bfloat16),
+            pltpu.VMEM((2, span, width), jnp.bfloat16),
             pltpu.SemaphoreType.DMA((n,)),
             pltpu.SemaphoreType.DMA((n,)),
             pltpu.SemaphoreType.DMA,
@@ -138,8 +148,70 @@
         compiler_params=pltpu.CompilerParams(
             collective_id=0, has_side_effects=True, vmem_limit_bytes=48 * 1024 * 1024
         ),
-    )(factors, first_halves, second_halves)
-    return jnp.sum(arrived, axis=0)
+    )(factors, other_rows, direct)
+    return jnp.sum(arrived.astype(jnp.float32), axis=0)
+
+
+def _turn_kernel(n, blocks_ref, out_ref, send_sems, recv_sems):
+    me = lax.axis_index("vir")
+    group = lax.axis_index("occ")
+    partner = lax.rem(group + lax.axis_size("occ") // 2, lax.axis_size("occ"))
+
+    barrier = pltpu.get_barrier_semaphore()
+
+    def greet(k, carry):
+        pl.semaphore_signal(barrier, inc=1, device_id=(partner, k), device_id_type=pl.DeviceIdType.MESH)
+        return carry
+
+    lax.fori_loop(0, n, greet, 0)
+    pl.semaphore_wait(barrier, n)
+
+    def copy_to(k):
+        dest = lax.rem(me + k, n)
+        return pltpu.make_async_remote_copy(
+            src_ref=blocks_ref.at[dest],
+            dst_ref=out_ref.at[me],
+            send_sem=send_sems.at[dest],
+            recv_sem=recv_sems.at[me],
+            device_id=(partner, dest),
+            device_id_type=pl.DeviceIdType.MESH,
+        )
+
+    def send(k, carry):
+        copy_to(k).start()
+        return carry
+
+    lax.fori_loop(0, n, send, 0)
+
+    def finish(k, carry):
+        copy_to(k).wait_send()
+        source = lax.rem(me + n - k, n)
+        pltpu.make_async_remote_copy(
+            src_ref=blocks_ref.at[source],
+            dst_ref=out_ref.at[source],
+            send_sem=send_sems.at[source],
+            recv_sem=recv_sems.at[source],
+            device_id=(partner, source),
+            device_id_type=pl.DeviceIdType.MESH,
+        ).wait_recv()
+        return carry
+
+    lax.fori_loop(0, n, finish, 0)
+
+
+def partner_transpose(own_rows, vir_axis):
+    n = lax.axis_size(vir_axis)
+    rows, width = own_rows.shape
+    blocks = jnp.transpose(own_rows.reshape(rows, n, width // n), (1, 2, 0))
+    arrived = pl.pallas_call(
+        functools.partial(_turn_kernel, n),
+        out_shape=jax.ShapeDtypeStruct(blocks.shape, blocks.dtype),
+        in_specs=[pl.BlockSpec(memory_space=pl.ANY)],
+        out_specs=pl.BlockSpec(memory_space=pl.ANY),
+        scratch_shapes=[pltpu.SemaphoreType.DMA((n,)), pltpu.SemaphoreType.DMA((n,))],
+        compiler_params=pltpu.CompilerParams(collective_id=1, has_side_effects=True),
+    )(blocks)
+    return jnp.transpose(arrived, (1, 0, 2)).reshape(width // n, n * rows)
 
 
 def per_device(amplitudes, factors, occ_energy, vir_energy, occ_irrep, vir_irrep, pair_orbitals):
@@ -152,10 +224,10 @@
     vir_index = lax.axis_index("vir")
     lower_half = occ_index < occ_devices // 2
 
+    own = jnp.where(lower_half, amplitudes[0], amplitudes[1])
     outgoing = jnp.where(lower_half, amplitudes[1], amplitudes[0])
-    incoming = passed_along(outgoing, "occ", occ_devices // 2)
-    first = jnp.where(lower_half, amplitudes[0], incoming)
-    second = jnp.where(lower_half, incoming, amplitudes[1])
+    other = passed_along(outgoing, "occ", occ_devices // 2)
+    own, other = lax.optimization_barrier((own, other))
 
     def gather_rows(block):
         spread = jnp.broadcast_to(block[None], (vir_devices,) + block.shape)
@@ -163,21 +235,15 @@
         return pieces.reshape(vir_devices * row_count, block.shape[-1])
 
     def half_products(rows):
-        def half_product(factor):
-            product = jnp.einsum("cd,bd->bc", rows, factor, preferred_element_type=jnp.float32)
-            return product.astype(jnp.bfloat16)
-
-        return lax.map(half_product, factors)
-
-    halves_first = half_products(gather_rows(first))
-    halves_second = half_products(gather_rows(second))
-    own_rows = ladder_rows(factors, halves_first, halves_second, "vir")
-    cols = lax.all_to_all(own_rows, "vir", split_axis=1, concat_axis=0, tiled=True)
-    own_cols = jnp.transpose(cols, (1, 0))
-    outgoing_block = jnp.where(lower_half, own_cols, own_rows)
-    incoming_block = passed_along(outgoing_block, "occ", occ_devices // 2)
-    first_out = jnp.where(lower_half, own_rows, incoming_block)
-    second_out = jnp.where(lower_half, incoming_block, own_cols)
+        product = jnp.einsum("cd,qbd->qbc", rows, factors, preferred_element_type=jnp.float32)
+        return product.astype(jnp.bfloat16)
+
+    halves_first = half_products(gather_rows(own))
+    direct = jnp.einsum("qac,qbc->ab", factors, halves_first, preferred_element_type=jnp.float32)
+    own_rows = turned_rows(factors, gather_rows(other), direct, "vir")
+    partner_cols = partner_transpose(own_rows, "vir")
+    first_out = jnp.where(lower_half, own_rows, partner_cols)
+    second_out = jnp.where(lower_half, partner_cols, own_rows)
     summed_pair = jnp.stack([first_out, second_out], axis=0)
 
     pair_ids = lax.dynamic_slice_in_dim(pair_orbitals, occ_index * local_pairs, local_pairs, 0)

time: 225 us -> 154 us (0.68)
  starting transfers between devices: 34.8 us -> 16.6 us
  Pallas kernels: 78 us -> 63.4 us
  waiting for transfers between devices: 56.5 us -> 42.5 us
  matrix products: 33.7 us -> 20.3 us
  local copies, waits for them, and re-layouts: 14.9 us -> 6.42 us
  other arithmetic: 6.63 us -> 2.7 us
    all_to_all x1 -> x0, starting transfers between devices: 17.8 us -> none  [per_device(): lax.all_to_all(own_rows, 'vir', split_axis=1, concat_axis=0, tiled=True)]
    pallas_call x1 -> x2, Pallas kernels: 78 us -> 63.4 us  [the longest x1 49.1 us: turned_rows(): pl.pallas_call(functools.partial(_turned_scatter_kernel, n, groups), out_...]
    dot_general x6 -> x1, matrix products: 33.7 us -> 20.3 us  [per_device(): jnp.einsum('qac,qbc->ab', factors, halves_first, preferred_element_type=j...]
    all_to_all x1 -> x0, waiting for transfers between devices: 10.1 us -> none  [per_device(): lax.all_to_all(own_rows, 'vir', split_axis=1, concat_axis=0, tiled=True)]
    another operation x2 -> x0, local copies, waits for them, and re-layouts: 6.91 us -> none
    ppermute x2 -> x1, waiting for transfers between devices: 7.23 us -> 2.61 us  [passed_along(): return lax.ppermute(block, axis, route)]
    unnamed x16 -> x12, local copies, waits for them, and re-layouts: 3.24 us -> 0.27 us
  transfers between devices with their start and end apart: 5 -> 3, of which waited for: 5 -> 3; matrix products, arithmetic and copies ran while one was open for 10% -> 14% of each run, Pallas kernels for 0% -> 0%
where the time goes in v16:
time: 154 us; the launch traced here: 152 us
  Pallas kernels  63.4 us (41%)
  waiting for transfers between devices  42.5 us (28%)
  matrix products  20.3 us (13%)
  starting transfers between devices  16.6 us (11%)
  local copies, waits for them, and re-layouts  6.42 us (4%)
  other arithmetic  2.7 us (2%)
    pallas_call x1, Pallas kernels, turned_rows(): pl.pallas_call(functools.partial(_turned_scatter_kernel, n, groups), out_...  49.1 us
    all_to_all x2, waiting for transfers between devices, gather_rows(): lax.all_to_all(spread, 'vir', split_axis=0, concat_axis=0, tiled=True)  39.9 us
    dot_general x1, matrix products, per_device(): jnp.einsum('qac,qbc->ab', factors, halves_first, preferred_element_type=j...  20.3 us
    all_to_all x2, starting transfers between devices, gather_rows(): lax.all_to_all(spread, 'vir', split_axis=0, concat_axis=0, tiled=True)  14.9 us
    pallas_call x1, Pallas kernels, partner_transpose(): pl.pallas_call(functools.partial(_turn_kernel, n), out_shape=jax.ShapeDty...  14.3 us
    broadcast_in_dim x2, local copies, waits for them, and re-layouts, gather_rows(): spread = jnp.broadcast_to(block[None], (vir_devices,) + block.shape)  3.36 us
  transfers between devices with their start and end apart: 3, of which 3 were waited for; matrix products, arithmetic and copies ran while one was open for 14% of the time, Pallas kernels for 0%

profile of v16, /device:TPU:0, one launch (start us, length us, event | category | flops | bytes accessed | tf_op | source)
XLA Modules:
  0.0 152.1 jit_solution(3610798199158558277)
XLA Ops:
  0.0 0.9 select_bitcast_fusion
  0.9 1.7 %collective-permute-start = (bf16[32,1024]{1,0:T(8,128)(2,1)S(1)}, bf16[32,1024]{1,0:T(8,128)(2,1)S(1)}, u32[]{:S(2)}, u32[]{:S(2)}) collective-permute-start(bf16[32,1024]{1,0:T(8,128)(2,1)S(1)} %get-tuple-element.15), channel_id=1, source_target_pairs={{64,0},{96,32},{0,64},{32,96},{65,1},{97,33},{1,65},{33,97},{66,2}... | collective-permute-start | bytes 196616 | tf_op jit(solution)/shard_map/ppermute | solution.py:14
  2.7 2.6 %collective-permute-done = bf16[32,1024]{1,0:T(8,128)(2,1)S(1)} collective-permute-done((bf16[32,1024]{1,0:T(8,128)(2,1)S(1)}, bf16[32,1024]{1,0:T(8,128)(2,1)S(1)}, u32[]{:S(2)}, u32[]{:S(2)}) %collective-permute-start) | collective-permute-done | bytes 65568 | tf_op jit(solution)/shard_map/ppermute | solution.py:14
  5.3 1.6 %broadcast_in_dim.63 = bf16[32,32,1024]{2,1,0:T(8,128)(2,1)} broadcast(bf16[32,1024]{1,0:T(8,128)(2,1)S(1)} %get-tuple-element.8), dimensions={1,2} | broadcast | bytes 2162688 | tf_op jit(solution)/shard_map/broadcast_in_dim | solution.py:233
  6.9 10.9 %all-to-all-start.1 = ((bf16[32,32,1024]{2,1,0:T(8,128)(2,1)}), bf16[32,32,1024]{2,1,0:T(8,128)(2,1)S(1)}, u32[]{:S(2)}, u32[]{:S(2)}) async-start(bf16[32,32,1024]{2,1,0:T(8,128)(2,1)} %broadcast_in_dim.63), calls=%async_computation.1 | async-start | bytes 4194304 | tf_op jit(solution)/shard_map/all_to_all | solution.py:234
  17.8 0.1 dynamic_slice.11
  17.9 0.1 dynamic_slice.10
  17.9 0.1 constant_dynamic-slice_fusion
  18.0 0.2 select_reduce_fusion
  18.3 0.2 select_reduce_fusion.2
  18.6 0.1 broadcast_add_fusion
  18.6 29.5 %all-to-all-done.1 = bf16[32,32,1024]{2,1,0:T(8,128)(2,1)S(1)} async-done(((bf16[32,32,1024]{2,1,0:T(8,128)(2,1)}), bf16[32,32,1024]{2,1,0:T(8,128)(2,1)S(1)}, u32[]{:S(2)}, u32[]{:S(2)}) %all-to-all-start.1) | async-done | bytes 2097184 | tf_op jit(solution)/shard_map/all_to_all | solution.py:234
  48.2 1.8 %broadcast_in_dim.62 = bf16[32,32,1024]{2,1,0:T(8,128)(2,1)} broadcast(bf16[32,1024]{1,0:T(8,128)(2,1)S(1)} %collective-permute-done), dimensions={1,2} | broadcast | bytes 2162688 | tf_op jit(solution)/shard_map/broadcast_in_dim | solution.py:233
  49.9 0.2 copy-done.1
  50.2 4.0 %all-to-all-start = ((bf16[32,32,1024]{2,1,0:T(8,128)(2,1)}), bf16[32,32,1024]{2,1,0:T(8,128)(2,1)S(1)}, u32[]{:S(2)}, u32[]{:S(2)}) async-start(bf16[32,32,1024]{2,1,0:T(8,128)(2,1)} %broadcast_in_dim.62), calls=%async_computation | async-start | bytes 4194304 | tf_op jit(solution)/shard_map/all_to_all | solution.py:234
  54.2 20.3 %fusion.5.direct_ref = f32[1024,1024]{1,0:T(8,128)} fusion(bf16[3,1024,1024]{2,1,0:T(8,128)(2,1)} %factors_ref.1, bf16[1024,1024,1]{1,0,2:T(8,128)(2,1)} %bitcast.33), kind=kOutput, calls=%fused_computation.5 | convolution fusion | flops 12888047616 | bytes 12582912 | tf_op jit(solution)/shard_map/qac,qbc->ab/dot_general | solution.py:242
  74.5 10.4 %all-to-all-done = bf16[32,32,1024]{2,1,0:T(8,128)(2,1)S(1)} async-done(((bf16[32,32,1024]{2,1,0:T(8,128)(2,1)}), bf16[32,32,1024]{2,1,0:T(8,128)(2,1)S(1)}, u32[]{:S(2)}, u32[]{:S(2)}) %all-to-all-start) | async-done | bytes 2097184 | tf_op jit(solution)/shard_map/all_to_all | solution.py:234
  84.9 49.1 %shard_map.73 = bf16[32,32,1024]{2,1,0:T(8,128)(2,1)S(1)} custom-call(bf16[3,1024,1024]{2,1,0:T(8,128)(2,1)} %factors_ref.1, bf16[1024,1024]{1,0:T(8,128)(2,1)S(1)} %bitcast.31, f32[1024,1024]{1,0:T(8,128)} %fusion.5.direct_ref), custom_call_target="tpu_custom_call" | custom-call | tf_op jit(solution)/shard_map/pallas_call | solution.py:136
  133.9 0.4 convert_reduce_fusion
  134.3 1.0 copy.15
  135.3 14.3 %shard_map.74 = f32[32,32,32]{2,1,0:T(8,128)} custom-call(f32[32,32,32]{2,1,0:T(8,128)} %bitcast.32), custom_call_target="tpu_custom_call" | custom-call | tf_op jit(solution)/shard_map/pallas_call | solution.py:206
  149.6 1.4 copy.16
  151.0 0.2 reshape.125
  151.3 0.8 fusion.8
  (16 shorter events, 0.1 us)
Async XLA Ops:
  0.0 17.9 %copy-start = (s32[8,2]{0,1:T(2,128)S(1)}, s32[8,2]{0,1:T(2,128)}, u32[]{:S(2)}) copy-start(s32[8,2]{0,1:T(2,128)} %param.13) | copy-start | bytes 196
  0.0 17.8 %copy-start.3 = (f32[1024]{0:T(1024)S(1)}, f32[1024]{0:T(1024)}, u32[]{:S(2)}) copy-start(f32[1024]{0:T(1024)} %param.10) | copy-start | bytes 12292
  0.0 17.9 %copy-start.2 = (s32[1024]{0:T(1024)S(1)}, s32[1024]{0:T(1024)}, u32[]{:S(2)}) copy-start(s32[1024]{0:T(1024)} %param.12) | copy-start | bytes 12292
  0.0 18.0 %copy-start.4 = (f32[100]{0:T(128)S(1)}, f32[100]{0:T(128)}, u32[]{:S(2)}) copy-start(f32[100]{0:T(128)} %param.9) | copy-start | bytes 1204
  0.0 18.2 %copy-start.5 = (s32[100]{0:T(128)S(1)}, s32[100]{0:T(128)}, u32[]{:S(2)}) copy-start(s32[100]{0:T(128)} %param.11) | copy-start | bytes 1204
  0.9 4.3 %collective-permute-start = (bf16[32,1024]{1,0:T(8,128)(2,1)S(1)}, bf16[32,1024]{1,0:T(8,128)(2,1)S(1)}, u32[]{:S(2)}, u32[]{:S(2)}) collective-permute-start(bf16[32,1024]{1,0:T(8,128)(2,1)S(1)} %get-tuple-element.15), channel_id=1, source_target_pairs={{64,0},{96,32},{0,64},{32,96},{65,1},{97,33},{1,65},{33,97},{66,2}... | collective-permute-start | bytes 196616 | tf_op jit(solution)/shard_map/ppermute | solution.py:14
  6.9 41.3 %all-to-all-start.1 = ((bf16[32,32,1024]{2,1,0:T(8,128)(2,1)}), bf16[32,32,1024]{2,1,0:T(8,128)(2,1)S(1)}, u32[]{:S(2)}, u32[]{:S(2)}) async-start(bf16[32,32,1024]{2,1,0:T(8,128)(2,1)} %broadcast_in_dim.63), calls=%async_computation.1 | async-start | bytes 4194304 | tf_op jit(solution)/shard_map/all_to_all | solution.py:234
  48.2 2.0 %copy-start.1 = (bf16[32,32,1024]{2,1,0:T(8,128)(2,1)}, bf16[32,32,1024]{2,1,0:T(8,128)(2,1)S(1)}, u32[]{:S(2)}) copy-start(bf16[32,32,1024]{2,1,0:T(8,128)(2,1)S(1)} %all-to-all-done.1) | copy-start | bytes 6291460
  50.2 34.7 %all-to-all-start = ((bf16[32,32,1024]{2,1,0:T(8,128)(2,1)}), bf16[32,32,1024]{2,1,0:T(8,128)(2,1)S(1)}, u32[]{:S(2)}, u32[]{:S(2)}) async-start(bf16[32,32,1024]{2,1,0:T(8,128)(2,1)} %broadcast_in_dim.62), calls=%async_computation | async-start | bytes 4194304 | tf_op jit(solution)/shard_map/all_to_all | solution.py:234

commit v17 on v16

--- a/solution.py
+++ b/solution.py
@@ -131,7 +131,7 @@
     n = lax.axis_size(vir_axis)
     width = factors.shape[1]
     rows = width // n
-    groups = 4
+    groups = 8
     span = (n // groups) * rows
     arrived = pl.pallas_call(
         functools.partial(_turned_scatter_kernel, n, groups),

time: 154 us -> 168 us (1.091)
  Pallas kernels: 63.4 us -> 78.7 us
    pallas_call x1, Pallas kernels: 49.1 us -> 61.2 us  [turned_rows(): pl.pallas_call(functools.partial(_turned_scatter_kernel, n, groups), out_...]
    pallas_call x1, Pallas kernels: 14.3 us -> 17.5 us  [partner_transpose(): pl.pallas_call(functools.partial(_turn_kernel, n), out_shape=jax.ShapeDty...]
  transfers between devices with their start and end apart: 3 -> 3, of which waited for: 3 -> 3; matrix products, arithmetic and copies ran while one was open for 14% -> 13% of each run, Pallas kernels for 0% -> 0%
where the time goes in v17:
time: 168 us; the launch traced here: 167 us
  Pallas kernels  78.7 us (47%)
  waiting for transfers between devices  42.5 us (25%)
  matrix products  20.3 us (12%)
  starting transfers between devices  16.6 us (10%)
  local copies, waits for them, and re-layouts  6.42 us (4%)
  other arithmetic  2.7 us (2%)
    pallas_call x1, Pallas kernels, turned_rows(): pl.pallas_call(functools.partial(_turned_scatter_kernel, n, groups), out_...  61.2 us
    all_to_all x2, waiting for transfers between devices, gather_rows(): lax.all_to_all(spread, 'vir', split_axis=0, concat_axis=0, tiled=True)  39.9 us
    dot_general x1, matrix products, per_device(): jnp.einsum('qac,qbc->ab', factors, halves_first, preferred_element_type=j...  20.3 us
    pallas_call x1, Pallas kernels, partner_transpose(): pl.pallas_call(functools.partial(_turn_kernel, n), out_shape=jax.ShapeDty...  17.5 us
    all_to_all x2, starting transfers between devices, gather_rows(): lax.all_to_all(spread, 'vir', split_axis=0, concat_axis=0, tiled=True)  14.9 us
  transfers between devices with their start and end apart: 3, of which 3 were waited for; matrix products, arithmetic and copies ran while one was open for 13% of the time, Pallas kernels for 0%

profile of v17, /device:TPU:0, one launch (start us, length us, event | category | flops | bytes accessed | tf_op | source)
XLA Modules:
  0.0 167.4 jit_solution(9180322922547980304)
XLA Ops:
  0.0 0.9 select_bitcast_fusion
  0.9 1.7 %collective-permute-start = (bf16[32,1024]{1,0:T(8,128)(2,1)S(1)}, bf16[32,1024]{1,0:T(8,128)(2,1)S(1)}, u32[]{:S(2)}, u32[]{:S(2)}) collective-permute-start(bf16[32,1024]{1,0:T(8,128)(2,1)S(1)} %get-tuple-element.15), channel_id=1, source_target_pairs={{64,0},{96,32},{0,64},{32,96},{65,1},{97,33},{1,65},{33,97},{66,2}... | collective-permute-start | bytes 196616 | tf_op jit(solution)/shard_map/ppermute | solution.py:14
  2.7 2.6 %collective-permute-done = bf16[32,1024]{1,0:T(8,128)(2,1)S(1)} collective-permute-done((bf16[32,1024]{1,0:T(8,128)(2,1)S(1)}, bf16[32,1024]{1,0:T(8,128)(2,1)S(1)}, u32[]{:S(2)}, u32[]{:S(2)}) %collective-permute-start) | collective-permute-done | bytes 65568 | tf_op jit(solution)/shard_map/ppermute | solution.py:14
  5.3 1.6 broadcast_in_dim.63
  6.9 10.9 %all-to-all-start.1 = ((bf16[32,32,1024]{2,1,0:T(8,128)(2,1)}), bf16[32,32,1024]{2,1,0:T(8,128)(2,1)S(1)}, u32[]{:S(2)}, u32[]{:S(2)}) async-start(bf16[32,32,1024]{2,1,0:T(8,128)(2,1)} %broadcast_in_dim.63), calls=%async_computation.1 | async-start | bytes 4194304 | tf_op jit(solution)/shard_map/all_to_all | solution.py:234
  17.8 0.1 dynamic_slice.11
  17.9 0.1 dynamic_slice.10
  17.9 0.1 constant_dynamic-slice_fusion
  18.0 0.2 select_reduce_fusion
  18.3 0.2 select_reduce_fusion.2
  18.6 0.1 broadcast_add_fusion
  18.6 29.5 %all-to-all-done.1 = bf16[32,32,1024]{2,1,0:T(8,128)(2,1)S(1)} async-done(((bf16[32,32,1024]{2,1,0:T(8,128)(2,1)}), bf16[32,32,1024]{2,1,0:T(8,128)(2,1)S(1)}, u32[]{:S(2)}, u32[]{:S(2)}) %all-to-all-start.1) | async-done | bytes 2097184 | tf_op jit(solution)/shard_map/all_to_all | solution.py:234
  48.2 1.8 %broadcast_in_dim.62 = bf16[32,32,1024]{2,1,0:T(8,128)(2,1)} broadcast(bf16[32,1024]{1,0:T(8,128)(2,1)S(1)} %collective-permute-done), dimensions={1,2} | broadcast | bytes 2162688 | tf_op jit(solution)/shard_map/broadcast_in_dim | solution.py:233
  49.9 0.2 copy-done.1
  50.2 4.0 %all-to-all-start = ((bf16[32,32,1024]{2,1,0:T(8,128)(2,1)}), bf16[32,32,1024]{2,1,0:T(8,128)(2,1)S(1)}, u32[]{:S(2)}, u32[]{:S(2)}) async-start(bf16[32,32,1024]{2,1,0:T(8,128)(2,1)} %broadcast_in_dim.62), calls=%async_computation | async-start | bytes 4194304 | tf_op jit(solution)/shard_map/all_to_all | solution.py:234
  54.2 20.3 %fusion.5.direct_ref = f32[1024,1024]{1,0:T(8,128)} fusion(bf16[3,1024,1024]{2,1,0:T(8,128)(2,1)} %factors_ref.1, bf16[1024,1024,1]{1,0,2:T(8,128)(2,1)} %bitcast.33), kind=kOutput, calls=%fused_computation.5 | convolution fusion | flops 12888047616 | bytes 12582912 | tf_op jit(solution)/shard_map/qac,qbc->ab/dot_general | solution.py:242
  74.5 10.4 %all-to-all-done = bf16[32,32,1024]{2,1,0:T(8,128)(2,1)S(1)} async-done(((bf16[32,32,1024]{2,1,0:T(8,128)(2,1)}), bf16[32,32,1024]{2,1,0:T(8,128)(2,1)S(1)}, u32[]{:S(2)}, u32[]{:S(2)}) %all-to-all-start) | async-done | bytes 2097184 | tf_op jit(solution)/shard_map/all_to_all | solution.py:234
  84.9 61.2 %shard_map.73 = bf16[32,32,1024]{2,1,0:T(8,128)(2,1)S(1)} custom-call(bf16[3,1024,1024]{2,1,0:T(8,128)(2,1)} %factors_ref.1, bf16[1024,1024]{1,0:T(8,128)(2,1)S(1)} %bitcast.31, f32[1024,1024]{1,0:T(8,128)} %fusion.5.direct_ref), custom_call_target="tpu_custom_call" | custom-call | tf_op jit(solution)/shard_map/pallas_call | solution.py:136
  146.1 0.4 convert_reduce_fusion
  146.4 1.0 copy.15
  147.4 17.5 %shard_map.74 = f32[32,32,32]{2,1,0:T(8,128)} custom-call(f32[32,32,32]{2,1,0:T(8,128)} %bitcast.32), custom_call_target="tpu_custom_call" | custom-call | tf_op jit(solution)/shard_map/pallas_call | solution.py:206
  165.0 1.4 copy.16
  166.3 0.2 reshape.125
  166.6 0.8 fusion.8
  (16 shorter events, 0.1 us)
Async XLA Ops:
  0.0 17.9 %copy-start = (s32[8,2]{0,1:T(2,128)S(1)}, s32[8,2]{0,1:T(2,128)}, u32[]{:S(2)}) copy-start(s32[8,2]{0,1:T(2,128)} %param.13) | copy-start | bytes 196
  0.0 17.8 %copy-start.3 = (f32[1024]{0:T(1024)S(1)}, f32[1024]{0:T(1024)}, u32[]{:S(2)}) copy-start(f32[1024]{0:T(1024)} %param.10) | copy-start | bytes 12292
  0.0 17.9 %copy-start.2 = (s32[1024]{0:T(1024)S(1)}, s32[1024]{0:T(1024)}, u32[]{:S(2)}) copy-start(s32[1024]{0:T(1024)} %param.12) | copy-start | bytes 12292
  0.0 18.0 %copy-start.4 = (f32[100]{0:T(128)S(1)}, f32[100]{0:T(128)}, u32[]{:S(2)}) copy-start(f32[100]{0:T(128)} %param.9) | copy-start | bytes 1204
  0.0 18.2 %copy-start.5 = (s32[100]{0:T(128)S(1)}, s32[100]{0:T(128)}, u32[]{:S(2)}) copy-start(s32[100]{0:T(128)} %param.11) | copy-start | bytes 1204
  0.9 4.3 %collective-permute-start = (bf16[32,1024]{1,0:T(8,128)(2,1)S(1)}, bf16[32,1024]{1,0:T(8,128)(2,1)S(1)}, u32[]{:S(2)}, u32[]{:S(2)}) collective-permute-start(bf16[32,1024]{1,0:T(8,128)(2,1)S(1)} %get-tuple-element.15), channel_id=1, source_target_pairs={{64,0},{96,32},{0,64},{32,96},{65,1},{97,33},{1,65},{33,97},{66,2}... | collective-permute-start | bytes 196616 | tf_op jit(solution)/shard_map/ppermute | solution.py:14
  6.9 41.3 %all-to-all-start.1 = ((bf16[32,32,1024]{2,1,0:T(8,128)(2,1)}), bf16[32,32,1024]{2,1,0:T(8,128)(2,1)S(1)}, u32[]{:S(2)}, u32[]{:S(2)}) async-start(bf16[32,32,1024]{2,1,0:T(8,128)(2,1)} %broadcast_in_dim.63), calls=%async_computation.1 | async-start | bytes 4194304 | tf_op jit(solution)/shard_map/all_to_all | solution.py:234
  48.2 2.0 %copy-start.1 = (bf16[32,32,1024]{2,1,0:T(8,128)(2,1)}, bf16[32,32,1024]{2,1,0:T(8,128)(2,1)S(1)}, u32[]{:S(2)}) copy-start(bf16[32,32,1024]{2,1,0:T(8,128)(2,1)S(1)} %all-to-all-done.1) | copy-start | bytes 6291460
  50.2 34.7 %all-to-all-start = ((bf16[32,32,1024]{2,1,0:T(8,128)(2,1)}), bf16[32,32,1024]{2,1,0:T(8,128)(2,1)S(1)}, u32[]{:S(2)}, u32[]{:S(2)}) async-start(bf16[32,32,1024]{2,1,0:T(8,128)(2,1)} %broadcast_in_dim.62), calls=%async_computation | async-start | bytes 4194304 | tf_op jit(solution)/shard_map/all_to_all | solution.py:234

commit v18 on v16

--- a/solution.py
+++ b/solution.py
@@ -14,7 +14,7 @@
     return lax.ppermute(block, axis, route)
 
 
-def _turned_scatter_kernel(n, groups, factors_ref, other_ref, direct_ref, out_ref, hbuf, cbuf, send_sems, recv_sems, own_sem):
+def _turned_scatter_kernel(n, groups, factors_ref, flipped_ref, other_ref, direct_ref, out_ref, hbuf, cbuf, send_sems, recv_sems, own_sem):
     me = lax.axis_index("vir")
     group = lax.axis_index("occ")
     q_count = factors_ref.shape[0]
@@ -77,9 +77,9 @@
         def halves(t, carry):
             col0 = pl.multiple_of(t * tile, tile)
             for q in range(q_count):
-                product = lax.dot_general(
-                    factors_ref[q, pl.ds(row0, span), :], other_ref[pl.ds(col0, tile), :],
-                    dims, preferred_element_type=jnp.float32,
+                product = jnp.dot(
+                    factors_ref[q, pl.ds(row0, span), :], other_ref[:, pl.ds(col0, tile)],
+                    preferred_element_type=jnp.float32,
                 )
                 hbuf[q, :, pl.ds(col0, tile)] = product.astype(hbuf.dtype)
             return carry
@@ -90,9 +90,8 @@
             col0 = pl.multiple_of(t * tile, tile)
             acc = direct_ref[pl.ds(row0, span), pl.ds(col0, tile)]
             for q in range(q_count):
-                acc += lax.dot_general(
-                    hbuf[q], factors_ref[q, pl.ds(col0, tile), :],
-                    dims, preferred_element_type=jnp.float32,
+                acc += jnp.dot(
+                    hbuf[q], flipped_ref[q, :, pl.ds(col0, tile)], preferred_element_type=jnp.float32
                 )
             cbuf[slot, :, pl.ds(col0, tile)] = acc.astype(cbuf.dtype)
             return carry
@@ -136,7 +135,7 @@
     arrived = pl.pallas_call(
         functools.partial(_turned_scatter_kernel, n, groups),
         out_shape=jax.ShapeDtypeStruct((n, rows, width), jnp.bfloat16),
-        in_specs=[pl.BlockSpec(memory_space=pltpu.VMEM)] * 3,
+        in_specs=[pl.BlockSpec(memory_space=pltpu.VMEM)] * 4,
         out_specs=pl.BlockSpec(memory_space=pl.ANY),
         scratch_shapes=[
             pltpu.VMEM((factors.shape[0], span, width), jnp.bfloat16),
@@ -148,7 +147,7 @@
         compiler_params=pltpu.CompilerParams(
             collective_id=0, has_side_effects=True, vmem_limit_bytes=48 * 1024 * 1024
         ),
-    )(factors, other_rows, direct)
+    )(factors, jnp.transpose(factors, (0, 2, 1)), jnp.transpose(other_rows, (1, 0)), direct)
     return jnp.sum(arrived.astype(jnp.float32), axis=0)
 
 

time: 154 us -> 173 us (1.12)
  blocking collectives: 0 us -> 40.2 us
  waiting for transfers between devices: 42.5 us -> 19.3 us
  starting transfers between devices: 16.6 us -> 6.5 us
  local copies, waits for them, and re-layouts: 6.42 us -> 16.3 us
  Pallas kernels: 63.4 us -> 65.7 us
    all_to_all x0 -> x1, blocking collectives: none -> 40.2 us  [gather_rows(): lax.all_to_all(spread, 'vir', split_axis=0, concat_axis=0, tiled=True)]
    all_to_all x2 -> x1, waiting for transfers between devices: 39.9 us -> 16.7 us  [gather_rows(): lax.all_to_all(spread, 'vir', split_axis=0, concat_axis=0, tiled=True)]
    all_to_all x2 -> x1, starting transfers between devices: 14.9 us -> 4.76 us  [gather_rows(): lax.all_to_all(spread, 'vir', split_axis=0, concat_axis=0, tiled=True)]
    unnamed x12 -> x11, local copies, waits for them, and re-layouts: 0.27 us -> 8.71 us
    reshape x0 -> x1, local copies, waits for them, and re-layouts: none -> 2.86 us  [gather_rows(): return pieces.reshape(vir_devices * row_count, block.shape[-1])]
    pallas_call x1, Pallas kernels: 49.1 us -> 50.9 us  [turned_rows(): pl.pallas_call(functools.partial(_turned_scatter_kernel, n, groups), out_...]
  transfers between devices with their start and end apart: 3 -> 2, of which waited for: 3 -> 2; matrix products, arithmetic and copies ran while one was open for 14% -> 7% of each run, Pallas kernels for 0% -> 0%
where the time goes in v18:
time: 173 us; the launch traced here: 171 us
  Pallas kernels  65.7 us (38%)
  blocking collectives  40.2 us (23%)
  matrix products  20.4 us (12%)
  waiting for transfers between devices  19.3 us (11%)
  local copies, waits for them, and re-layouts  16.3 us (9%)
  starting transfers between devices  6.5 us (4%)
  other arithmetic  2.7 us (2%)
    pallas_call x1, Pallas kernels, turned_rows(): pl.pallas_call(functools.partial(_turned_scatter_kernel, n, groups), out_...  50.9 us
    all_to_all x1, blocking collectives, gather_rows(): lax.all_to_all(spread, 'vir', split_axis=0, concat_axis=0, tiled=True)  40.2 us
    dot_general x1, matrix products, per_device(): jnp.einsum('qac,qbc->ab', factors, halves_first, preferred_element_type=j...  20.4 us
    all_to_all x1, waiting for transfers between devices, gather_rows(): lax.all_to_all(spread, 'vir', split_axis=0, concat_axis=0, tiled=True)  16.7 us
    pallas_call x1, Pallas kernels, partner_transpose(): pl.pallas_call(functools.partial(_turn_kernel, n), out_shape=jax.ShapeDty...  14.7 us
    unnamed x11, local copies, waits for them, and re-layouts  8.71 us
    all_to_all x1, starting transfers between devices, gather_rows(): lax.all_to_all(spread, 'vir', split_axis=0, concat_axis=0, tiled=True)  4.76 us
  transfers between devices with their start and end apart: 2, of which 2 were waited for; matrix products, arithmetic and copies ran while one was open for 7% of the time, Pallas kernels for 0%

profile of v18, /device:TPU:0, one launch (start us, length us, event | category | flops | bytes accessed | tf_op | source)
XLA Modules:
  0.0 171.2 jit_solution(11163420437923825958)
XLA Ops:
  0.0 0.9 select_bitcast_fusion
  0.9 1.7 %collective-permute-start = (bf16[32,1024]{1,0:T(8,128)(2,1)S(1)}, bf16[32,1024]{1,0:T(8,128)(2,1)S(1)}, u32[]{:S(2)}, u32[]{:S(2)}) collective-permute-start(bf16[32,1024]{1,0:T(8,128)(2,1)S(1)} %get-tuple-element.15), channel_id=1, source_target_pairs={{64,0},{96,32},{0,64},{32,96},{65,1},{97,33},{1,65},{33,97},{66,2}... | collective-permute-start | bytes 196616 | tf_op jit(solution)/shard_map/ppermute | solution.py:14
  2.6 2.6 %collective-permute-done = bf16[32,1024]{1,0:T(8,128)(2,1)S(1)} collective-permute-done((bf16[32,1024]{1,0:T(8,128)(2,1)S(1)}, bf16[32,1024]{1,0:T(8,128)(2,1)S(1)}, u32[]{:S(2)}, u32[]{:S(2)}) %collective-permute-start) | collective-permute-done | bytes 65568 | tf_op jit(solution)/shard_map/ppermute | solution.py:14
  5.2 0.2 broadcast_in_dim.62
  5.5 40.2 %all_to_all.10 = bf16[32,32,1024]{2,1,0:T(8,128)(2,1)} all-to-all(bf16[32,32,1024]{2,1,0:T(8,128)(2,1)S(1)} %broadcast_in_dim.62), channel_id=1, replica_groups=mesh['occ'=4,'vir'=32] {'vir'}, dimensions={0} | all-to-all | bytes 4194304 | tf_op jit(solution)/shard_map/all_to_all | solution.py:233
  45.7 1.7 broadcast_in_dim.63
  47.4 4.8 %all-to-all-start.1 = ((bf16[32,32,1024]{2,1,0:T(8,128)(2,1)}), bf16[32,32,1024]{2,1,0:T(8,128)(2,1)}, u32[]{:S(2)}, u32[]{:S(2)}) async-start(bf16[32,32,1024]{2,1,0:T(8,128)(2,1)} %broadcast_in_dim.63), calls=%async_computation.1 | async-start | bytes 4194304 | tf_op jit(solution)/shard_map/all_to_all | solution.py:233
  52.2 8.7 %copy.17 = bf16[3,1024,1024]{1,2,0:T(8,128)(2,1)} copy(bf16[3,1024,1024]{2,1,0:T(8,128)(2,1)} %factors_ref.1) | data formatting | bytes 12582912 | tf_op args[1]
  60.9 0.1 dynamic_slice.11
  60.9 0.1 dynamic_slice.10
  61.0 0.1 constant_dynamic-slice_fusion
  61.1 0.2 select_reduce_fusion
  61.3 0.2 select_reduce_fusion.2
  61.6 0.1 broadcast_add_fusion
  61.7 2.9 %copy.18 = bf16[1024,1024]{0,1:T(8,128)(2,1)S(1)} copy(bf16[1024,1024]{1,0:T(8,128)(2,1)} %bitcast.35) | data formatting | bytes 4194304 | tf_op jit(solution)/shard_map/reshape | solution.py:234
  64.6 16.7 %all-to-all-done.1 = bf16[32,32,1024]{2,1,0:T(8,128)(2,1)} async-done(((bf16[32,32,1024]{2,1,0:T(8,128)(2,1)}), bf16[32,32,1024]{2,1,0:T(8,128)(2,1)}, u32[]{:S(2)}, u32[]{:S(2)}) %all-to-all-start.1) | async-done | bytes 2097184 | tf_op jit(solution)/shard_map/all_to_all | solution.py:233
  81.3 20.4 %fusion.5.direct_ref = f32[1024,1024]{1,0:T(8,128)} fusion(bf16[3,1024,1024]{2,1,0:T(8,128)(2,1)} %factors_ref.1, bf16[1024,1024,1]{1,0,2:T(8,128)(2,1)} %bitcast.8), kind=kOutput, calls=%fused_computation.5 | convolution fusion | flops 12888047616 | bytes 12582912 | tf_op jit(solution)/shard_map/qac,qbc->ab/dot_general | solution.py:241
  101.7 50.9 %shard_map.73 = bf16[32,32,1024]{2,1,0:T(8,128)(2,1)S(1)} custom-call(bf16[3,1024,1024]{2,1,0:T(8,128)(2,1)} %factors_ref.1, bf16[3,1024,1024]{2,1,0:T(8,128)(2,1)} %bitcast.34, bf16[1024,1024]{1,0:T(8,128)(2,1)S(1)} %bitcast.33, f32[1024,1024]{1,0:T(8,128)} %fusion.5.direct_ref), custom_call_target="tpu_custom_call" | custom-call | tf_op jit(solution)/shard_map/pallas_call | solution.py:135
  152.6 0.4 convert_reduce_fusion
  153.0 1.0 copy.21
  154.0 14.7 %shard_map.74 = f32[32,32,32]{2,1,0:T(8,128)} custom-call(f32[32,32,32]{2,1,0:T(8,128)} %bitcast.36), custom_call_target="tpu_custom_call" | custom-call | tf_op jit(solution)/shard_map/pallas_call | solution.py:205
  168.7 1.4 copy.22
  170.1 0.2 reshape.125
  170.4 0.8 fusion.8
  (15 shorter events, 0.1 us)
Async XLA Ops:
  0.0 61.0 %copy-start = (s32[8,2]{0,1:T(2,128)S(1)}, s32[8,2]{0,1:T(2,128)}, u32[]{:S(2)}) copy-start(s32[8,2]{0,1:T(2,128)} %param.13) | copy-start | bytes 196
  0.9 4.3 %collective-permute-start = (bf16[32,1024]{1,0:T(8,128)(2,1)S(1)}, bf16[32,1024]{1,0:T(8,128)(2,1)S(1)}, u32[]{:S(2)}, u32[]{:S(2)}) collective-permute-start(bf16[32,1024]{1,0:T(8,128)(2,1)S(1)} %get-tuple-element.15), channel_id=1, source_target_pairs={{64,0},{96,32},{0,64},{32,96},{65,1},{97,33},{1,65},{33,97},{66,2}... | collective-permute-start | bytes 196616 | tf_op jit(solution)/shard_map/ppermute | solution.py:14
  47.4 33.9 %all-to-all-start.1 = ((bf16[32,32,1024]{2,1,0:T(8,128)(2,1)}), bf16[32,32,1024]{2,1,0:T(8,128)(2,1)}, u32[]{:S(2)}, u32[]{:S(2)}) async-start(bf16[32,32,1024]{2,1,0:T(8,128)(2,1)} %broadcast_in_dim.63), calls=%async_computation.1 | async-start | bytes 4194304 | tf_op jit(solution)/shard_map/all_to_all | solution.py:233
  52.1 8.7 %copy-start.2 = (f32[1024]{0:T(1024)S(1)}, f32[1024]{0:T(1024)}, u32[]{:S(2)}) copy-start(f32[1024]{0:T(1024)} %param.10) | copy-start | bytes 12292
  52.2 8.8 %copy-start.1 = (s32[1024]{0:T(1024)S(1)}, s32[1024]{0:T(1024)}, u32[]{:S(2)}) copy-start(s32[1024]{0:T(1024)} %param.12) | copy-start | bytes 12292
  52.2 8.9 %copy-start.3 = (f32[100]{0:T(128)S(1)}, f32[100]{0:T(128)}, u32[]{:S(2)}) copy-start(f32[100]{0:T(128)} %param.9) | copy-start | bytes 1204
  52.2 9.2 %copy-start.4 = (s32[100]{0:T(128)S(1)}, s32[100]{0:T(128)}, u32[]{:S(2)}) copy-start(s32[100]{0:T(128)} %param.11) | copy-start | bytes 1204

commit v19 on v13

--- a/solution.py
+++ b/solution.py
@@ -88,19 +88,21 @@
 
     own = jnp.where(lower_half, amplitudes[0], amplitudes[1])
     outgoing = jnp.where(lower_half, amplitudes[1], amplitudes[0])
+    spread_own = jnp.broadcast_to(own[None], (vir_devices,) + own.shape)
     other = passed_along(outgoing, "occ", occ_devices // 2)
+    spread_other = jnp.broadcast_to(other[None], (vir_devices,) + other.shape)
+    spread_own, spread_other = lax.optimization_barrier((spread_own, spread_other))
 
-    def gather_rows(block):
-        spread = jnp.broadcast_to(block[None], (vir_devices,) + block.shape)
+    def gather_rows(spread):
         pieces = lax.all_to_all(spread, "vir", split_axis=0, concat_axis=0, tiled=True)
-        return pieces.reshape(vir_devices * row_count, block.shape[-1])
+        return pieces.reshape(vir_devices * row_count, spread.shape[-1])
 
     def half_products(rows):
         product = jnp.einsum("cd,qbd->qbc", rows, factors, preferred_element_type=jnp.float32)
         return product.astype(jnp.bfloat16)
 
-    halves_first = half_products(gather_rows(own))
-    halves_second = half_products(gather_rows(other))
+    halves_first = half_products(gather_rows(spread_own))
+    halves_second = half_products(gather_rows(spread_other))
     direct = jnp.einsum("qac,qbc->ab", factors, halves_first, preferred_element_type=jnp.float32)
     turned_term = jnp.einsum("qac,qbc->ab", halves_second, factors, preferred_element_type=jnp.float32)
     combined = direct + turned_term

time: 155 us -> 150 us (0.968)
  blocking collectives: 0 us -> 40.2 us
  waiting for transfers between devices: 73 us -> 41.1 us
  starting transfers between devices: 21.3 us -> 9.91 us
    all_to_all x0 -> x1, blocking collectives: none -> 40.2 us  [gather_rows(): lax.all_to_all(spread, 'vir', split_axis=0, concat_axis=0, tiled=True)]
    all_to_all x2 -> x1, waiting for transfers between devices: 28.2 us -> 8.81 us  [gather_rows(): lax.all_to_all(spread, 'vir', split_axis=0, concat_axis=0, tiled=True)]
    ppermute x1, waiting for transfers between devices: 15.1 us -> 2.61 us  [passed_along(): return lax.ppermute(block, axis, route)]
    all_to_all x2 -> x1, starting transfers between devices: 16.4 us -> 4.01 us  [gather_rows(): lax.all_to_all(spread, 'vir', split_axis=0, concat_axis=0, tiled=True)]
  transfers between devices with their start and end apart: 4 -> 3, of which waited for: 4 -> 3; matrix products, arithmetic and copies ran while one was open for 13% -> 14% of each run, Pallas kernels for 0% -> 0%
where the time goes in v19:
time: 150 us
  waiting for transfers between devices  41.1 us (27%)
  blocking collectives  40.2 us (27%)
  matrix products  39.1 us (26%)
  Pallas kernels  12.1 us (8%)
  starting transfers between devices  9.91 us (7%)
  local copies, waits for them, and re-layouts  4.67 us (3%)
  other arithmetic  2.71 us (2%)
    all_to_all x1, blocking collectives, gather_rows(): lax.all_to_all(spread, 'vir', split_axis=0, concat_axis=0, tiled=True)  40.2 us
    all_to_all x1, waiting for transfers between devices, per_device(): lax.all_to_all(blocks, 'vir', split_axis=0, concat_axis=0, tiled=True)  29.7 us
    dot_general x1, matrix products, per_device(): jnp.einsum('qac,qbc->ab', factors, halves_first, preferred_element_type=j...  20.3 us
    dot_general x1, matrix products, per_device(): jnp.einsum('qac,qbc->ab', halves_second, factors, preferred_element_type=...  18.8 us
    pallas_call x1, Pallas kernels, partner_transpose(): pl.pallas_call(functools.partial(_turn_kernel, n), out_shape=jax.ShapeDty...  12.1 us
    all_to_all x1, waiting for transfers between devices, gather_rows(): lax.all_to_all(spread, 'vir', split_axis=0, concat_axis=0, tiled=True)  8.81 us
    all_to_all x1, starting transfers between devices, per_device(): lax.all_to_all(blocks, 'vir', split_axis=0, concat_axis=0, tiled=True)  4.15 us
    all_to_all x1, starting transfers between devices, gather_rows(): lax.all_to_all(spread, 'vir', split_axis=0, concat_axis=0, tiled=True)  4.01 us
  transfers between devices with their start and end apart: 3, of which 3 were waited for; matrix products, arithmetic and copies ran while one was open for 14% of the time, Pallas kernels for 0%

profile of v19, /device:TPU:0, one launch (start us, length us, event | category | flops | bytes accessed | tf_op | source)
XLA Modules:
  0.0 150.0 jit_solution(2129080588876601757)
XLA Ops:
  0.0 0.9 select_bitcast_fusion
  0.9 1.7 %collective-permute-start = (bf16[32,1024]{1,0:T(8,128)(2,1)S(1)}, bf16[32,1024]{1,0:T(8,128)(2,1)S(1)}, u32[]{:S(2)}, u32[]{:S(2)}) collective-permute-start(bf16[32,1024]{1,0:T(8,128)(2,1)S(1)} %get-tuple-element.15), channel_id=1, source_target_pairs={{64,0},{96,32},{0,64},{32,96},{65,1},{97,33},{1,65},{33,97},{66,2}... | collective-permute-start | bytes 196616 | tf_op jit(solution)/shard_map/ppermute | solution.py:14
  2.6 2.6 %collective-permute-done = bf16[32,1024]{1,0:T(8,128)(2,1)S(1)} collective-permute-done((bf16[32,1024]{1,0:T(8,128)(2,1)S(1)}, bf16[32,1024]{1,0:T(8,128)(2,1)S(1)}, u32[]{:S(2)}, u32[]{:S(2)}) %collective-permute-start) | collective-permute-done | bytes 65568 | tf_op jit(solution)/shard_map/ppermute | solution.py:14
  5.2 0.2 broadcast_in_dim.65
  5.5 1.6 %broadcast_in_dim.66 = bf16[32,32,1024]{2,1,0:T(8,128)(2,1)} broadcast(bf16[32,1024]{1,0:T(8,128)(2,1)S(1)} %collective-permute-done), dimensions={1,2} | broadcast | bytes 2162688 | tf_op jit(solution)/shard_map/broadcast_in_dim | solution.py:93
  7.1 40.2 %all_to_all.15 = bf16[32,32,1024]{2,1,0:T(8,128)(2,1)} all-to-all(bf16[32,32,1024]{2,1,0:T(8,128)(2,1)S(1)} %broadcast_in_dim.65), channel_id=1, replica_groups=mesh['occ'=4,'vir'=32] {'vir'}, dimensions={0} | all-to-all | bytes 4194304 | tf_op jit(solution)/shard_map/all_to_all | solution.py:97
  47.3 4.0 %all-to-all-start.1 = ((bf16[32,32,1024]{2,1,0:T(8,128)(2,1)}), bf16[32,32,1024]{2,1,0:T(8,128)(2,1)S(1)}, u32[]{:S(2)}, u32[]{:S(2)}) async-start(bf16[32,32,1024]{2,1,0:T(8,128)(2,1)} %broadcast_in_dim.66), calls=%async_computation.1 | async-start | bytes 4194304 | tf_op jit(solution)/shard_map/all_to_all | solution.py:97
  51.3 20.3 %fusion.2 = f32[1024,1024,1]{0,1,2:T(8,128)} fusion(bf16[3,1024,1024]{2,1,0:T(8,128)(2,1)} %param.8, bf16[1024,1024,1]{1,0,2:T(8,128)(2,1)} %bitcast.47), kind=kOutput, calls=%fused_computation.2 | convolution fusion | flops 12888047616 | bytes 12582912 | tf_op jit(solution)/shard_map/qac,qbc->ab/dot_general | solution.py:106
  71.6 8.8 %all-to-all-done.1 = bf16[32,32,1024]{2,1,0:T(8,128)(2,1)S(1)} async-done(((bf16[32,32,1024]{2,1,0:T(8,128)(2,1)}), bf16[32,32,1024]{2,1,0:T(8,128)(2,1)S(1)}, u32[]{:S(2)}, u32[]{:S(2)}) %all-to-all-start.1) | async-done | bytes 2097184 | tf_op jit(solution)/shard_map/all_to_all | solution.py:97
  80.5 18.8 %fusion.6 = bf16[1024,1024]{1,0:T(8,128)(2,1)} fusion(f32[1024,1024,1]{0,1,2:T(8,128)} %fusion.2, bf16[3,1024,1024]{2,1,0:T(8,128)(2,1)} %param.8, bf16[1024,1024,1]{1,0,2:T(8,128)(2,1)S(1)} %bitcast.46), kind=kOutput, calls=%fused_computation.7 | convolution fusion | flops 12890144768 | bytes 14680064 | tf_op jit(solution)/shard_map/qac,qbc->ab/dot_general | solution.py:107
  99.3 4.2 %all-to-all-start.2 = ((bf16[32,32,1024]{2,1,0:T(8,128)(2,1)}), bf16[32,32,1024]{2,1,0:T(8,128)(2,1)S(1)}, u32[]{:S(2)}, u32[]{:S(2)}) async-start(bf16[32,32,1024]{2,1,0:T(8,128)(2,1)} %bitcast.45), calls=%async_computation.2 | async-start | bytes 4194304 | tf_op jit(solution)/shard_map/all_to_all | solution.py:110
  103.5 0.1 dynamic_slice.11
  103.5 0.1 dynamic_slice.10
  103.7 0.2 select_reduce_fusion
  103.9 0.2 select_reduce_fusion.2
  104.2 0.1 broadcast_xor_fusion
  104.2 0.1 broadcast_add_fusion
  104.3 29.7 %all-to-all-done.2 = bf16[32,32,1024]{2,1,0:T(8,128)(2,1)S(1)} async-done(((bf16[32,32,1024]{2,1,0:T(8,128)(2,1)}), bf16[32,32,1024]{2,1,0:T(8,128)(2,1)S(1)}, u32[]{:S(2)}, u32[]{:S(2)}) %all-to-all-start.2) | async-done | bytes 2097184 | tf_op jit(solution)/shard_map/all_to_all | solution.py:110
  134.0 0.4 convert_reduce_fusion
  134.4 1.0 copy.13
  135.4 12.1 %shard_map.73 = f32[32,32,32]{2,1,0:T(8,128)} custom-call(f32[32,32,32]{2,1,0:T(8,128)} %bitcast.44), custom_call_target="tpu_custom_call" | custom-call | tf_op jit(solution)/shard_map/pallas_call | solution.py:68
  147.5 1.4 copy.14
  148.9 0.2 reshape.124
  149.1 0.8 fusion.13
  (15 shorter events, 0.1 us)
Async XLA Ops:
  0.0 103.6 %copy-start = (s32[8,2]{0,1:T(2,128)S(1)}, s32[8,2]{0,1:T(2,128)}, u32[]{:S(2)}) copy-start(s32[8,2]{0,1:T(2,128)} %param.13) | copy-start | bytes 196
  0.9 4.3 %collective-permute-start = (bf16[32,1024]{1,0:T(8,128)(2,1)S(1)}, bf16[32,1024]{1,0:T(8,128)(2,1)S(1)}, u32[]{:S(2)}, u32[]{:S(2)}) collective-permute-start(bf16[32,1024]{1,0:T(8,128)(2,1)S(1)} %get-tuple-element.15), channel_id=1, source_target_pairs={{64,0},{96,32},{0,64},{32,96},{65,1},{97,33},{1,65},{33,97},{66,2}... | collective-permute-start | bytes 196616 | tf_op jit(solution)/shard_map/ppermute | solution.py:14
  47.3 33.2 %all-to-all-start.1 = ((bf16[32,32,1024]{2,1,0:T(8,128)(2,1)}), bf16[32,32,1024]{2,1,0:T(8,128)(2,1)S(1)}, u32[]{:S(2)}, u32[]{:S(2)}) async-start(bf16[32,32,1024]{2,1,0:T(8,128)(2,1)} %broadcast_in_dim.66), calls=%async_computation.1 | async-start | bytes 4194304 | tf_op jit(solution)/shard_map/all_to_all | solution.py:97
  99.3 4.2 %copy-start.2 = (f32[1024]{0:T(1024)S(1)}, f32[1024]{0:T(1024)}, u32[]{:S(2)}) copy-start(f32[1024]{0:T(1024)} %param.10) | copy-start | bytes 12292
  99.3 4.3 %copy-start.1 = (s32[1024]{0:T(1024)S(1)}, s32[1024]{0:T(1024)}, u32[]{:S(2)}) copy-start(s32[1024]{0:T(1024)} %param.12) | copy-start | bytes 12292
  99.3 4.4 %copy-start.3 = (f32[100]{0:T(128)S(1)}, f32[100]{0:T(128)}, u32[]{:S(2)}) copy-start(f32[100]{0:T(128)} %param.9) | copy-start | bytes 1204
  99.3 4.7 %copy-start.4 = (s32[100]{0:T(128)S(1)}, s32[100]{0:T(128)}, u32[]{:S(2)}) copy-start(s32[100]{0:T(128)} %param.11) | copy-start | bytes 1204
  99.3 34.8 %all-to-all-start.2 = ((bf16[32,32,1024]{2,1,0:T(8,128)(2,1)}), bf16[32,32,1024]{2,1,0:T(8,128)(2,1)S(1)}, u32[]{:S(2)}, u32[]{:S(2)}) async-start(bf16[32,32,1024]{2,1,0:T(8,128)(2,1)} %bitcast.45), calls=%async_computation.2 | async-start | bytes 4194304 | tf_op jit(solution)/shard_map/all_to_all | solution.py:110

commit v20 on v13

--- a/solution.py
+++ b/solution.py
@@ -12,6 +12,45 @@
     devices = range(lax.axis_size(axis))
     route = [((i - distance) % len(devices), i) for i in devices]
     return lax.ppermute(block, axis, route)
+
+
+def _swap_kernel(amps_ref, own_ref, other_ref, sems):
+    group = lax.axis_index("occ")
+    me = lax.axis_index("vir")
+    half = lax.axis_size("occ") // 2
+    partner = lax.rem(group + half, lax.axis_size("occ"))
+    upper = group // half
+    send_sem, recv_sem, local_sem = sems
+
+    barrier = pltpu.get_barrier_semaphore()
+    pl.semaphore_signal(barrier, inc=1, device_id=(partner, me), device_id_type=pl.DeviceIdType.MESH)
+    pl.semaphore_wait(barrier, 1)
+
+    local = pltpu.make_async_copy(amps_ref.at[upper], own_ref, local_sem)
+    local.start()
+    trade = pltpu.make_async_remote_copy(
+        src_ref=amps_ref.at[1 - upper],
+        dst_ref=other_ref,
+        send_sem=send_sem,
+        recv_sem=recv_sem,
+        device_id=(partner, me),
+        device_id_type=pl.DeviceIdType.MESH,
+    )
+    trade.start()
+    trade.wait()
+    local.wait()
+
+
+def swap_pairs(amplitudes):
+    block = jax.ShapeDtypeStruct(amplitudes.shape[1:], amplitudes.dtype)
+    return pl.pallas_call(
+        _swap_kernel,
+        out_shape=(block, block),
+        in_specs=[pl.BlockSpec(memory_space=pl.ANY)],
+        out_specs=(pl.BlockSpec(memory_space=pl.ANY), pl.BlockSpec(memory_space=pl.ANY)),
+        scratch_shapes=[(pltpu.SemaphoreType.DMA, pltpu.SemaphoreType.DMA, pltpu.SemaphoreType.DMA)],
+        compiler_params=pltpu.CompilerParams(collective_id=2, has_side_effects=True),
+    )(amplitudes)
 
 
 def _turn_kernel(n, blocks_ref, out_ref, send_sems, recv_sems):
@@ -86,9 +125,7 @@
     vir_index = lax.axis_index("vir")
     lower_half = occ_index < occ_devices // 2
 
-    own = jnp.where(lower_half, amplitudes[0], amplitudes[1])
-    outgoing = jnp.where(lower_half, amplitudes[1], amplitudes[0])
-    other = passed_along(outgoing, "occ", occ_devices // 2)
+    own, other = swap_pairs(amplitudes)
 
     def gather_rows(block):
         spread = jnp.broadcast_to(block[None], (vir_devices,) + block.shape)

time: 155 us -> 153 us (0.987)
  blocking collectives: 0 us -> 40.7 us
  waiting for transfers between devices: 73 us -> 39.7 us
  starting transfers between devices: 21.3 us -> 8.16 us
  Pallas kernels: 12.1 us -> 16.9 us
    all_to_all x0 -> x1, blocking collectives: none -> 40.7 us  [gather_rows(): lax.all_to_all(spread, 'vir', split_axis=0, concat_axis=0, tiled=True)]
    all_to_all x2 -> x1, waiting for transfers between devices: 28.2 us -> 9.83 us  [gather_rows(): lax.all_to_all(spread, 'vir', split_axis=0, concat_axis=0, tiled=True)]
    ppermute x1 -> x0, waiting for transfers between devices: 15.1 us -> none  [passed_along(): return lax.ppermute(block, axis, route)]
    all_to_all x2 -> x1, starting transfers between devices: 16.4 us -> 4.01 us  [gather_rows(): lax.all_to_all(spread, 'vir', split_axis=0, concat_axis=0, tiled=True)]
    pallas_call x0 -> x1, Pallas kernels: none -> 4.77 us  [swap_pairs(): pl.pallas_call(_swap_kernel, out_shape=(block, block), in_specs=[pl.Block...]
  transfers between devices with their start and end apart: 4 -> 2, of which waited for: 4 -> 2; matrix products, arithmetic and copies ran while one was open for 13% -> 14% of each run, Pallas kernels for 0% -> 0%
where the time goes in v20:
time: 153 us; the launch traced here: 152 us
  blocking collectives  40.7 us (27%)
  waiting for transfers between devices  39.7 us (26%)
  matrix products  39.3 us (26%)
  Pallas kernels  16.9 us (11%)
  starting transfers between devices  8.16 us (5%)
  local copies, waits for them, and re-layouts  5.56 us (4%)
  other arithmetic  1.81 us (1%)
    all_to_all x1, blocking collectives, gather_rows(): lax.all_to_all(spread, 'vir', split_axis=0, concat_axis=0, tiled=True)  40.7 us
    all_to_all x1, waiting for transfers between devices, per_device(): lax.all_to_all(blocks, 'vir', split_axis=0, concat_axis=0, tiled=True)  29.9 us
    dot_general x1, matrix products, per_device(): jnp.einsum('qac,qbc->ab', halves_second, factors, preferred_element_type=...  20.4 us
    dot_general x1, matrix products, per_device(): jnp.einsum('qac,qbc->ab', factors, halves_first, preferred_element_type=j...  18.9 us
    pallas_call x1, Pallas kernels, partner_transpose(): pl.pallas_call(functools.partial(_turn_kernel, n), out_shape=jax.ShapeDty...  12.1 us
    all_to_all x1, waiting for transfers between devices, gather_rows(): lax.all_to_all(spread, 'vir', split_axis=0, concat_axis=0, tiled=True)  9.83 us
    pallas_call x1, Pallas kernels, swap_pairs(): pl.pallas_call(_swap_kernel, out_shape=(block, block), in_specs=[pl.Block...  4.77 us
    all_to_all x1, starting transfers between devices, per_device(): lax.all_to_all(blocks, 'vir', split_axis=0, concat_axis=0, tiled=True)  4.16 us
  transfers between devices with their start and end apart: 2, of which 2 were waited for; matrix products, arithmetic and copies ran while one was open for 14% of the time, Pallas kernels for 0%

profile of v20, /device:TPU:0, one launch (start us, length us, event | category | flops | bytes accessed | tf_op | source)
XLA Modules:
  0.0 152.3 jit_solution(3020619304214738601)
XLA Ops:
  0.0 4.8 %shard_map.73 = (bf16[32,1024]{1,0:T(8,128)(2,1)}, bf16[32,1024]{1,0:T(8,128)(2,1)}) custom-call(bf16[2,32,1024]{2,1,0:T(8,128)(2,1)} %amps_ref.1), custom_call_target="tpu_custom_call" | custom-call | tf_op jit(solution)/shard_map/pallas_call | solution.py:46
  4.8 1.1 broadcast_in_dim.63
  5.9 40.7 %all_to_all.15 = bf16[32,32,1024]{2,1,0:T(8,128)(2,1)} all-to-all(bf16[32,32,1024]{2,1,0:T(8,128)(2,1)S(1)} %broadcast_in_dim.63), channel_id=1, replica_groups=mesh['occ'=4,'vir'=32] {'vir'}, dimensions={0} | all-to-all | bytes 4194304 | tf_op jit(solution)/shard_map/all_to_all | solution.py:132
  46.6 1.6 %broadcast_in_dim.62 = bf16[32,32,1024]{2,1,0:T(8,128)(2,1)} broadcast(bf16[32,1024]{1,0:T(8,128)(2,1)S(1)} %copy-done.1), dimensions={1,2} | broadcast | bytes 2162688 | tf_op jit(solution)/shard_map/broadcast_in_dim | solution.py:131
  48.2 4.0 %all-to-all-start = ((bf16[32,32,1024]{2,1,0:T(8,128)(2,1)}), bf16[32,32,1024]{2,1,0:T(8,128)(2,1)S(1)}, u32[]{:S(2)}, u32[]{:S(2)}) async-start(bf16[32,32,1024]{2,1,0:T(8,128)(2,1)} %broadcast_in_dim.62), calls=%async_computation | async-start | bytes 4194304 | tf_op jit(solution)/shard_map/all_to_all | solution.py:132
  52.2 20.4 %fusion = f32[1024,1024,1]{1,0,2:T(8,128)} fusion(bf16[3,1024,1024]{2,1,0:T(8,128)(2,1)} %param.8, bf16[1024,1024,1]{1,0,2:T(8,128)(2,1)} %bitcast.44), kind=kOutput, calls=%fused_computation | convolution fusion | flops 12888047616 | bytes 12582912 | tf_op jit(solution)/shard_map/qac,qbc->ab/dot_general | solution.py:142
  72.6 9.8 %all-to-all-done = bf16[32,32,1024]{2,1,0:T(8,128)(2,1)S(1)} async-done(((bf16[32,32,1024]{2,1,0:T(8,128)(2,1)}), bf16[32,32,1024]{2,1,0:T(8,128)(2,1)S(1)}, u32[]{:S(2)}, u32[]{:S(2)}) %all-to-all-start) | async-done | bytes 2097184 | tf_op jit(solution)/shard_map/all_to_all | solution.py:132
  82.4 18.9 %fusion.4 = bf16[1024,1024]{1,0:T(8,128)(2,1)} fusion(f32[1024,1024,1]{1,0,2:T(8,128)} %fusion, bf16[3,1024,1024]{2,1,0:T(8,128)(2,1)} %param.8, bf16[1024,1024,1]{1,0,2:T(8,128)(2,1)S(1)} %bitcast.43), kind=kOutput, calls=%fused_computation.5 | convolution fusion | flops 12886999040 | bytes 14680064 | tf_op jit(solution)/shard_map/qac,qbc->ab/dot_general | solution.py:141
  101.4 0.0 copy-start.5
  101.4 4.2 %all-to-all-start.2 = ((bf16[32,32,1024]{2,1,0:T(8,128)(2,1)}), bf16[32,32,1024]{2,1,0:T(8,128)(2,1)S(1)}, u32[]{:S(2)}, u32[]{:S(2)}) async-start(bf16[32,32,1024]{2,1,0:T(8,128)(2,1)} %bitcast.42), calls=%async_computation.2 | async-start | bytes 4194304 | tf_op jit(solution)/shard_map/all_to_all | solution.py:145
  105.6 0.1 dynamic_slice.11
  105.7 0.1 dynamic_slice.10
  105.7 0.1 constant_dynamic-slice_fusion
  105.8 0.2 select_reduce_fusion
  106.1 0.2 select_reduce_fusion.2
  106.3 0.1 broadcast_xor_fusion
  106.4 0.1 broadcast_add_fusion
  106.4 29.9 %all-to-all-done.2 = bf16[32,32,1024]{2,1,0:T(8,128)(2,1)S(1)} async-done(((bf16[32,32,1024]{2,1,0:T(8,128)(2,1)}), bf16[32,32,1024]{2,1,0:T(8,128)(2,1)S(1)}, u32[]{:S(2)}, u32[]{:S(2)}) %all-to-all-start.2) | async-done | bytes 2097184 | tf_op jit(solution)/shard_map/all_to_all | solution.py:145
  136.3 0.4 convert_reduce_fusion
  136.7 1.0 copy.11
  137.7 12.1 %shard_map.74 = f32[32,32,32]{2,1,0:T(8,128)} custom-call(f32[32,32,32]{2,1,0:T(8,128)} %bitcast.41), custom_call_target="tpu_custom_call" | custom-call | tf_op jit(solution)/shard_map/pallas_call | solution.py:107
  149.8 1.4 copy.12
  151.1 0.2 reshape.123
  151.4 0.8 fusion.9
  (15 shorter events, 0.1 us)
Async XLA Ops:
  0.0 105.7 %copy-start = (s32[8,2]{0,1:T(2,128)S(1)}, s32[8,2]{0,1:T(2,128)}, u32[]{:S(2)}) copy-start(s32[8,2]{0,1:T(2,128)} %param.13) | copy-start | bytes 196
  4.8 41.8 %copy-start.1 = (bf16[32,1024]{1,0:T(8,128)(2,1)S(1)}, bf16[32,1024]{1,0:T(8,128)(2,1)}, u32[]{:S(2)}) copy-start(bf16[32,1024]{1,0:T(8,128)(2,1)} %get-tuple-element.7) | copy-start | bytes 196612
  48.2 34.2 %all-to-all-start = ((bf16[32,32,1024]{2,1,0:T(8,128)(2,1)}), bf16[32,32,1024]{2,1,0:T(8,128)(2,1)S(1)}, u32[]{:S(2)}, u32[]{:S(2)}) async-start(bf16[32,32,1024]{2,1,0:T(8,128)(2,1)} %broadcast_in_dim.62), calls=%async_computation | async-start | bytes 4194304 | tf_op jit(solution)/shard_map/all_to_all | solution.py:132
  101.4 4.2 %copy-start.3 = (f32[1024]{0:T(1024)S(1)}, f32[1024]{0:T(1024)}, u32[]{:S(2)}) copy-start(f32[1024]{0:T(1024)} %param.10) | copy-start | bytes 12292
  101.4 4.3 %copy-start.2 = (s32[1024]{0:T(1024)S(1)}, s32[1024]{0:T(1024)}, u32[]{:S(2)}) copy-start(s32[1024]{0:T(1024)} %param.12) | copy-start | bytes 12292
  101.4 4.4 %copy-start.4 = (f32[100]{0:T(128)S(1)}, f32[100]{0:T(128)}, u32[]{:S(2)}) copy-start(f32[100]{0:T(128)} %param.9) | copy-start | bytes 1204
  101.4 4.7 %copy-start.5 = (s32[100]{0:T(128)S(1)}, s32[100]{0:T(128)}, u32[]{:S(2)}) copy-start(s32[100]{0:T(128)} %param.11) | copy-start | bytes 1204
  101.4 34.9 %all-to-all-start.2 = ((bf16[32,32,1024]{2,1,0:T(8,128)(2,1)}), bf16[32,32,1024]{2,1,0:T(8,128)(2,1)S(1)}, u32[]{:S(2)}, u32[]{:S(2)}) async-start(bf16[32,32,1024]{2,1,0:T(8,128)(2,1)} %bitcast.42), calls=%async_computation.2 | async-start | bytes 4194304 | tf_op jit(solution)/shard_map/all_to_all | solution.py:145

commit v21 on v10

--- a/solution.py
+++ b/solution.py
@@ -101,9 +101,11 @@
         return product.astype(jnp.bfloat16)
 
     halves_first = half_products(gather_rows(own))
-    halves_second = half_products(gather_rows(other))
+    other_rows = gather_rows(other)
+    halves_second = jnp.einsum("cd,qad->qca", other_rows, factors, preferred_element_type=jnp.float32)
+    halves_second = halves_second.astype(jnp.bfloat16)
     direct = jnp.einsum("qac,qbc->ab", factors, halves_first, preferred_element_type=jnp.float32)
-    turned_term = jnp.einsum("qac,qbc->ab", halves_second, factors, preferred_element_type=jnp.float32)
+    turned_term = jnp.einsum("qca,qbc->ab", halves_second, factors, preferred_element_type=jnp.float32)
     combined = direct + turned_term
     blocks = combined.reshape(vir_devices, row_count, combined.shape[-1]).astype(jnp.bfloat16)
     arrived = lax.all_to_all(blocks, "vir", split_axis=0, concat_axis=0, tiled=True)

time: 150 us -> 150 us (level)
  no operation moved by 1% of the time
where the time goes in v21:
time: 150 us
  waiting for transfers between devices  41.1 us (27%)
  blocking collectives  40.2 us (27%)
  matrix products  39.1 us (26%)
  Pallas kernels  12.1 us (8%)
  starting transfers between devices  9.91 us (7%)
  local copies, waits for them, and re-layouts  4.68 us (3%)
  other arithmetic  2.71 us (2%)
    all_to_all x1, blocking collectives, gather_rows(): lax.all_to_all(spread, 'vir', split_axis=0, concat_axis=0, tiled=True)  40.2 us
    all_to_all x1, waiting for transfers between devices, per_device(): lax.all_to_all(blocks, 'vir', split_axis=0, concat_axis=0, tiled=True)  29.7 us
    dot_general x1, matrix products, per_device(): jnp.einsum('qac,qbc->ab', factors, halves_first, preferred_element_type=j...  20.3 us
    dot_general x1, matrix products, per_device(): jnp.einsum('qca,qbc->ab', halves_second, factors, preferred_element_type=...  18.8 us
    pallas_call x1, Pallas kernels, partner_transpose(): pl.pallas_call(functools.partial(_turn_kernel, n), out_shape=jax.ShapeDty...  12.1 us
    all_to_all x1, waiting for transfers between devices, gather_rows(): lax.all_to_all(spread, 'vir', split_axis=0, concat_axis=0, tiled=True)  8.81 us
    all_to_all x1, starting transfers between devices, per_device(): lax.all_to_all(blocks, 'vir', split_axis=0, concat_axis=0, tiled=True)  4.15 us
    all_to_all x1, starting transfers between devices, gather_rows(): lax.all_to_all(spread, 'vir', split_axis=0, concat_axis=0, tiled=True)  4.01 us
  transfers between devices with their start and end apart: 3, of which 3 were waited for; matrix products, arithmetic and copies ran while one was open for 14% of the time, Pallas kernels for 0%

profile of v21, /device:TPU:0, one launch (start us, length us, event | category | flops | bytes accessed | tf_op | source)
XLA Modules:
  0.0 150.0 jit_solution(4888687774855270688)
XLA Ops:
  0.0 0.9 select_bitcast_fusion
  0.9 1.7 %collective-permute-start = (bf16[32,1024]{1,0:T(8,128)(2,1)S(1)}, bf16[32,1024]{1,0:T(8,128)(2,1)S(1)}, u32[]{:S(2)}, u32[]{:S(2)}) collective-permute-start(bf16[32,1024]{1,0:T(8,128)(2,1)S(1)} %get-tuple-element.15), channel_id=1, source_target_pairs={{64,0},{96,32},{0,64},{32,96},{65,1},{97,33},{1,65},{33,97},{66,2}... | collective-permute-start | bytes 196616 | tf_op jit(solution)/shard_map/ppermute | solution.py:14
  2.6 2.6 %collective-permute-done = bf16[32,1024]{1,0:T(8,128)(2,1)S(1)} collective-permute-done((bf16[32,1024]{1,0:T(8,128)(2,1)S(1)}, bf16[32,1024]{1,0:T(8,128)(2,1)S(1)}, u32[]{:S(2)}, u32[]{:S(2)}) %collective-permute-start) | collective-permute-done | bytes 65568 | tf_op jit(solution)/shard_map/ppermute | solution.py:14
  5.2 0.2 broadcast_in_dim.62
  5.5 40.2 %all_to_all.15 = bf16[32,32,1024]{2,1,0:T(8,128)(2,1)} all-to-all(bf16[32,32,1024]{2,1,0:T(8,128)(2,1)S(1)} %broadcast_in_dim.62), channel_id=1, replica_groups=mesh['occ'=4,'vir'=32] {'vir'}, dimensions={0} | all-to-all | bytes 4194304 | tf_op jit(solution)/shard_map/all_to_all | solution.py:96
  45.7 1.6 %broadcast_in_dim.63 = bf16[32,32,1024]{2,1,0:T(8,128)(2,1)} broadcast(bf16[32,1024]{1,0:T(8,128)(2,1)S(1)} %collective-permute-done), dimensions={1,2} | broadcast | bytes 2162688 | tf_op jit(solution)/shard_map/broadcast_in_dim | solution.py:95
  47.3 4.0 %all-to-all-start.1 = ((bf16[32,32,1024]{2,1,0:T(8,128)(2,1)}), bf16[32,32,1024]{2,1,0:T(8,128)(2,1)S(1)}, u32[]{:S(2)}, u32[]{:S(2)}) async-start(bf16[32,32,1024]{2,1,0:T(8,128)(2,1)} %broadcast_in_dim.63), calls=%async_computation.1 | async-start | bytes 4194304 | tf_op jit(solution)/shard_map/all_to_all | solution.py:96
  51.3 20.3 %fusion.2 = f32[1024,1024,1]{0,1,2:T(8,128)} fusion(bf16[3,1024,1024]{2,1,0:T(8,128)(2,1)} %param.8, bf16[1024,1024,1]{1,0,2:T(8,128)(2,1)} %bitcast.47), kind=kOutput, calls=%fused_computation.2 | convolution fusion | flops 12888047616 | bytes 12582912 | tf_op jit(solution)/shard_map/qac,qbc->ab/dot_general | solution.py:107
  71.7 8.8 %all-to-all-done.1 = bf16[32,32,1024]{2,1,0:T(8,128)(2,1)S(1)} async-done(((bf16[32,32,1024]{2,1,0:T(8,128)(2,1)}), bf16[32,32,1024]{2,1,0:T(8,128)(2,1)S(1)}, u32[]{:S(2)}, u32[]{:S(2)}) %all-to-all-start.1) | async-done | bytes 2097184 | tf_op jit(solution)/shard_map/all_to_all | solution.py:96
  80.5 18.8 %fusion.6 = bf16[1024,1024]{1,0:T(8,128)(2,1)} fusion(f32[1024,1024,1]{0,1,2:T(8,128)} %fusion.2, bf16[3,1024,1024]{2,1,0:T(8,128)(2,1)} %param.8, bf16[1024,1024,1]{1,0,2:T(8,128)(2,1)S(1)} %bitcast.46), kind=kOutput, calls=%fused_computation.7 | convolution fusion | flops 12890144768 | bytes 14680064 | tf_op jit(solution)/shard_map/qca,qbc->ab/dot_general | solution.py:108
  99.3 4.2 %all-to-all-start.2 = ((bf16[32,32,1024]{2,1,0:T(8,128)(2,1)}), bf16[32,32,1024]{2,1,0:T(8,128)(2,1)S(1)}, u32[]{:S(2)}, u32[]{:S(2)}) async-start(bf16[32,32,1024]{2,1,0:T(8,128)(2,1)} %bitcast.45), calls=%async_computation.2 | async-start | bytes 4194304 | tf_op jit(solution)/shard_map/all_to_all | solution.py:111
  103.5 0.1 dynamic_slice.11
  103.6 0.1 dynamic_slice.10
  103.6 0.1 constant_dynamic-slice_fusion
  103.7 0.2 select_reduce_fusion
  104.0 0.2 select_reduce_fusion.2
  104.3 0.1 broadcast_add_fusion
  104.3 29.7 %all-to-all-done.2 = bf16[32,32,1024]{2,1,0:T(8,128)(2,1)S(1)} async-done(((bf16[32,32,1024]{2,1,0:T(8,128)(2,1)}), bf16[32,32,1024]{2,1,0:T(8,128)(2,1)S(1)}, u32[]{:S(2)}, u32[]{:S(2)}) %all-to-all-start.2) | async-done | bytes 2097184 | tf_op jit(solution)/shard_map/all_to_all | solution.py:111
  134.1 0.4 convert_reduce_fusion
  134.4 1.0 copy.13
  135.4 12.1 %shard_map.73 = f32[32,32,32]{2,1,0:T(8,128)} custom-call(f32[32,32,32]{2,1,0:T(8,128)} %bitcast.44), custom_call_target="tpu_custom_call" | custom-call | tf_op jit(solution)/shard_map/pallas_call | solution.py:68
  147.5 1.4 copy.14
  148.9 0.2 reshape.127
  149.2 0.8 fusion.13
  (15 shorter events, 0.1 us)
Async XLA Ops:
  0.0 103.6 %copy-start = (s32[8,2]{0,1:T(2,128)S(1)}, s32[8,2]{0,1:T(2,128)}, u32[]{:S(2)}) copy-start(s32[8,2]{0,1:T(2,128)} %param.13) | copy-start | bytes 196
  0.9 4.3 %collective-permute-start = (bf16[32,1024]{1,0:T(8,128)(2,1)S(1)}, bf16[32,1024]{1,0:T(8,128)(2,1)S(1)}, u32[]{:S(2)}, u32[]{:S(2)}) collective-permute-start(bf16[32,1024]{1,0:T(8,128)(2,1)S(1)} %get-tuple-element.15), channel_id=1, source_target_pairs={{64,0},{96,32},{0,64},{32,96},{65,1},{97,33},{1,65},{33,97},{66,2}... | collective-permute-start | bytes 196616 | tf_op jit(solution)/shard_map/ppermute | solution.py:14
  47.3 33.2 %all-to-all-start.1 = ((bf16[32,32,1024]{2,1,0:T(8,128)(2,1)}), bf16[32,32,1024]{2,1,0:T(8,128)(2,1)S(1)}, u32[]{:S(2)}, u32[]{:S(2)}) async-start(bf16[32,32,1024]{2,1,0:T(8,128)(2,1)} %broadcast_in_dim.63), calls=%async_computation.1 | async-start | bytes 4194304 | tf_op jit(solution)/shard_map/all_to_all | solution.py:96
  99.3 4.2 %copy-start.2 = (f32[1024]{0:T(1024)S(1)}, f32[1024]{0:T(1024)}, u32[]{:S(2)}) copy-start(f32[1024]{0:T(1024)} %param.10) | copy-start | bytes 12292
  99.3 4.3 %copy-start.1 = (s32[1024]{0:T(1024)S(1)}, s32[1024]{0:T(1024)}, u32[]{:S(2)}) copy-start(s32[1024]{0:T(1024)} %param.12) | copy-start | bytes 12292
  99.3 4.4 %copy-start.3 = (f32[100]{0:T(128)S(1)}, f32[100]{0:T(128)}, u32[]{:S(2)}) copy-start(f32[100]{0:T(128)} %param.9) | copy-start | bytes 1204
  99.3 4.7 %copy-start.4 = (s32[100]{0:T(128)S(1)}, s32[100]{0:T(128)}, u32[]{:S(2)}) copy-start(s32[100]{0:T(128)} %param.11) | copy-start | bytes 1204
  99.3 34.8 %all-to-all-start.2 = ((bf16[32,32,1024]{2,1,0:T(8,128)(2,1)}), bf16[32,32,1024]{2,1,0:T(8,128)(2,1)S(1)}, u32[]{:S(2)}, u32[]{:S(2)}) async-start(bf16[32,32,1024]{2,1,0:T(8,128)(2,1)} %bitcast.45), calls=%async_computation.2 | async-start | bytes 4194304 | tf_op jit(solution)/shard_map/all_to_all | solution.py:111
